TPU v7x, 512 devices: a whole 4x8x8 slice. The times are simulated.
512 devices in a mesh: seq: 64 (over y, x, core), ch: 8 (over z).
Axes of the slice: x: 4, y: 8, z: 8, core: 2. Of those that a mesh axis runs over, the one named last changes fastest.
Arguments:
- qkv: bfloat16 [16384, 3, 4096], P('seq', None, 'ch'), may hold values from -6 to 6
- short_w: float32 [3, 3, 4096], P(None, None, 'ch'), may hold values from -3 to 3
- skip: float32 [4096], P('ch'), may hold values from -4 to 4
- filt: float32 [16384, 4096], P('seq', 'ch'), may hold values from -4 to 4
Outputs:
- mixed: bfloat16 [16384, 4096], P('seq', 'ch')
All inputs are finite; a program needn't handle non-finite values.
Results may differ from a plain program's by a relative error of at most 0.001.
Values may be sent and summed in bfloat16 or wider, within the bound.
A program may use at most 64 MiB of HBM per device.

v0:
```python
import math

import jax
import jax.numpy as jnp
from jax import lax
from jax.sharding import PartitionSpec as P

HIGHEST = lax.Precision.HIGHEST


def shifted(block, axis, distance):
    devices = range(lax.axis_size(axis))
    route = [(i - distance, i) for i in devices if i - distance in devices]
    return lax.ppermute(block, axis, route)


def phase_table(count_out, count_in, modulus, sign):
    out_idx = jnp.arange(count_out, dtype=jnp.int32)[:, None]
    in_idx = jnp.arange(count_in, dtype=jnp.int32)[None, :]
    phase = out_idx * in_idx % modulus
    angles = sign * 2.0 * math.pi / modulus * phase.astype(jnp.float32)
    return jnp.cos(angles), jnp.sin(angles)


def long_conv(pieces):
    blocks, _, group, rows = pieces.shape
    coarse = 2 * blocks
    total = coarse * rows
    half = blocks + 1
    cos1, sin1 = phase_table(half, blocks, coarse, -1.0)
    y_re = jnp.einsum("kd,dsgr->skgr", cos1, pieces, precision=HIGHEST)
    y_im = jnp.einsum("kd,dsgr->skgr", sin1, pieces, precision=HIGHEST)
    tw_cos, tw_sin = phase_table(half, rows, total, -1.0)
    tw_cos = tw_cos[None, :, None, :]
    tw_sin = tw_sin[None, :, None, :]
    y_re, y_im = y_re * tw_cos - y_im * tw_sin, y_re * tw_sin + y_im * tw_cos
    cos2, sin2 = phase_table(rows, rows, rows, -1.0)
    z_re = jnp.einsum("skgr,rm->skgm", y_re, cos2, precision=HIGHEST) - jnp.einsum(
        "skgr,rm->skgm", y_im, sin2, precision=HIGHEST
    )
    z_im = jnp.einsum("skgr,rm->skgm", y_im, cos2, precision=HIGHEST) + jnp.einsum(
        "skgr,rm->skgm", y_re, sin2, precision=HIGHEST
    )
    p_re = z_re[0] * z_re[1] - z_im[0] * z_im[1]
    p_im = z_re[0] * z_im[1] + z_im[0] * z_re[1]
    q_re = jnp.einsum("kgm,mr->kgr", p_re, cos2, precision=HIGHEST) + jnp.einsum(
        "kgm,mr->kgr", p_im, sin2, precision=HIGHEST
    )
    q_im = jnp.einsum("kgm,mr->kgr", p_im, cos2, precision=HIGHEST) - jnp.einsum(
        "kgm,mr->kgr", p_re, sin2, precision=HIGHEST
    )
    tw_cos = tw_cos[0]
    tw_sin = tw_sin[0]
    q_re, q_im = q_re * tw_cos + q_im * tw_sin, q_im * tw_cos - q_re * tw_sin
    weight = jnp.where(
        (jnp.arange(half) == 0) | (jnp.arange(half) == blocks), 1.0, 2.0
    ).astype(jnp.float32) / total
    cos3, sin3 = phase_table(blocks, half, coarse, 1.0)
    cos3 = cos3 * weight[None, :]
    sin3 = sin3 * weight[None, :]
    return jnp.einsum("dk,kgr->dgr", cos3, q_re, precision=HIGHEST) - jnp.einsum(
        "dk,kgr->dgr", sin3, q_im, precision=HIGHEST
    )


def on_device(qkv, short_w, skip, filt):
    rows, _, width = qkv.shape
    taps = short_w.shape[0]
    shards = lax.axis_size("seq")
    group = width // shards
    rim = shifted(qkv[rows - (taps - 1) :], "seq", 1)
    extended = jnp.concatenate([rim, qkv], axis=0).astype(jnp.float32)
    feat = short_w[0] * extended[taps - 1 : taps - 1 + rows]
    for tap in range(1, taps):
        feat = feat + short_w[tap] * extended[taps - 1 - tap : taps - 1 - tap + rows]
    query = feat[:, 0, :]
    signal = feat[:, 1, :] * feat[:, 2, :]
    source = jnp.stack([signal, filt]).reshape(2, rows, shards, group).transpose(2, 0, 3, 1)
    pieces = lax.all_to_all(source, "seq", split_axis=0, concat_axis=0, tiled=True)
    values = long_conv(pieces)
    back = lax.all_to_all(values, "seq", split_axis=0, concat_axis=0, tiled=True)
    conv = back.reshape(width, rows).T
    return (query * (conv + skip * signal)).astype(jnp.bfloat16)


def solution(mesh):
    return jax.shard_map(
        on_device,
        mesh=mesh,
        in_specs=(P("seq", None, "ch"), P(None, None, "ch"), P("ch"), P("seq", "ch")),
        out_specs=P("seq", "ch"),
        check_vma=False,
    )
```

profile of v0, /device:TPU:1, one launch (start us, length us, event | category | flops | bytes accessed | tf_op | source)
XLA Modules:
  0.0 100.3 jit_solution(5657370296019627992)
XLA Ops:
  0.0 0.8 slice.47
  0.8 0.3 copy.24
  1.1 4.5 %collective-permute-start = (bf16[2,3,512]{0,2,1:T(8,128)(2,1)S(1)}, bf16[2,3,512]{0,2,1:T(8,128)(2,1)S(1)}, u32[]{:S(2)}, u32[]{:S(2)}) collective-permute-start(bf16[2,3,512]{0,2,1:T(8,128)(2,1)S(1)} %copy.24), channel_id=1, source_target_pairs={{0,8},{8,16},{16,24},{24,32},{32,40},{40,48},{48,56},{56,64},{64,7... | collective-permute-start | bytes 18440 | tf_op jit(solution)/shard_map/ppermute | solution.py:14
  5.6 0.7 slice_bitcast_fusion.3
  6.3 1.4 %copy.25 = bf16[256,3,512]{0,2,1:T(8,128)(2,1)S(1)} copy(bf16[256,3,512]{2,0,1:T(8,128)(2,1)} %param.4) | data formatting | bytes 1572864 | tf_op args[0]
  7.8 0.2 copy.26
  8.0 2.5 %collective-permute-done = bf16[2,3,512]{0,2,1:T(8,128)(2,1)S(1)} collective-permute-done((bf16[2,3,512]{0,2,1:T(8,128)(2,1)S(1)}, bf16[2,3,512]{0,2,1:T(8,128)(2,1)S(1)}, u32[]{:S(2)}, u32[]{:S(2)}) %collective-permute-start) | collective-permute-done | bytes 6176 | tf_op jit(solution)/shard_map/ppermute | solution.py:14
  10.5 0.5 maximum_convert_fusion
  11.0 1.6 %fusion = f32[256,3,512]{0,2,1:T(8,128)S(1)} fusion(f32[258,3,512]{0,2,1:T(8,128)S(1)} %maximum_convert_fusion, f32[3,512]{1,0:T(4,128)S(1)} %get-tuple-element.12, f32[3,512]{1,0:T(4,128)S(1)} %get-tuple-element.13, f32[3,512]{1,0:T(4,128)S(1)} %get-tuple-element.11), kind=kLoop, calls=%fused_computation.1 | loop fusion | flops 1966080 | bytes 6309888 | tf_op jit(solution)/shard_map/add | solution.py:75
  12.6 0.1 fusion.35
  12.7 0.1 maximum_bitcast_fusion
  12.7 1.1 %copy.27 = f32[64,2,8,256]{3,2,1,0:T(8,128)} copy(f32[64,2,8,256]{3,2,0,1:T(8,128)S(1)} %maximum_bitcast_fusion) | data formatting | bytes 2097152 | tf_op jit(solution)/shard_map/transpose | solution.py:78
  13.9 12.4 %all-to-all-start = ((f32[64,2,8,256]{3,2,1,0:T(8,128)}), f32[64,2,8,256]{3,2,1,0:T(8,128)S(1)}, u32[]{:S(2)}, u32[]{:S(2)}) async-start(f32[64,2,8,256]{3,2,1,0:T(8,128)} %copy.27), calls=%async_computation | async-start | bytes 2097152 | tf_op jit(solution)/shard_map/all_to_all | solution.py:79
  26.3 0.3 fusion.52
  26.6 27.5 %all-to-all-done = f32[64,2,8,256]{3,2,1,0:T(8,128)S(1)} async-done(((f32[64,2,8,256]{3,2,1,0:T(8,128)}), f32[64,2,8,256]{3,2,1,0:T(8,128)S(1)}, u32[]{:S(2)}, u32[]{:S(2)}) %all-to-all-start) | async-done | bytes 1048608 | tf_op jit(solution)/shard_map/all_to_all | solution.py:79
  54.1 1.9 %convolution_bitcast_fusion.1 = f32[2,65,8,256]{3,1,2,0:T(8,128)S(1)} fusion(f32[64,2,8,256]{3,2,1,0:T(8,128)S(1)} %all-to-all-done), kind=kOutput, calls=%fused_computation.6 | convolution fusion | flops 204530560 | bytes 2113536 | tf_op jit(solution)/shard_map/kd,dsgr->skgr/dot_general | solution.py:31
  56.0 2.1 %multiply_subtract_fusion = (f32[2,65,8,256]{3,1,2,0:T(8,128)S(1)}, f32[2,65,8,256]{3,1,2,0:T(8,128)S(1)}) fusion(f32[2,65,8,256]{3,1,2,0:T(8,128)S(1)} %convolution_bitcast_fusion.1, f32[65,256]{1,0:T(8,128)S(1)} %get-tuple-element.14, f32[65,256]{1,0:T(8,128)S(1)} %get-tuple-element.15, f32[64,2,8,256]{3,2,1,0:T(8,128)S(1)} %all-to-all-done), kind=kOutput, calls=%fused_computation.14 | convolution fusion | flops 206128000 | bytes 4376576 | tf_op jit(solution)/shard_map/kd,dsgr->skgr/dot_general | solution.py:32
  58.1 2.1 %fusion.8 = f32[2,65,8,256]{3,2,1,0:T(8,128)S(1)} fusion(f32[2,65,8,256]{3,1,2,0:T(8,128)S(1)} %get-tuple-element.5), kind=kOutput, calls=%fused_computation.22 | convolution fusion | flops 818806784 | bytes 2129920 | tf_op jit(solution)/shard_map/skgr,rm->skgm/dot_general | solution.py:38
  60.3 2.1 %fusion.4 = f32[2,65,8,256]{3,2,1,0:T(8,128)S(1)} fusion(f32[2,65,8,256]{3,1,2,0:T(8,128)S(1)} %get-tuple-element.6), kind=kOutput, calls=%fused_computation.18 | convolution fusion | flops 818806784 | bytes 2129920 | tf_op jit(solution)/shard_map/skgr,rm->skgm/dot_general | solution.py:41
  62.4 2.1 %convolution_subtract_fusion = f32[2,65,8,256]{3,2,1,0:T(8,128)S(1)} fusion(f32[2,65,8,256]{3,2,1,0:T(8,128)S(1)} %fusion.8, f32[2,65,8,256]{3,1,2,0:T(8,128)S(1)} %get-tuple-element.6), kind=kOutput, calls=%fused_computation.8 | convolution fusion | flops 819073024 | bytes 3194880 | tf_op jit(solution)/shard_map/skgr,rm->skgm/dot_general | solution.py:38
  64.5 2.4 %convolution_add_fusion = f32[2,65,8,256]{3,2,1,0:T(8,128)S(1)} fusion(f32[2,65,8,256]{3,2,1,0:T(8,128)S(1)} %fusion.4, f32[2,65,8,256]{3,1,2,0:T(8,128)S(1)} %get-tuple-element.5), kind=kOutput, calls=%fused_computation.7 | convolution fusion | flops 819073024 | bytes 3194880 | tf_op jit(solution)/shard_map/skgr,rm->skgm/dot_general | solution.py:41
  66.9 0.1 multiply_subtract_fusion.2
  67.0 1.6 %fusion.13 = f32[65,8,256]{2,1,0:T(8,128)S(1)} fusion(f32[1,65,8,256]{3,2,1,0:T(8,128)S(1)} %get-tuple-element.8), kind=kOutput, calls=%fused_computation.27 | convolution fusion | flops 409862144 | bytes 1064960 | tf_op jit(solution)/shard_map/kgm,mr->kgr/dot_general | solution.py:49
  68.6 1.6 %fusion.17 = f32[65,8,256]{2,1,0:T(8,128)S(1)} fusion(f32[1,65,8,256]{3,2,1,0:T(8,128)S(1)} %get-tuple-element.7), kind=kOutput, calls=%fused_computation.31 | convolution fusion | flops 409862144 | bytes 1064960 | tf_op jit(solution)/shard_map/kgm,mr->kgr/dot_general | solution.py:46
  70.2 1.6 %convolution_subtract_fusion.1 = f32[65,8,256]{2,1,0:T(8,128)S(1)} fusion(f32[65,8,256]{2,1,0:T(8,128)S(1)} %fusion.13, f32[1,65,8,256]{3,2,1,0:T(8,128)S(1)} %get-tuple-element.7), kind=kOutput, calls=%fused_computation.9 | convolution fusion | flops 409995264 | bytes 1597440 | tf_op jit(solution)/shard_map/kgm,mr->kgr/dot_general | solution.py:49
  71.7 1.7 %multiply_subtract_fusion.1 = (f32[65,8,256]{2,1,0:T(8,128)S(1)}, f32[65,8,256]{2,1,0:T(8,128)S(1)}) fusion(f32[65,8,256]{2,1,0:T(8,128)S(1)} %convolution_subtract_fusion.1, f32[65,256]{1,0:T(8,128)S(1)} %get-tuple-element.14, f32[65,256]{1,0:T(8,128)S(1)} %get-tuple-element.15, f32[65,8,256]{2,1,0:T(8,128)S(1)} %fusion.17, ...), kind=kOutput, calls=%fused_computation.33 | convolution fusion | flops 410793984 | bytes 2795520 | tf_op jit(solution)/shard_map/kgm,mr->kgr/dot_general | solution.py:46
  73.4 0.8 fusion.11
  74.2 0.8 convolution_subtract_fusion.2
  75.0 0.3 copy.36
  75.4 24.0 %all_to_all.10 = f32[64,8,256]{2,1,0:T(8,128)S(1)} all-to-all(f32[64,8,256]{2,1,0:T(8,128)S(1)} %copy.36), channel_id=1, replica_groups=mesh['seq'=64,'ch'=8] {'seq'}, dimensions={0} | all-to-all | bytes 1048576 | tf_op jit(solution)/shard_map/all_to_all | solution.py:81
  99.4 0.1 fusion.20
  99.5 0.8 copy.37
  (5 shorter events, 0.0 us)
Async XLA Ops:
  0.0 7.7 %copy-start = (f32[256,512]{1,0:T(8,128)S(1)}, f32[256,512]{1,0:T(8,128)}, u32[]{:S(2)}) copy-start(f32[256,512]{1,0:T(8,128)} %param.7) | copy-start | bytes 1572868
  1.1 9.4 %collective-permute-start = (bf16[2,3,512]{0,2,1:T(8,128)(2,1)S(1)}, bf16[2,3,512]{0,2,1:T(8,128)(2,1)S(1)}, u32[]{:S(2)}, u32[]{:S(2)}) collective-permute-start(bf16[2,3,512]{0,2,1:T(8,128)(2,1)S(1)} %copy.24), channel_id=1, source_target_pairs={{0,8},{8,16},{16,24},{24,32},{32,40},{40,48},{48,56},{56,64},{64,7... | collective-permute-start | bytes 18440 | tf_op jit(solution)/shard_map/ppermute | solution.py:14
  13.9 40.2 %all-to-all-start = ((f32[64,2,8,256]{3,2,1,0:T(8,128)}), f32[64,2,8,256]{3,2,1,0:T(8,128)S(1)}, u32[]{:S(2)}, u32[]{:S(2)}) async-start(f32[64,2,8,256]{3,2,1,0:T(8,128)} %copy.27), calls=%async_computation | async-start | bytes 2097152 | tf_op jit(solution)/shard_map/all_to_all | solution.py:79
  75.0 24.3 %copy-start.1 = (f32[512]{0:T(512)S(1)}, f32[512]{0:T(512)}, u32[]{:S(2)}) copy-start(f32[512]{0:T(512)} %param.6) | copy-start | bytes 6148
where the time goes:
time: 101 us; the launch traced here: 100 us
  waiting for transfers between devices  30 us (30%)
  blocking collectives  24 us (24%)
  matrix products  20.7 us (20%)
  starting transfers between devices  16.9 us (17%)
  local copies, waits for them, and re-layouts  5.69 us (6%)
  other arithmetic  2.86 us (3%)
    all_to_all x1, waiting for transfers between devices, on_device(): lax.all_to_all(source, 'seq', split_axis=0, concat_axis=0, tiled=True)  27.5 us
    all_to_all x1, blocking collectives, on_device(): lax.all_to_all(values, 'seq', split_axis=0, concat_axis=0, tiled=True)  24 us
    all_to_all x1, starting transfers between devices, on_device(): lax.all_to_all(source, 'seq', split_axis=0, concat_axis=0, tiled=True)  12.4 us
    ppermute x1, starting transfers between devices, shifted(): return lax.ppermute(block, axis, route)  4.51 us
    ppermute x1, waiting for transfers between devices, shifted(): return lax.ppermute(block, axis, route)  2.49 us
    dot_general x1, matrix products, long_conv(): jnp.einsum('skgr,rm->skgm', y_re, sin2, precision=HIGHEST)  2.35 us
    dot_general x1, matrix products, long_conv(): y_im = jnp.einsum('kd,dsgr->skgr', sin1, pieces, precision=HIGHEST)  2.15 us
    dot_general x1, matrix products, long_conv(): jnp.einsum('skgr,rm->skgm', y_im, sin2, precision=HIGHEST)  2.13 us
  transfers between devices with their start and end apart: 2, of which 2 were waited for; matrix products, arithmetic and copies ran while one was open for 3% of the time, Pallas kernels for 0%

commit v1 on v0

--- a/solution.py
+++ b/solution.py
@@ -5,7 +5,7 @@
 from jax import lax
 from jax.sharding import PartitionSpec as P
 
-HIGHEST = lax.Precision.HIGHEST
+PRECISION = lax.Precision.HIGH
 
 
 def shifted(block, axis, distance):
@@ -28,26 +28,26 @@
     total = coarse * rows
     half = blocks + 1
     cos1, sin1 = phase_table(half, blocks, coarse, -1.0)
-    y_re = jnp.einsum("kd,dsgr->skgr", cos1, pieces, precision=HIGHEST)
-    y_im = jnp.einsum("kd,dsgr->skgr", sin1, pieces, precision=HIGHEST)
+    y_re = jnp.einsum("kd,dsgr->skgr", cos1, pieces, precision=PRECISION)
+    y_im = jnp.einsum("kd,dsgr->skgr", sin1, pieces, precision=PRECISION)
     tw_cos, tw_sin = phase_table(half, rows, total, -1.0)
     tw_cos = tw_cos[None, :, None, :]
     tw_sin = tw_sin[None, :, None, :]
     y_re, y_im = y_re * tw_cos - y_im * tw_sin, y_re * tw_sin + y_im * tw_cos
     cos2, sin2 = phase_table(rows, rows, rows, -1.0)
-    z_re = jnp.einsum("skgr,rm->skgm", y_re, cos2, precision=HIGHEST) - jnp.einsum(
-        "skgr,rm->skgm", y_im, sin2, precision=HIGHEST
+    z_re = jnp.einsum("skgr,rm->skgm", y_re, cos2, precision=PRECISION) - jnp.einsum(
+        "skgr,rm->skgm", y_im, sin2, precision=PRECISION
     )
-    z_im = jnp.einsum("skgr,rm->skgm", y_im, cos2, precision=HIGHEST) + jnp.einsum(
-        "skgr,rm->skgm", y_re, sin2, precision=HIGHEST
+    z_im = jnp.einsum("skgr,rm->skgm", y_im, cos2, precision=PRECISION) + jnp.einsum(
+        "skgr,rm->skgm", y_re, sin2, precision=PRECISION
     )
     p_re = z_re[0] * z_re[1] - z_im[0] * z_im[1]
     p_im = z_re[0] * z_im[1] + z_im[0] * z_re[1]
-    q_re = jnp.einsum("kgm,mr->kgr", p_re, cos2, precision=HIGHEST) + jnp.einsum(
-        "kgm,mr->kgr", p_im, sin2, precision=HIGHEST
+    q_re = jnp.einsum("kgm,mr->kgr", p_re, cos2, precision=PRECISION) + jnp.einsum(
+        "kgm,mr->kgr", p_im, sin2, precision=PRECISION
     )
-    q_im = jnp.einsum("kgm,mr->kgr", p_im, cos2, precision=HIGHEST) - jnp.einsum(
-        "kgm,mr->kgr", p_re, sin2, precision=HIGHEST
+    q_im = jnp.einsum("kgm,mr->kgr", p_im, cos2, precision=PRECISION) - jnp.einsum(
+        "kgm,mr->kgr", p_re, sin2, precision=PRECISION
     )
     tw_cos = tw_cos[0]
     tw_sin = tw_sin[0]
@@ -58,8 +58,8 @@
     cos3, sin3 = phase_table(blocks, half, coarse, 1.0)
     cos3 = cos3 * weight[None, :]
     sin3 = sin3 * weight[None, :]
-    return jnp.einsum("dk,kgr->dgr", cos3, q_re, precision=HIGHEST) - jnp.einsum(
-        "dk,kgr->dgr", sin3, q_im, precision=HIGHEST
+    return jnp.einsum("dk,kgr->dgr", cos3, q_re, precision=PRECISION) - jnp.einsum(
+        "dk,kgr->dgr", sin3, q_im, precision=PRECISION
     )
 
 

time: 101 us -> 96.7 us (0.957)
  matrix products: 20.7 us -> 16.7 us
    dot_general x12, matrix products: 20.7 us -> 16.7 us  [the longest x1 1.77 us: long_conv(): jnp.einsum('skgr,rm->skgm', y_im, cos2, precision=PRECISION)]
where the time goes in v1:
time: 96.7 us; the launch traced here: 96.3 us
  waiting for transfers between devices  30 us (31%)
  blocking collectives  24 us (25%)
  starting transfers between devices  16.9 us (17%)
  matrix products  16.7 us (17%)
  local copies, waits for them, and re-layouts  5.69 us (6%)
  other arithmetic  2.86 us (3%)
    all_to_all x1, waiting for transfers between devices, on_device(): lax.all_to_all(source, 'seq', split_axis=0, concat_axis=0, tiled=True)  27.5 us
    all_to_all x1, blocking collectives, on_device(): lax.all_to_all(values, 'seq', split_axis=0, concat_axis=0, tiled=True)  24 us
    all_to_all x1, starting transfers between devices, on_device(): lax.all_to_all(source, 'seq', split_axis=0, concat_axis=0, tiled=True)  12.4 us
    ppermute x1, starting transfers between devices, shifted(): return lax.ppermute(block, axis, route)  4.51 us
    ppermute x1, waiting for transfers between devices, shifted(): return lax.ppermute(block, axis, route)  2.49 us
  transfers between devices with their start and end apart: 2, of which 2 were waited for; matrix products, arithmetic and copies ran while one was open for 3% of the time, Pallas kernels for 0%

profile of v1, /device:TPU:1, one launch (start us, length us, event | category | flops | bytes accessed | tf_op | source)
XLA Modules:
  0.0 96.3 jit_solution(868487024865035248)
XLA Ops:
  0.0 0.8 slice.47
  0.8 0.3 copy.24
  1.1 4.5 %collective-permute-start = (bf16[2,3,512]{0,2,1:T(8,128)(2,1)S(1)}, bf16[2,3,512]{0,2,1:T(8,128)(2,1)S(1)}, u32[]{:S(2)}, u32[]{:S(2)}) collective-permute-start(bf16[2,3,512]{0,2,1:T(8,128)(2,1)S(1)} %copy.24), channel_id=1, source_target_pairs={{0,8},{8,16},{16,24},{24,32},{32,40},{40,48},{48,56},{56,64},{64,7... | collective-permute-start | bytes 18440 | tf_op jit(solution)/shard_map/ppermute | solution.py:14
  5.6 0.7 slice_bitcast_fusion.3
  6.3 1.4 %copy.25 = bf16[256,3,512]{0,2,1:T(8,128)(2,1)S(1)} copy(bf16[256,3,512]{2,0,1:T(8,128)(2,1)} %param.4) | data formatting | bytes 1572864 | tf_op args[0]
  7.8 0.2 copy.26
  8.0 2.5 %collective-permute-done = bf16[2,3,512]{0,2,1:T(8,128)(2,1)S(1)} collective-permute-done((bf16[2,3,512]{0,2,1:T(8,128)(2,1)S(1)}, bf16[2,3,512]{0,2,1:T(8,128)(2,1)S(1)}, u32[]{:S(2)}, u32[]{:S(2)}) %collective-permute-start) | collective-permute-done | bytes 6176 | tf_op jit(solution)/shard_map/ppermute | solution.py:14
  10.5 0.5 maximum_convert_fusion
  11.0 1.6 %fusion = f32[256,3,512]{0,2,1:T(8,128)S(1)} fusion(f32[258,3,512]{0,2,1:T(8,128)S(1)} %maximum_convert_fusion, f32[3,512]{1,0:T(4,128)S(1)} %get-tuple-element.12, f32[3,512]{1,0:T(4,128)S(1)} %get-tuple-element.13, f32[3,512]{1,0:T(4,128)S(1)} %get-tuple-element.11), kind=kLoop, calls=%fused_computation.1 | loop fusion | flops 1966080 | bytes 6309888 | tf_op jit(solution)/shard_map/add | solution.py:75
  12.6 0.1 fusion.35
  12.7 0.1 maximum_bitcast_fusion
  12.7 1.1 %copy.27 = f32[64,2,8,256]{3,2,1,0:T(8,128)} copy(f32[64,2,8,256]{3,2,0,1:T(8,128)S(1)} %maximum_bitcast_fusion) | data formatting | bytes 2097152 | tf_op jit(solution)/shard_map/transpose | solution.py:78
  13.9 12.4 %all-to-all-start = ((f32[64,2,8,256]{3,2,1,0:T(8,128)}), f32[64,2,8,256]{3,2,1,0:T(8,128)S(1)}, u32[]{:S(2)}, u32[]{:S(2)}) async-start(f32[64,2,8,256]{3,2,1,0:T(8,128)} %copy.27), calls=%async_computation | async-start | bytes 2097152 | tf_op jit(solution)/shard_map/all_to_all | solution.py:79
  26.3 0.3 fusion.52
  26.6 27.5 %all-to-all-done = f32[64,2,8,256]{3,2,1,0:T(8,128)S(1)} async-done(((f32[64,2,8,256]{3,2,1,0:T(8,128)}), f32[64,2,8,256]{3,2,1,0:T(8,128)S(1)}, u32[]{:S(2)}, u32[]{:S(2)}) %all-to-all-start) | async-done | bytes 1048608 | tf_op jit(solution)/shard_map/all_to_all | solution.py:79
  54.1 1.3 %convolution_bitcast_fusion.1 = f32[2,65,8,256]{3,1,2,0:T(8,128)S(1)} fusion(f32[64,2,8,256]{3,2,1,0:T(8,128)S(1)} %all-to-all-done), kind=kOutput, calls=%fused_computation.6 | convolution fusion | flops 102294400 | bytes 2113536 | tf_op jit(solution)/shard_map/kd,dsgr->skgr/dot_general | solution.py:31
  55.3 1.5 %multiply_subtract_fusion = (f32[2,65,8,256]{3,1,2,0:T(8,128)S(1)}, f32[2,65,8,256]{3,1,2,0:T(8,128)S(1)}) fusion(f32[2,65,8,256]{3,1,2,0:T(8,128)S(1)} %convolution_bitcast_fusion.1, f32[65,256]{1,0:T(8,128)S(1)} %get-tuple-element.14, f32[65,256]{1,0:T(8,128)S(1)} %get-tuple-element.15, f32[64,2,8,256]{3,2,1,0:T(8,128)S(1)} %all-to-all-done), kind=kOutput, calls=%fused_computation.14 | convolution fusion | flops 103891840 | bytes 4376576 | tf_op jit(solution)/shard_map/kd,dsgr->skgr/dot_general | solution.py:32
  56.9 1.8 %fusion.8 = f32[2,65,8,256]{3,2,1,0:T(8,128)S(1)} fusion(f32[2,65,8,256]{3,1,2,0:T(8,128)S(1)} %get-tuple-element.5), kind=kOutput, calls=%fused_computation.22 | convolution fusion | flops 409862144 | bytes 2129920 | tf_op jit(solution)/shard_map/skgr,rm->skgm/dot_general | solution.py:38
  58.7 1.8 %fusion.4 = f32[2,65,8,256]{3,2,1,0:T(8,128)S(1)} fusion(f32[2,65,8,256]{3,1,2,0:T(8,128)S(1)} %get-tuple-element.6), kind=kOutput, calls=%fused_computation.18 | convolution fusion | flops 409862144 | bytes 2129920 | tf_op jit(solution)/shard_map/skgr,rm->skgm/dot_general | solution.py:41
  60.4 1.8 %convolution_subtract_fusion = f32[2,65,8,256]{3,2,1,0:T(8,128)S(1)} fusion(f32[2,65,8,256]{3,2,1,0:T(8,128)S(1)} %fusion.8, f32[2,65,8,256]{3,1,2,0:T(8,128)S(1)} %get-tuple-element.6), kind=kOutput, calls=%fused_computation.8 | convolution fusion | flops 410128384 | bytes 3194880 | tf_op jit(solution)/shard_map/skgr,rm->skgm/dot_general | solution.py:38
  62.2 1.8 %convolution_add_fusion = f32[2,65,8,256]{3,2,1,0:T(8,128)S(1)} fusion(f32[2,65,8,256]{3,2,1,0:T(8,128)S(1)} %fusion.4, f32[2,65,8,256]{3,1,2,0:T(8,128)S(1)} %get-tuple-element.5), kind=kOutput, calls=%fused_computation.7 | convolution fusion | flops 410128384 | bytes 3194880 | tf_op jit(solution)/shard_map/skgr,rm->skgm/dot_general | solution.py:41
  64.0 0.1 multiply_subtract_fusion.2
  64.1 1.4 %fusion.13 = f32[65,8,256]{2,1,0:T(8,128)S(1)} fusion(f32[1,65,8,256]{3,2,1,0:T(8,128)S(1)} %get-tuple-element.8), kind=kOutput, calls=%fused_computation.27 | convolution fusion | flops 205389824 | bytes 1064960 | tf_op jit(solution)/shard_map/kgm,mr->kgr/dot_general | solution.py:49
  65.5 1.6 %fusion.17 = f32[65,8,256]{2,1,0:T(8,128)S(1)} fusion(f32[1,65,8,256]{3,2,1,0:T(8,128)S(1)} %get-tuple-element.7), kind=kOutput, calls=%fused_computation.31 | convolution fusion | flops 205389824 | bytes 1064960 | tf_op jit(solution)/shard_map/kgm,mr->kgr/dot_general | solution.py:46
  67.1 1.4 %convolution_subtract_fusion.1 = f32[65,8,256]{2,1,0:T(8,128)S(1)} fusion(f32[65,8,256]{2,1,0:T(8,128)S(1)} %fusion.13, f32[1,65,8,256]{3,2,1,0:T(8,128)S(1)} %get-tuple-element.7), kind=kOutput, calls=%fused_computation.9 | convolution fusion | flops 205522944 | bytes 1597440 | tf_op jit(solution)/shard_map/kgm,mr->kgr/dot_general | solution.py:49
  68.4 1.4 %multiply_subtract_fusion.1 = (f32[65,8,256]{2,1,0:T(8,128)S(1)}, f32[65,8,256]{2,1,0:T(8,128)S(1)}) fusion(f32[65,8,256]{2,1,0:T(8,128)S(1)} %convolution_subtract_fusion.1, f32[65,256]{1,0:T(8,128)S(1)} %get-tuple-element.14, f32[65,256]{1,0:T(8,128)S(1)} %get-tuple-element.15, f32[65,8,256]{2,1,0:T(8,128)S(1)} %fusion.17, ...), kind=kOutput, calls=%fused_computation.33 | convolution fusion | flops 206321664 | bytes 2795520 | tf_op jit(solution)/shard_map/kgm,mr->kgr/dot_general | solution.py:46
  69.9 0.6 fusion.11
  70.4 0.6 convolution_subtract_fusion.2
  71.0 0.3 copy.36
  71.3 24.0 %all_to_all.10 = f32[64,8,256]{2,1,0:T(8,128)S(1)} all-to-all(f32[64,8,256]{2,1,0:T(8,128)S(1)} %copy.36), channel_id=1, replica_groups=mesh['seq'=64,'ch'=8] {'seq'}, dimensions={0} | all-to-all | bytes 1048576 | tf_op jit(solution)/shard_map/all_to_all | solution.py:81
  95.3 0.1 fusion.20
  95.5 0.8 copy.37
  (5 shorter events, 0.0 us)
Async XLA Ops:
  0.0 7.7 %copy-start = (f32[256,512]{1,0:T(8,128)S(1)}, f32[256,512]{1,0:T(8,128)}, u32[]{:S(2)}) copy-start(f32[256,512]{1,0:T(8,128)} %param.7) | copy-start | bytes 1572868
  1.1 9.4 %collective-permute-start = (bf16[2,3,512]{0,2,1:T(8,128)(2,1)S(1)}, bf16[2,3,512]{0,2,1:T(8,128)(2,1)S(1)}, u32[]{:S(2)}, u32[]{:S(2)}) collective-permute-start(bf16[2,3,512]{0,2,1:T(8,128)(2,1)S(1)} %copy.24), channel_id=1, source_target_pairs={{0,8},{8,16},{16,24},{24,32},{32,40},{40,48},{48,56},{56,64},{64,7... | collective-permute-start | bytes 18440 | tf_op jit(solution)/shard_map/ppermute | solution.py:14
  13.9 40.2 %all-to-all-start = ((f32[64,2,8,256]{3,2,1,0:T(8,128)}), f32[64,2,8,256]{3,2,1,0:T(8,128)S(1)}, u32[]{:S(2)}, u32[]{:S(2)}) async-start(f32[64,2,8,256]{3,2,1,0:T(8,128)} %copy.27), calls=%async_computation | async-start | bytes 2097152 | tf_op jit(solution)/shard_map/all_to_all | solution.py:79
  71.0 24.3 %copy-start.1 = (f32[512]{0:T(512)S(1)}, f32[512]{0:T(512)}, u32[]{:S(2)}) copy-start(f32[512]{0:T(512)} %param.6) | copy-start | bytes 6148

commit v2 on v1

--- a/solution.py
+++ b/solution.py
@@ -1,11 +1,14 @@
+import functools
 import math
 
 import jax
 import jax.numpy as jnp
 from jax import lax
+from jax.experimental import pallas as pl
+from jax.experimental.pallas import tpu as pltpu
 from jax.sharding import PartitionSpec as P
 
-PRECISION = lax.Precision.HIGH
+PRECISION = lax.Precision.HIGHEST
 
 
 def shifted(block, axis, distance):
@@ -20,6 +23,73 @@
     phase = out_idx * in_idx % modulus
     angles = sign * 2.0 * math.pi / modulus * phase.astype(jnp.float32)
     return jnp.cos(angles), jnp.sin(angles)
+
+
+def exchange_kernel(shards, x_ref, o_ref, send_sem, recv_sem, own_sem):
+    me = lax.axis_index("seq")
+    row = lax.axis_index("ch")
+    mesh_id = pl.DeviceIdType.MESH
+    barrier = pltpu.get_barrier_semaphore()
+
+    def peer_of(step):
+        return lax.rem(me + 1 + step, shards)
+
+    def greet(step, carry):
+        pl.semaphore_signal(barrier, inc=1, device_id=(peer_of(step), row), device_id_type=mesh_id)
+        return carry
+
+    lax.fori_loop(0, shards - 1, greet, 0)
+    pl.semaphore_wait(barrier, shards - 1)
+    own = pltpu.make_async_copy(x_ref.at[me], o_ref.at[me], own_sem)
+    own.start()
+
+    def copy_to(peer):
+        return pltpu.make_async_remote_copy(
+            src_ref=x_ref.at[peer],
+            dst_ref=o_ref.at[me],
+            send_sem=send_sem.at[peer],
+            recv_sem=recv_sem.at[me],
+            device_id=(peer, row),
+            device_id_type=mesh_id,
+        )
+
+    def send(step, carry):
+        copy_to(peer_of(step)).start()
+        return carry
+
+    lax.fori_loop(0, shards - 1, send, 0)
+
+    def finish(step, carry):
+        peer = peer_of(step)
+        copy_to(peer).wait_send()
+        pltpu.make_async_remote_copy(
+            src_ref=x_ref.at[peer],
+            dst_ref=o_ref.at[peer],
+            send_sem=send_sem.at[peer],
+            recv_sem=recv_sem.at[peer],
+            device_id=(peer, row),
+            device_id_type=mesh_id,
+        ).wait_recv()
+        return carry
+
+    lax.fori_loop(0, shards - 1, finish, 0)
+    own.wait()
+
+
+def exchange(x, collective_id):
+    shards = x.shape[0]
+    return pl.pallas_call(
+        functools.partial(exchange_kernel, shards),
+        out_shape=jax.ShapeDtypeStruct(x.shape, x.dtype),
+        in_specs=[pl.BlockSpec(memory_space=pl.ANY)],
+        out_specs=pl.BlockSpec(memory_space=pl.ANY),
+        scratch_shapes=[
+            pltpu.SemaphoreType.DMA((shards,)),
+            pltpu.SemaphoreType.DMA((shards,)),
+            pltpu.SemaphoreType.DMA(()),
+        ],
+        compiler_params=pltpu.CompilerParams(collective_id=collective_id, has_side_effects=True),
+    )(x)
 
 
 def long_conv(pieces):
@@ -76,9 +146,9 @@
     query = feat[:, 0, :]
     signal = feat[:, 1, :] * feat[:, 2, :]
     source = jnp.stack([signal, filt]).reshape(2, rows, shards, group).transpose(2, 0, 3, 1)
-    pieces = lax.all_to_all(source, "seq", split_axis=0, concat_axis=0, tiled=True)
+    pieces = exchange(source, 0)
     values = long_conv(pieces)
-    back = lax.all_to_all(values, "seq", split_axis=0, concat_axis=0, tiled=True)
+    back = exchange(values, 1)
     conv = back.reshape(width, rows).T
     return (query * (conv + skip * signal)).astype(jnp.bfloat16)
 

time: 96.7 us -> 95.5 us (0.988)
  Pallas kernels: 0 us -> 57.6 us
  waiting for transfers between devices: 30 us -> 2 us
  blocking collectives: 24 us -> 0 us
  starting transfers between devices: 16.9 us -> 4.51 us
  matrix products: 16.7 us -> 22 us
  other arithmetic: 2.86 us -> 4.59 us
  local copies, waits for them, and re-layouts: 5.69 us -> 4.24 us
    pallas_call x0 -> x2, Pallas kernels: none -> 57.6 us  [exchange(): pl.pallas_call(functools.partial(exchange_kernel, shards), out_shape=jax....]
    all_to_all x1 -> x0, waiting for transfers between devices: 27.5 us -> none  [on_device(): lax.all_to_all(source, 'seq', split_axis=0, concat_axis=0, tiled=True)]
    all_to_all x1 -> x0, blocking collectives: 24 us -> none  [on_device(): lax.all_to_all(values, 'seq', split_axis=0, concat_axis=0, tiled=True)]
    all_to_all x1 -> x0, starting transfers between devices: 12.4 us -> none  [on_device(): lax.all_to_all(source, 'seq', split_axis=0, concat_axis=0, tiled=True)]
    dot_general x1, matrix products: 1.27 us -> 3.18 us  [long_conv(): y_re = jnp.einsum('kd,dsgr->skgr', cos1, pieces, precision=PRECISION)]
    sub x1, other arithmetic: 0.14 us -> 1.38 us  [long_conv(): jnp.einsum('dk,kgr->dgr', cos3, q_re, precision=PRECISION)]
    reshape x0 -> x1, local copies, waits for them, and re-layouts: none -> 1.24 us  [on_device(): conv = back.reshape(width, rows).T]
    add x1, other arithmetic: 1.62 us -> 0.47 us  [on_device(): feat = feat + short_w[tap] * extended[taps - 1 - tap:taps - 1 - tap + rows]]
  transfers between devices with their start and end apart: 2 -> 1, of which waited for: 2 -> 1; matrix products, arithmetic and copies ran while one was open for 3% -> 2% of each run, Pallas kernels for 0% -> 0%
where the time goes in v2:
time: 95.5 us; the launch traced here: 95.1 us
  Pallas kernels  57.6 us (60%)
  matrix products  22 us (23%)
  other arithmetic  4.59 us (5%)
  starting transfers between devices  4.51 us (5%)
  local copies, waits for them, and re-layouts  4.24 us (4%)
  waiting for transfers between devices  2 us (2%)
    pallas_call x2, Pallas kernels, exchange(): pl.pallas_call(functools.partial(exchange_kernel, shards), out_shape=jax....  57.6 us
    ppermute x1, starting transfers between devices, shifted(): return lax.ppermute(block, axis, route)  4.51 us
    dot_general x1, matrix products, long_conv(): y_re = jnp.einsum('kd,dsgr->skgr', cos1, pieces, precision=PRECISION)  3.18 us
    dot_general x1, matrix products, long_conv(): jnp.einsum('skgr,rm->skgm', y_re, sin2, precision=PRECISION)  2.31 us
    dot_general x1, matrix products, long_conv(): y_im = jnp.einsum('kd,dsgr->skgr', sin1, pieces, precision=PRECISION)  2.14 us
    dot_general x1, matrix products, long_conv(): jnp.einsum('skgr,rm->skgm', y_im, sin2, precision=PRECISION)  2.13 us
    dot_general x1, matrix products, long_conv(): jnp.einsum('skgr,rm->skgm', y_im, cos2, precision=PRECISION)  2.12 us
    dot_general x1, matrix products, long_conv(): jnp.einsum('skgr,rm->skgm', y_re, cos2, precision=PRECISION)  2.12 us
  transfers between devices with their start and end apart: 1, of which 1 were waited for; matrix products, arithmetic and copies ran while one was open for 2% of the time, Pallas kernels for 0%

profile of v2, /device:TPU:1, one launch (start us, length us, event | category | flops | bytes accessed | tf_op | source)
XLA Modules:
  0.0 95.1 jit_solution(9906128263059711929)
XLA Ops:
  0.0 0.8 slice.47
  0.8 4.5 %collective-permute-start = (bf16[2,3,512]{2,0,1:T(2,128)(2,1)S(1)}, bf16[2,3,512]{2,0,1:T(2,128)(2,1)S(1)}, u32[]{:S(2)}, u32[]{:S(2)}) collective-permute-start(bf16[2,3,512]{2,0,1:T(2,128)(2,1)S(1)} %slice.47), channel_id=1, source_target_pairs={{0,8},{8,16},{16,24},{24,32},{32,40},{40,48},{48,56},{56,64},{64,7... | collective-permute-start | bytes 18440 | tf_op jit(solution)/shard_map/ppermute | solution.py:17
  5.3 0.3 fusion.53
  5.7 0.7 slice_bitcast_fusion.3
  6.4 1.2 %copy.6 = f32[256,512]{0,1:T(8,128)S(1)} copy(f32[256,512]{1,0:T(8,128)} %param.7) | data formatting | bytes 1048576 | tf_op args[3]
  7.6 2.0 %collective-permute-done = bf16[2,3,512]{2,0,1:T(2,128)(2,1)S(1)} collective-permute-done((bf16[2,3,512]{2,0,1:T(2,128)(2,1)S(1)}, bf16[2,3,512]{2,0,1:T(2,128)(2,1)S(1)}, u32[]{:S(2)}, u32[]{:S(2)}) %collective-permute-start) | collective-permute-done | bytes 6176 | tf_op jit(solution)/shard_map/ppermute | solution.py:17
  9.6 0.0 copy-done.1
  9.6 0.2 maximum_convert_fusion
  9.9 0.5 fusion
  10.4 0.1 slice_multiply_fusion.3
  10.4 0.2 copy.5
  10.7 1.0 %maximum_bitcast_fusion.x_ref = f32[64,2,8,256]{3,2,1,0:T(8,128)} fusion(f32[1,256,64,8]{1,3,0,2:T(8,128)S(1)} %bitcast.86, f32[1,256,64,8]{1,3,0,2:T(8,128)S(1)} %bitcast.87), kind=kLoop, calls=%fused_computation.13 | loop fusion | flops 262144 | bytes 2097152 | tf_op jit(solution)/shard_map/transpose | solution.py:148
  11.7 34.6 %shard_map.46 = f32[64,2,8,256]{3,2,1,0:T(8,128)} custom-call(f32[64,2,8,256]{3,2,1,0:T(8,128)} %maximum_bitcast_fusion.x_ref), custom_call_target="tpu_custom_call" | custom-call | tf_op jit(solution)/shard_map/pallas_call | solution.py:81
  46.3 0.0 copy-start
  46.3 3.2 %convolution_bitcast_fusion.1 = f32[2,65,8,256]{3,1,2,0:T(8,128)S(1)} fusion(f32[64,2,8,256]{3,2,1,0:T(8,128)} %shard_map.46), kind=kOutput, calls=%fused_computation.6 | convolution fusion | flops 204530560 | bytes 2113536 | tf_op jit(solution)/shard_map/kd,dsgr->skgr/dot_general | solution.py:101
  49.5 0.0 copy-done
  49.5 2.1 %multiply_subtract_fusion = (f32[2,65,8,256]{3,1,2,0:T(8,128)S(1)}, f32[2,65,8,256]{3,1,2,0:T(8,128)S(1)}) fusion(f32[2,65,8,256]{3,1,2,0:T(8,128)S(1)} %convolution_bitcast_fusion.1, f32[65,256]{1,0:T(8,128)S(1)} %get-tuple-element.14, f32[65,256]{1,0:T(8,128)S(1)} %get-tuple-element.15, f32[64,2,8,256]{3,2,1,0:T(8,128)S(1)} %copy-done), kind=kOutput, calls=%fused_computation.12 | convolution fusion | flops 206128000 | bytes 4376576 | tf_op jit(solution)/shard_map/kd,dsgr->skgr/dot_general | solution.py:102
  51.6 2.1 %fusion.8 = f32[2,65,8,256]{3,2,1,0:T(8,128)S(1)} fusion(f32[2,65,8,256]{3,1,2,0:T(8,128)S(1)} %get-tuple-element.5), kind=kOutput, calls=%fused_computation.20 | convolution fusion | flops 818806784 | bytes 2129920 | tf_op jit(solution)/shard_map/skgr,rm->skgm/dot_general | solution.py:108
  53.8 2.1 %fusion.4 = f32[2,65,8,256]{3,2,1,0:T(8,128)S(1)} fusion(f32[2,65,8,256]{3,1,2,0:T(8,128)S(1)} %get-tuple-element.6), kind=kOutput, calls=%fused_computation.16 | convolution fusion | flops 818806784 | bytes 2129920 | tf_op jit(solution)/shard_map/skgr,rm->skgm/dot_general | solution.py:111
  55.9 2.1 %convolution_subtract_fusion = f32[2,65,8,256]{3,2,1,0:T(8,128)S(1)} fusion(f32[2,65,8,256]{3,2,1,0:T(8,128)S(1)} %fusion.8, f32[2,65,8,256]{3,1,2,0:T(8,128)S(1)} %get-tuple-element.6), kind=kOutput, calls=%fused_computation.8 | convolution fusion | flops 819073024 | bytes 3194880 | tf_op jit(solution)/shard_map/skgr,rm->skgm/dot_general | solution.py:108
  58.0 2.3 %convolution_add_fusion = f32[2,65,8,256]{3,2,1,0:T(8,128)S(1)} fusion(f32[2,65,8,256]{3,2,1,0:T(8,128)S(1)} %fusion.4, f32[2,65,8,256]{3,1,2,0:T(8,128)S(1)} %get-tuple-element.5), kind=kOutput, calls=%fused_computation.7 | convolution fusion | flops 819073024 | bytes 3194880 | tf_op jit(solution)/shard_map/skgr,rm->skgm/dot_general | solution.py:111
  60.4 0.1 multiply_add_fusion.2
  60.5 1.6 %fusion.18 = f32[65,8,256]{2,1,0:T(8,128)S(1)} fusion(f32[1,65,8,256]{3,2,1,0:T(8,128)S(1)} %get-tuple-element.8), kind=kOutput, calls=%fused_computation.31 | convolution fusion | flops 409862144 | bytes 1064960 | tf_op jit(solution)/shard_map/kgm,mr->kgr/dot_general | solution.py:116
  62.1 1.6 %fusion.14 = f32[65,8,256]{2,1,0:T(8,128)S(1)} fusion(f32[1,65,8,256]{3,2,1,0:T(8,128)S(1)} %get-tuple-element.7), kind=kOutput, calls=%fused_computation.27 | convolution fusion | flops 409862144 | bytes 1064960 | tf_op jit(solution)/shard_map/kgm,mr->kgr/dot_general | solution.py:119
  63.6 1.6 %convolution_add_fusion.1 = f32[65,8,256]{2,1,0:T(8,128)S(1)} fusion(f32[65,8,256]{2,1,0:T(8,128)S(1)} %fusion.18, f32[1,65,8,256]{3,2,1,0:T(8,128)S(1)} %get-tuple-element.7), kind=kOutput, calls=%fused_computation.10 | convolution fusion | flops 409995264 | bytes 1597440 | tf_op jit(solution)/shard_map/kgm,mr->kgr/dot_general | solution.py:116
  65.2 1.7 %multiply_add_fusion.1 = (f32[65,8,256]{2,1,0:T(8,128)S(1)}, f32[65,8,256]{2,1,0:T(8,128)S(1)}) fusion(f32[65,8,256]{2,1,0:T(8,128)S(1)} %convolution_add_fusion.1, f32[65,256]{1,0:T(8,128)S(1)} %get-tuple-element.14, f32[65,256]{1,0:T(8,128)S(1)} %get-tuple-element.15, f32[65,8,256]{2,1,0:T(8,128)S(1)} %fusion.14, f32[1,65,8,256]{3,2,1,0:T(8,128)S(1)} %get-tuple-element.8), kind=kOutput, calls=%fused_computation.34 | convolution fusion | flops 410793984 | bytes 2795520 | tf_op jit(solution)/shard_map/kgm,mr->kgr/dot_general | solution.py:119
  66.9 0.8 fusion.10
  67.7 0.8 fusion.12
  68.5 1.4 %copy_subtract_fusion.x_ref = f32[64,8,256]{2,1,0:T(8,128)} fusion(f32[64,8,256]{2,0,1:T(8,128)S(1)} %fusion.10, f32[64,8,256]{2,0,1:T(8,128)S(1)} %fusion.12), kind=kLoop, calls=%fused_computation.43 | loop fusion | flops 131072 | bytes 1572864 | tf_op jit(solution)/shard_map/sub | solution.py:131
  69.9 23.0 %shard_map.47 = f32[64,8,256]{2,1,0:T(8,128)} custom-call(f32[64,8,256]{2,1,0:T(8,128)} %copy_subtract_fusion.x_ref), custom_call_target="tpu_custom_call" | custom-call | tf_op jit(solution)/shard_map/pallas_call | solution.py:81
  92.9 1.2 %copy.17 = f32[512,256]{0,1:T(8,128)S(1)} copy(f32[512,256]{1,0:T(8,128)} %bitcast.85) | data formatting | bytes 1048576 | tf_op jit(solution)/shard_map/reshape | solution.py:152
  94.2 0.9 fusion.21
  (4 shorter events, 0.0 us)
Async XLA Ops:
  0.0 9.6 %copy-start.1 = (bf16[256,3,512]{2,0,1:T(8,128)(2,1)S(1)}, bf16[256,3,512]{2,0,1:T(8,128)(2,1)}, u32[]{:S(2)}) copy-start(bf16[256,3,512]{2,0,1:T(8,128)(2,1)} %param.4) | copy-start | bytes 2359300
  0.8 8.8 %collective-permute-start = (bf16[2,3,512]{2,0,1:T(2,128)(2,1)S(1)}, bf16[2,3,512]{2,0,1:T(2,128)(2,1)S(1)}, u32[]{:S(2)}, u32[]{:S(2)}) collective-permute-start(bf16[2,3,512]{2,0,1:T(2,128)(2,1)S(1)} %slice.47), channel_id=1, source_target_pairs={{0,8},{8,16},{16,24},{24,32},{32,40},{40,48},{48,56},{56,64},{64,7... | collective-permute-start | bytes 18440 | tf_op jit(solution)/shard_map/ppermute | solution.py:17
  46.3 3.2 %copy-start = (f32[64,2,8,256]{3,2,1,0:T(8,128)S(1)}, f32[64,2,8,256]{3,2,1,0:T(8,128)}, u32[]{:S(2)}) copy-start(f32[64,2,8,256]{3,2,1,0:T(8,128)} %shard_map.46) | copy-start | bytes 3145732
  69.9 24.3 %copy-start.2 = (f32[512]{0:T(512)S(1)}, f32[512]{0:T(512)}, u32[]{:S(2)}) copy-start(f32[512]{0:T(512)} %param.6) | copy-start | bytes 6148

commit v3 on v2

--- a/solution.py
+++ b/solution.py
@@ -11,12 +11,6 @@
 PRECISION = lax.Precision.HIGHEST
 
 
-def shifted(block, axis, distance):
-    devices = range(lax.axis_size(axis))
-    route = [(i - distance, i) for i in devices if i - distance in devices]
-    return lax.ppermute(block, axis, route)
-
-
 def phase_table(count_out, count_in, modulus, sign):
     out_idx = jnp.arange(count_out, dtype=jnp.int32)[:, None]
     in_idx = jnp.arange(count_in, dtype=jnp.int32)[None, :]
@@ -25,7 +19,10 @@
     return jnp.cos(angles), jnp.sin(angles)
 
 
-def exchange_kernel(shards, x_ref, o_ref, send_sem, recv_sem, own_sem):
+def exchange_kernel(shards, *refs):
+    count = (len(refs) - 2) // 2
+    x_refs, o_refs = refs[:count], refs[count : 2 * count]
+    send_sem, recv_sem = refs[2 * count :]
     me = lax.axis_index("seq")
     row = lax.axis_index("ch")
     mesh_id = pl.DeviceIdType.MESH
@@ -40,56 +37,57 @@
 
     lax.fori_loop(0, shards - 1, greet, 0)
     pl.semaphore_wait(barrier, shards - 1)
-    own = pltpu.make_async_copy(x_ref.at[me], o_ref.at[me], own_sem)
-    own.start()
+    own = [
+        pltpu.make_async_copy(x.at[me], o.at[me], send_sem.at[k, me])
+        for k, (x, o) in enumerate(zip(x_refs, o_refs))
+    ]
+    for copy in own:
+        copy.start()
 
-    def copy_to(peer):
+    def copy_to(k, peer, slot):
         return pltpu.make_async_remote_copy(
-            src_ref=x_ref.at[peer],
-            dst_ref=o_ref.at[me],
-            send_sem=send_sem.at[peer],
-            recv_sem=recv_sem.at[me],
+            src_ref=x_refs[k].at[peer],
+            dst_ref=o_refs[k].at[slot],
+            send_sem=send_sem.at[k, peer],
+            recv_sem=recv_sem.at[k, slot],
             device_id=(peer, row),
             device_id_type=mesh_id,
         )
 
     def send(step, carry):
-        copy_to(peer_of(step)).start()
+        peer = peer_of(step)
+        for k in range(count):
+            copy_to(k, peer, me).start()
         return carry
 
     lax.fori_loop(0, shards - 1, send, 0)
 
     def finish(step, carry):
         peer = peer_of(step)
-        copy_to(peer).wait_send()
-        pltpu.make_async_remote_copy(
-            src_ref=x_ref.at[peer],
-            dst_ref=o_ref.at[peer],
-            send_sem=send_sem.at[peer],
-            recv_sem=recv_sem.at[peer],
-            device_id=(peer, row),
-            device_id_type=mesh_id,
-        ).wait_recv()
+        for k in range(count):
+            copy_to(k, peer, me).wait_send()
+            copy_to(k, peer, peer).wait_recv()
         return carry
 
     lax.fori_loop(0, shards - 1, finish, 0)
-    own.wait()
+    for copy in own:
+        copy.wait()
 
 
-def exchange(x, collective_id):
-    shards = x.shape[0]
+def exchange(xs, collective_id):
+    shards = xs[0].shape[0]
+    count = len(xs)
     return pl.pallas_call(
         functools.partial(exchange_kernel, shards),
-        out_shape=jax.ShapeDtypeStruct(x.shape, x.dtype),
-        in_specs=[pl.BlockSpec(memory_space=pl.ANY)],
-        out_specs=pl.BlockSpec(memory_space=pl.ANY),
+        out_shape=[jax.ShapeDtypeStruct(x.shape, x.dtype) for x in xs],
+        in_specs=[pl.BlockSpec(memory_space=pl.ANY)] * count,
+        out_specs=[pl.BlockSpec(memory_space=pl.ANY)] * count,
         scratch_shapes=[
-            pltpu.SemaphoreType.DMA((shards,)),
-            pltpu.SemaphoreType.DMA((shards,)),
-            pltpu.SemaphoreType.DMA(()),
+            pltpu.SemaphoreType.DMA((count, shards)),
+            pltpu.SemaphoreType.DMA((count, shards)),
         ],
         compiler_params=pltpu.CompilerParams(collective_id=collective_id, has_side_effects=True),
-    )(x)
+    )(*xs)
 
 
 def long_conv(pieces):
@@ -134,23 +132,29 @@
 
 
 def on_device(qkv, short_w, skip, filt):
-    rows, _, width = qkv.shape
+    rows, streams, width = qkv.shape
     taps = short_w.shape[0]
     shards = lax.axis_size("seq")
     group = width // shards
-    rim = shifted(qkv[rows - (taps - 1) :], "seq", 1)
-    extended = jnp.concatenate([rim, qkv], axis=0).astype(jnp.float32)
-    feat = short_w[0] * extended[taps - 1 : taps - 1 + rows]
+    place = lax.axis_index("seq")
+    qkv_out = qkv.reshape(rows, streams, shards, group).transpose(2, 1, 3, 0)
+    filt_out = filt.reshape(rows, shards, group).transpose(1, 2, 0)
+    qkv_in, filt_in = exchange([qkv_out, filt_out], 0)
+    length = shards * rows
+    wide = qkv_in.astype(jnp.float32).transpose(1, 2, 0, 3).reshape(streams, group, length)
+    extended = jnp.pad(wide, ((0, 0), (0, 0), (taps - 1, 0)))
+    weights = lax.dynamic_slice_in_dim(short_w, place * group, group, axis=2)[:, :, :, None]
+    feat = weights[0] * extended[:, :, taps - 1 : taps - 1 + length]
     for tap in range(1, taps):
-        feat = feat + short_w[tap] * extended[taps - 1 - tap : taps - 1 - tap + rows]
-    query = feat[:, 0, :]
-    signal = feat[:, 1, :] * feat[:, 2, :]
-    source = jnp.stack([signal, filt]).reshape(2, rows, shards, group).transpose(2, 0, 3, 1)
-    pieces = exchange(source, 0)
-    values = long_conv(pieces)
-    back = exchange(values, 1)
-    conv = back.reshape(width, rows).T
-    return (query * (conv + skip * signal)).astype(jnp.bfloat16)
+        feat = feat + weights[tap] * extended[:, :, taps - 1 - tap : taps - 1 - tap + length]
+    feat = feat.reshape(streams, group, shards, rows).transpose(0, 2, 1, 3)
+    query = feat[0]
+    signal = feat[1] * feat[2]
+    conv = long_conv(jnp.stack([signal, filt_in], axis=1))
+    gain = lax.dynamic_slice_in_dim(skip, place * group, group)[None, :, None]
+    mixed = (query * (conv + gain * signal)).astype(jnp.bfloat16)
+    (back,) = exchange([mixed], 1)
+    return back.reshape(width, rows).T
 
 
 def solution(mesh):

time: 95.5 us -> 95.9 us (level)
  Pallas kernels: 57.6 us -> 63.4 us
  starting transfers between devices: 4.51 us -> 0 us
  local copies, waits for them, and re-layouts: 4.24 us -> 7.83 us
  matrix products: 22 us -> 20 us
  waiting for transfers between devices: 2 us -> 0 us
    pallas_call x2, Pallas kernels: 57.6 us -> 63.4 us  [exchange(): pl.pallas_call(functools.partial(exchange_kernel, shards), out_shape=[jax...]
    ppermute x1 -> x0, starting transfers between devices: 4.51 us -> none  [shifted(): return lax.ppermute(block, axis, route)]
    unnamed x7 -> x6, local copies, waits for them, and re-layouts: 1.25 us -> 3.42 us
    ppermute x1 -> x0, waiting for transfers between devices: 2 us -> none  [shifted(): return lax.ppermute(block, axis, route)]
    dot_general x1, matrix products: 3.18 us -> 1.56 us  [long_conv(): y_re = jnp.einsum('kd,dsgr->skgr', cos1, pieces, precision=PRECISION)]
    sub x1 -> x0, other arithmetic: 1.38 us -> none  [long_conv(): jnp.einsum('dk,kgr->dgr', cos3, q_re, precision=PRECISION)]
    unnamed x0 -> x1, other arithmetic: none -> 1.25 us
    transpose x1 -> x0, other arithmetic: 1.05 us -> none  [on_device(): jnp.stack([signal, filt]).reshape(2, rows, shards, group)]
  transfers between devices with their start and end apart: 1 -> 0, of which waited for: 1 -> 0; matrix products, arithmetic and copies ran while one was open for 2% -> 0% of each run, Pallas kernels for 0% -> 0%
where the time goes in v3:
time: 95.9 us; the launch traced here: 95.5 us
  Pallas kernels  63.4 us (66%)
  matrix products  20 us (21%)
  local copies, waits for them, and re-layouts  7.83 us (8%)
  other arithmetic  4.1 us (4%)
    pallas_call x2, Pallas kernels, exchange(): pl.pallas_call(functools.partial(exchange_kernel, shards), out_shape=[jax...  63.4 us
    unnamed x6, local copies, waits for them, and re-layouts  3.42 us
    dot_general x1, matrix products, long_conv(): jnp.einsum('skgr,rm->skgm', y_re, sin2, precision=PRECISION)  2.31 us
    dot_general x1, matrix products, long_conv(): jnp.einsum('skgr,rm->skgm', y_im, sin2, precision=PRECISION)  2.13 us
    dot_general x1, matrix products, long_conv(): jnp.einsum('skgr,rm->skgm', y_im, cos2, precision=PRECISION)  2.12 us
    dot_general x1, matrix products, long_conv(): jnp.einsum('skgr,rm->skgm', y_re, cos2, precision=PRECISION)  2.12 us

profile of v3, /device:TPU:1, one launch (start us, length us, event | category | flops | bytes accessed | tf_op | source)
XLA Modules:
  0.0 95.5 jit_solution(588483220724568896)
XLA Ops:
  0.0 0.8 dynamic-slice_bitcast_fusion.2
  0.8 0.0 copy-start
  0.8 1.5 %copy.17 = bf16[256,3,512]{0,2,1:T(8,128)(2,1)S(1)} copy(bf16[256,3,512]{2,0,1:T(8,128)(2,1)} %param.4) | data formatting | bytes 1572864 | tf_op args[0]
  2.3 0.9 copy_bitcast_fusion.refs_0_
  3.2 0.0 copy-done
  3.2 1.0 %copy.19 = f32[256,512]{0,1:T(8,128)} copy(f32[256,512]{1,0:T(8,128)S(1)} %copy-done) | data formatting | bytes 1048576 | tf_op args[3]
  4.2 43.6 %shard_map.46 = (bf16[64,3,8,256]{3,2,1,0:T(8,128)(2,1)}, f32[64,8,256]{2,1,0:T(8,128)}) custom-call(bf16[64,3,8,256]{3,2,1,0:T(8,128)(2,1)} %copy_bitcast_fusion.refs_0_, f32[64,8,256]{2,1,0:T(8,128)} %bitcast.101), custom_call_target="tpu_custom_call" | custom-call | tf_op jit(solution)/shard_map/pallas_call | solution.py:80
  47.7 1.2 %convert_bitcast_fusion = f32[64,3,1,8,256]{4,3,2,1,0:T(8,128)S(1)} fusion(bf16[64,3,8,256]{3,2,1,0:T(8,128)(2,1)} %get-tuple-element.7), kind=kLoop, calls=%fused_computation | loop fusion | flops 393216 | bytes 2359296
  49.0 0.1 copy.36
  49.1 0.9 multiply_add_fusion
  50.0 0.0 copy-start.1
  50.1 0.1 fusion.35
  50.1 1.0 %copy-done.1 = f32[64,8,256]{2,1,0:T(8,128)S(1)} copy-done((f32[64,8,256]{2,1,0:T(8,128)S(1)}, f32[64,8,256]{2,1,0:T(8,128)}, u32[]{:S(2)}) %copy-start.1) | copy-done | bytes 524312
  51.1 0.1 pad_maximum_fusion
  51.2 1.6 %convolution_bitcast_fusion.1 = f32[2,65,8,256]{3,1,2,0:T(8,128)S(1)} fusion(f32[64,2,8,256]{3,2,0,1:T(8,128)S(1)} %pad_maximum_fusion), kind=kOutput, calls=%fused_computation.3 | convolution fusion | flops 204530560 | bytes 2113536 | tf_op jit(solution)/shard_map/kd,dsgr->skgr/dot_general | solution.py:99
  52.7 0.3 fusion.52
  53.0 1.8 %multiply_subtract_fusion = (f32[2,65,8,256]{3,1,2,0:T(8,128)S(1)}, f32[2,65,8,256]{3,1,2,0:T(8,128)S(1)}) fusion(f32[2,65,8,256]{3,1,2,0:T(8,128)S(1)} %convolution_bitcast_fusion.1, f32[65,256]{1,0:T(8,128)S(1)} %get-tuple-element.18, f32[65,256]{1,0:T(8,128)S(1)} %get-tuple-element.19, f32[64,2,8,256]{3,2,0,1:T(8,128)S(1)} %pad_maximum_fusion), kind=kOutput, calls=%fused_computation.9 | convolution fusion | flops 206128000 | bytes 4376576 | tf_op jit(solution)/shard_map/kd,dsgr->skgr/dot_general | solution.py:100
  54.9 2.1 %fusion.6 = f32[2,65,8,256]{3,2,1,0:T(8,128)S(1)} fusion(f32[2,65,8,256]{3,1,2,0:T(8,128)S(1)} %get-tuple-element.9), kind=kOutput, calls=%fused_computation.17 | convolution fusion | flops 818806784 | bytes 2129920 | tf_op jit(solution)/shard_map/skgr,rm->skgm/dot_general | solution.py:106
  57.0 2.1 %convolution_subtract_fusion = f32[2,65,8,256]{3,2,1,0:T(8,128)S(1)} fusion(f32[2,65,8,256]{3,2,1,0:T(8,128)S(1)} %fusion.6, f32[2,65,8,256]{3,1,2,0:T(8,128)S(1)} %get-tuple-element.10), kind=kOutput, calls=%fused_computation.5 | convolution fusion | flops 819073024 | bytes 3194880 | tf_op jit(solution)/shard_map/skgr,rm->skgm/dot_general | solution.py:106
  59.1 2.1 %fusion.2 = f32[2,65,8,256]{3,2,1,0:T(8,128)S(1)} fusion(f32[2,65,8,256]{3,1,2,0:T(8,128)S(1)} %get-tuple-element.10), kind=kOutput, calls=%fused_computation.13 | convolution fusion | flops 818806784 | bytes 2129920 | tf_op jit(solution)/shard_map/skgr,rm->skgm/dot_general | solution.py:109
  61.3 2.3 %convolution_add_fusion = f32[2,65,8,256]{3,2,1,0:T(8,128)S(1)} fusion(f32[2,65,8,256]{3,2,1,0:T(8,128)S(1)} %fusion.2, f32[2,65,8,256]{3,1,2,0:T(8,128)S(1)} %get-tuple-element.9), kind=kOutput, calls=%fused_computation.4 | convolution fusion | flops 819073024 | bytes 3194880 | tf_op jit(solution)/shard_map/skgr,rm->skgm/dot_general | solution.py:109
  63.6 0.1 multiply_add_fusion.3
  63.7 1.6 %fusion.16 = f32[65,8,256]{2,1,0:T(8,128)S(1)} fusion(f32[1,65,8,256]{3,2,1,0:T(8,128)S(1)} %get-tuple-element.12), kind=kOutput, calls=%fused_computation.28 | convolution fusion | flops 409862144 | bytes 1064960 | tf_op jit(solution)/shard_map/kgm,mr->kgr/dot_general | solution.py:114
  65.3 1.6 %convolution_add_fusion.1 = f32[65,8,256]{2,1,0:T(8,128)S(1)} fusion(f32[65,8,256]{2,1,0:T(8,128)S(1)} %fusion.16, f32[1,65,8,256]{3,2,1,0:T(8,128)S(1)} %get-tuple-element.11), kind=kOutput, calls=%fused_computation.7 | convolution fusion | flops 409995264 | bytes 1597440 | tf_op jit(solution)/shard_map/kgm,mr->kgr/dot_general | solution.py:114
  66.9 1.6 %fusion.12 = f32[65,8,256]{2,1,0:T(8,128)S(1)} fusion(f32[1,65,8,256]{3,2,1,0:T(8,128)S(1)} %get-tuple-element.11), kind=kOutput, calls=%fused_computation.24 | convolution fusion | flops 409862144 | bytes 1064960 | tf_op jit(solution)/shard_map/kgm,mr->kgr/dot_general | solution.py:117
  68.5 1.7 %multiply_add_fusion.2 = (f32[65,8,256]{2,1,0:T(8,128)S(1)}, f32[65,8,256]{2,1,0:T(8,128)S(1)}) fusion(f32[65,8,256]{2,1,0:T(8,128)S(1)} %convolution_add_fusion.1, f32[65,256]{1,0:T(8,128)S(1)} %get-tuple-element.18, f32[65,256]{1,0:T(8,128)S(1)} %get-tuple-element.19, f32[65,8,256]{2,1,0:T(8,128)S(1)} %fusion.12, f32[1,65,8,256]{3,2,1,0:T(8,128)S(1)} %get-tuple-element.12), kind=kOutput, calls=%fused_computation.31 | convolution fusion | flops 410793984 | bytes 2795520 | tf_op jit(solution)/shard_map/kgm,mr->kgr/dot_general | solution.py:117
  70.1 0.8 fusion.10
  71.0 0.8 fusion.8
  71.8 0.8 dynamic_slice.7
  72.5 1.4 %fusion.19.refs_0_ = bf16[64,8,256]{2,1,0:T(8,128)(2,1)} fusion(f32[3,64,8,256]{3,2,1,0:T(8,128)S(1)} %bitcast.99, f32[64,8,256]{2,0,1:T(8,128)S(1)} %fusion.8, f32[64,8,256]{2,0,1:T(8,128)S(1)} %fusion.10, f32[8]{0:T(128)S(1)} %dynamic_slice.7), kind=kLoop, calls=%fused_computation.37 | loop fusion | flops 786432 | bytes 2883616 | tf_op jit(solution)/shard_map/convert_element_type | solution.py:155
  73.9 19.8 %shard_map.47 = bf16[64,8,256]{2,1,0:T(8,128)(2,1)} custom-call(bf16[64,8,256]{2,1,0:T(8,128)(2,1)} %fusion.19.refs_0_), custom_call_target="tpu_custom_call" | custom-call | tf_op jit(solution)/shard_map/pallas_call | solution.py:80
  93.7 1.8 %copy.31 = bf16[512,256]{0,1:T(8,128)(2,1)} copy(bf16[512,256]{1,0:T(8,128)(2,1)} %bitcast.102) | data formatting | bytes 524288 | tf_op jit(solution)/shard_map/reshape | solution.py:157
  (1 shorter events, 0.0 us)
Async XLA Ops:
  0.8 2.4 %copy-start = (f32[256,512]{1,0:T(8,128)S(1)}, f32[256,512]{1,0:T(8,128)}, u32[]{:S(2)}) copy-start(f32[256,512]{1,0:T(8,128)} %param.7) | copy-start | bytes 1572868
  50.0 1.0 %copy-start.1 = (f32[64,8,256]{2,1,0:T(8,128)S(1)}, f32[64,8,256]{2,1,0:T(8,128)}, u32[]{:S(2)}) copy-start(f32[64,8,256]{2,1,0:T(8,128)} %get-tuple-element.8) | copy-start | bytes 1572868

commit v4 on v3

--- a/solution.py
+++ b/solution.py
@@ -90,45 +90,76 @@
     )(*xs)
 
 
+def conv_kernel(
+    x_ref, c1_ref, s1_ref, twc_ref, tws_ref, vc_ref, vs_ref, ci_ref, si_ref, o_ref, yre_ref, yim_ref
+):
+    streams = x_ref.shape[0]
+    group = streams // 2
+    pad = c1_ref.shape[0]
+
+    def dot(a, b):
+        return jnp.dot(a, b, precision=PRECISION, preferred_element_type=jnp.float32)
+
+    twc = twc_ref[...]
+    tws = tws_ref[...]
+    c1 = c1_ref[...]
+    s1 = s1_ref[...]
+    for j in range(streams):
+        xj = x_ref[j]
+        a = dot(c1, xj)
+        b = dot(s1, xj)
+        yre_ref[j * pad : (j + 1) * pad, :] = a * twc - b * tws
+        yim_ref[j * pad : (j + 1) * pad, :] = a * tws + b * twc
+    vc = vc_ref[...]
+    vs = vs_ref[...]
+    yre = yre_ref[...]
+    yim = yim_ref[...]
+    zre = dot(yre, vc) - dot(yim, vs)
+    zim = dot(yim, vc) + dot(yre, vs)
+    half = group * pad
+    pre = zre[:half] * zre[half:] - zim[:half] * zim[half:]
+    pim = zre[:half] * zim[half:] + zim[:half] * zre[half:]
+    qre = dot(pre, vc) + dot(pim, vs)
+    qim = dot(pim, vc) - dot(pre, vs)
+    ci = ci_ref[...]
+    si = si_ref[...]
+    for g in range(group):
+        ure = qre[g * pad : (g + 1) * pad]
+        uim = qim[g * pad : (g + 1) * pad]
+        vre = ure * twc + uim * tws
+        vim = uim * twc - ure * tws
+        o_ref[g] = dot(ci, vre) - dot(si, vim)
+
+
 def long_conv(pieces):
-    blocks, _, group, rows = pieces.shape
+    streams, blocks, rows = pieces.shape
+    group = streams // 2
     coarse = 2 * blocks
     total = coarse * rows
     half = blocks + 1
-    cos1, sin1 = phase_table(half, blocks, coarse, -1.0)
-    y_re = jnp.einsum("kd,dsgr->skgr", cos1, pieces, precision=PRECISION)
-    y_im = jnp.einsum("kd,dsgr->skgr", sin1, pieces, precision=PRECISION)
-    tw_cos, tw_sin = phase_table(half, rows, total, -1.0)
-    tw_cos = tw_cos[None, :, None, :]
-    tw_sin = tw_sin[None, :, None, :]
-    y_re, y_im = y_re * tw_cos - y_im * tw_sin, y_re * tw_sin + y_im * tw_cos
-    cos2, sin2 = phase_table(rows, rows, rows, -1.0)
-    z_re = jnp.einsum("skgr,rm->skgm", y_re, cos2, precision=PRECISION) - jnp.einsum(
-        "skgr,rm->skgm", y_im, sin2, precision=PRECISION
-    )
-    z_im = jnp.einsum("skgr,rm->skgm", y_im, cos2, precision=PRECISION) + jnp.einsum(
-        "skgr,rm->skgm", y_re, sin2, precision=PRECISION
-    )
-    p_re = z_re[0] * z_re[1] - z_im[0] * z_im[1]
-    p_im = z_re[0] * z_im[1] + z_im[0] * z_re[1]
-    q_re = jnp.einsum("kgm,mr->kgr", p_re, cos2, precision=PRECISION) + jnp.einsum(
-        "kgm,mr->kgr", p_im, sin2, precision=PRECISION
-    )
-    q_im = jnp.einsum("kgm,mr->kgr", p_im, cos2, precision=PRECISION) - jnp.einsum(
-        "kgm,mr->kgr", p_re, sin2, precision=PRECISION
-    )
-    tw_cos = tw_cos[0]
-    tw_sin = tw_sin[0]
-    q_re, q_im = q_re * tw_cos + q_im * tw_sin, q_im * tw_cos - q_re * tw_sin
-    weight = jnp.where(
-        (jnp.arange(half) == 0) | (jnp.arange(half) == blocks), 1.0, 2.0
-    ).astype(jnp.float32) / total
-    cos3, sin3 = phase_table(blocks, half, coarse, 1.0)
-    cos3 = cos3 * weight[None, :]
-    sin3 = sin3 * weight[None, :]
-    return jnp.einsum("dk,kgr->dgr", cos3, q_re, precision=PRECISION) - jnp.einsum(
-        "dk,kgr->dgr", sin3, q_im, precision=PRECISION
-    )
+    pad = -(-half // 8) * 8
+    live = (jnp.arange(pad) < half).astype(jnp.float32)
+    c1, s1 = phase_table(pad, blocks, coarse, -1.0)
+    c1 = c1 * live[:, None]
+    s1 = s1 * live[:, None]
+    twc, tws = phase_table(pad, rows, total, -1.0)
+    vc, vs = phase_table(rows, rows, rows, -1.0)
+    k1 = jnp.arange(pad)
+    weight = jnp.where((k1 == 0) | (k1 == blocks), 1.0, 2.0) * live / total
+    ci, si = phase_table(blocks, pad, coarse, 1.0)
+    ci = ci * weight[None, :]
+    si = si * weight[None, :]
+    vmem = pl.BlockSpec(memory_space=pltpu.VMEM)
+    return pl.pallas_call(
+        conv_kernel,
+        out_shape=jax.ShapeDtypeStruct((group, blocks, rows), jnp.float32),
+        in_specs=[vmem] * 9,
+        out_specs=vmem,
+        scratch_shapes=[
+            pltpu.VMEM((streams * pad, rows), jnp.float32),
+            pltpu.VMEM((streams * pad, rows), jnp.float32),
+        ],
+    )(pieces, c1, s1, twc, tws, vc, vs, ci, si)
 
 
 def on_device(qkv, short_w, skip, filt):
@@ -150,7 +181,8 @@
     feat = feat.reshape(streams, group, shards, rows).transpose(0, 2, 1, 3)
     query = feat[0]
     signal = feat[1] * feat[2]
-    conv = long_conv(jnp.stack([signal, filt_in], axis=1))
+    pieces = jnp.concatenate([signal, filt_in], axis=1).transpose(1, 0, 2)
+    conv = long_conv(pieces).transpose(1, 0, 2)
     gain = lax.dynamic_slice_in_dim(skip, place * group, group)[None, :, None]
     mixed = (query * (conv + gain * signal)).astype(jnp.bfloat16)
     (back,) = exchange([mixed], 1)

time: 95.9 us -> 96.7 us (level)
  matrix products: 20 us -> 0 us
  Pallas kernels: 63.4 us -> 78.1 us
  other arithmetic: 4.1 us -> 8.68 us
  local copies, waits for them, and re-layouts: 7.83 us -> 9.41 us
    dot_general x12 -> x0, matrix products: 20 us -> none  [the longest x1 2.31 us: long_conv(): jnp.einsum('skgr,rm->skgm', y_re, sin2, precision=PRECISION)]
    pallas_call x0 -> x1, Pallas kernels: none -> 14.8 us  [long_conv(): pl.pallas_call(conv_kernel, out_shape=jax.ShapeDtypeStruct((group, blocks...]
    sin x1 -> x2, other arithmetic: 0.31 us -> 2.72 us  [phase_table(): return (jnp.cos(angles), jnp.sin(angles))]
    mul x0 -> x2, other arithmetic: none -> 1.59 us  [the longest x1 0.82 us: long_conv(): s1 = s1 * live[:, None]]
    transpose x0 -> x1, local copies, waits for them, and re-layouts: none -> 1.58 us  [on_device(): pieces = jnp.concatenate([signal, filt_in], axis=1).transpose(1, 0, 2)]
where the time goes in v4:
time: 96.7 us; the launch traced here: 96.3 us
  Pallas kernels  78.1 us (81%)
  local copies, waits for them, and re-layouts  9.41 us (10%)
  other arithmetic  8.68 us (9%)
    pallas_call x2, Pallas kernels, exchange(): pl.pallas_call(functools.partial(exchange_kernel, shards), out_shape=[jax...  63.4 us
    pallas_call x1, Pallas kernels, long_conv(): pl.pallas_call(conv_kernel, out_shape=jax.ShapeDtypeStruct((group, blocks...  14.8 us
    unnamed x6, local copies, waits for them, and re-layouts  3.42 us
    sin x2, other arithmetic, phase_table(): return (jnp.cos(angles), jnp.sin(angles))  2.72 us
    convert_element_type x1, other arithmetic, on_device(): mixed = (query * (conv + gain * signal)).astype(jnp.bfloat16)  2.08 us

profile of v4, /device:TPU:1, one launch (start us, length us, event | category | flops | bytes accessed | tf_op | source)
XLA Modules:
  0.0 96.3 jit_solution(8396258737503787769)
XLA Ops:
  0.0 0.8 dynamic-slice_bitcast_fusion.2
  0.8 0.0 copy-start
  0.8 1.5 %copy.9 = bf16[256,3,512]{0,2,1:T(8,128)(2,1)S(1)} copy(bf16[256,3,512]{2,0,1:T(8,128)(2,1)} %param.4) | data formatting | bytes 1572864 | tf_op args[0]
  2.3 0.9 copy_bitcast_fusion.refs_0_
  3.2 0.0 copy-done
  3.2 1.0 %copy.11 = f32[256,512]{0,1:T(8,128)} copy(f32[256,512]{1,0:T(8,128)S(1)} %copy-done) | data formatting | bytes 1048576 | tf_op args[3]
  4.2 43.6 %shard_map.46 = (bf16[64,3,8,256]{3,2,1,0:T(8,128)(2,1)}, f32[64,8,256]{2,1,0:T(8,128)}) custom-call(bf16[64,3,8,256]{3,2,1,0:T(8,128)(2,1)} %copy_bitcast_fusion.refs_0_, f32[64,8,256]{2,1,0:T(8,128)} %bitcast.42), custom_call_target="tpu_custom_call" | custom-call | tf_op jit(solution)/shard_map/pallas_call | solution.py:80
  47.7 1.2 %convert_bitcast_fusion = f32[64,3,1,8,256]{4,3,2,1,0:T(8,128)S(1)} fusion(bf16[64,3,8,256]{3,2,1,0:T(8,128)(2,1)} %get-tuple-element.7), kind=kLoop, calls=%fused_computation | loop fusion | flops 393216 | bytes 2359296
  49.0 0.1 copy.16
  49.1 0.9 multiply_add_fusion
  50.0 0.0 copy-start.1
  50.1 0.1 fusion
  50.1 1.0 copy-done.1
  51.1 0.1 maximum_bitcast_fusion
  51.2 1.6 %copy.13.x_ref = f32[16,64,256]{2,1,0:T(8,128)} copy(f32[16,64,256]{2,0,1:T(8,128)S(1)} %maximum_bitcast_fusion) | data formatting | bytes 2097152 | tf_op jit(solution)/shard_map/transpose | solution.py:184
  52.8 1.8 %fusion.9 = (f32[256,256]{1,0:T(8,128)}, f32[256,256]{1,0:T(8,128)}) fusion(), kind=kLoop, calls=%fused_computation.19 | loop fusion | flops 917504 | bytes 524288 | tf_op jit(solution)/shard_map/sin | solution.py:19
  54.5 1.0 %fusion.20 = (f32[72,256]{1,0:T(8,128)}, f32[72,256]{1,0:T(8,128)}) fusion(), kind=kLoop, calls=%fused_computation.39 | loop fusion | flops 258048 | bytes 147456 | tf_op jit(solution)/shard_map/sin | solution.py:19
  55.5 0.8 sine_multiply_fusion
  56.3 0.8 sine_multiply_fusion.1
  57.1 14.8 %shard_map.47 = f32[8,64,256]{2,1,0:T(8,128)} custom-call(f32[16,64,256]{2,1,0:T(8,128)} %copy.13.x_ref, f32[72,64]{1,0:T(8,128)} %get-tuple-element.15.c1_ref, f32[72,64]{1,0:T(8,128)} %get-tuple-element.14.s1_ref, f32[72,256]{1,0:T(8,128)} %get-tuple-element.19.twc_ref, f32[72,256]{1,0:T(8,128)} %get-tuple-element.18.tws_ref, ...), custom_call_target="tpu_custom_call" | custom-call | tf_op jit(solution)/shard_map/pallas_call | solution.py:153
  71.8 0.8 dynamic_slice.7
  72.6 2.1 %fusion.2.refs_0_ = bf16[64,8,256]{2,1,0:T(8,128)(2,1)} fusion(f32[3,64,8,256]{3,2,1,0:T(8,128)S(1)} %bitcast.40, f32[8,64,256]{2,1,0:T(8,128)} %shard_map.47, f32[8]{0:T(128)S(1)} %dynamic_slice.7), kind=kLoop, calls=%fused_computation.8 | loop fusion | flops 655360 | bytes 2359328 | tf_op jit(solution)/shard_map/convert_element_type | solution.py:187
  74.7 19.8 %shard_map.48 = bf16[64,8,256]{2,1,0:T(8,128)(2,1)} custom-call(bf16[64,8,256]{2,1,0:T(8,128)(2,1)} %fusion.2.refs_0_), custom_call_target="tpu_custom_call" | custom-call | tf_op jit(solution)/shard_map/pallas_call | solution.py:80
  94.5 1.8 %copy.15 = bf16[512,256]{0,1:T(8,128)(2,1)} copy(bf16[512,256]{1,0:T(8,128)(2,1)} %bitcast.43) | data formatting | bytes 524288 | tf_op jit(solution)/shard_map/reshape | solution.py:189
  (2 shorter events, 0.0 us)
Async XLA Ops:
  0.8 2.4 %copy-start = (f32[256,512]{1,0:T(8,128)S(1)}, f32[256,512]{1,0:T(8,128)}, u32[]{:S(2)}) copy-start(f32[256,512]{1,0:T(8,128)} %param.7) | copy-start | bytes 1572868
  50.0 1.0 %copy-start.1 = (f32[64,8,256]{2,1,0:T(8,128)S(1)}, f32[64,8,256]{2,1,0:T(8,128)}, u32[]{:S(2)}) copy-start(f32[64,8,256]{2,1,0:T(8,128)} %get-tuple-element.8) | copy-start | bytes 1572868

commit v5 on v4

--- a/solution.py
+++ b/solution.py
@@ -2,6 +2,7 @@
 import math
 
 import jax
+import numpy as np
 import jax.numpy as jnp
 from jax import lax
 from jax.experimental import pallas as pl
@@ -12,11 +13,9 @@
 
 
 def phase_table(count_out, count_in, modulus, sign):
-    out_idx = jnp.arange(count_out, dtype=jnp.int32)[:, None]
-    in_idx = jnp.arange(count_in, dtype=jnp.int32)[None, :]
-    phase = out_idx * in_idx % modulus
-    angles = sign * 2.0 * math.pi / modulus * phase.astype(jnp.float32)
-    return jnp.cos(angles), jnp.sin(angles)
+    phase = np.arange(count_out)[:, None] * np.arange(count_in)[None, :] % modulus
+    angles = sign * 2.0 * np.pi / modulus * phase
+    return np.cos(angles), np.sin(angles)
 
 
 def exchange_kernel(shards, *refs):
@@ -91,7 +90,8 @@
 
 
 def conv_kernel(
-    x_ref, c1_ref, s1_ref, twc_ref, tws_ref, vc_ref, vs_ref, ci_ref, si_ref, o_ref, yre_ref, yim_ref
+    x_ref, c1_ref, s1_ref, twc_ref, tws_ref, vc_ref, vs_ref, vsum_ref, vdiff_ref, ci_ref, si_ref, o_ref,
+    yre_ref, yim_ref,
 ):
     streams = x_ref.shape[0]
     group = streams // 2
@@ -114,13 +114,19 @@
     vs = vs_ref[...]
     yre = yre_ref[...]
     yim = yim_ref[...]
-    zre = dot(yre, vc) - dot(yim, vs)
-    zim = dot(yim, vc) + dot(yre, vs)
+    vsum = vsum_ref[...]
+    ac = dot(yre, vc)
+    bd = dot(yim, vs)
+    zre = ac - bd
+    zim = dot(yre + yim, vsum) - ac - bd
     half = group * pad
     pre = zre[:half] * zre[half:] - zim[:half] * zim[half:]
     pim = zre[:half] * zim[half:] + zim[:half] * zre[half:]
-    qre = dot(pre, vc) + dot(pim, vs)
-    qim = dot(pim, vc) - dot(pre, vs)
+    vdiff = vdiff_ref[...]
+    ac = dot(pre, vc)
+    bd = dot(pim, vs)
+    qre = ac + bd
+    qim = dot(pre + pim, vdiff) - ac + bd
     ci = ci_ref[...]
     si = si_ref[...]
     for g in range(group):
@@ -138,28 +144,30 @@
     total = coarse * rows
     half = blocks + 1
     pad = -(-half // 8) * 8
-    live = (jnp.arange(pad) < half).astype(jnp.float32)
+    live = (np.arange(pad) < half).astype(np.float64)
     c1, s1 = phase_table(pad, blocks, coarse, -1.0)
     c1 = c1 * live[:, None]
     s1 = s1 * live[:, None]
     twc, tws = phase_table(pad, rows, total, -1.0)
     vc, vs = phase_table(rows, rows, rows, -1.0)
-    k1 = jnp.arange(pad)
-    weight = jnp.where((k1 == 0) | (k1 == blocks), 1.0, 2.0) * live / total
+    k1 = np.arange(pad)
+    weight = np.where((k1 == 0) | (k1 == blocks), 1.0, 2.0) * live / total
     ci, si = phase_table(blocks, pad, coarse, 1.0)
     ci = ci * weight[None, :]
     si = si * weight[None, :]
+    tables = [c1, s1, twc, tws, vc, vs, vc + vs, vc - vs, ci, si]
+    tables = [jnp.asarray(t, dtype=jnp.float32) for t in tables]
     vmem = pl.BlockSpec(memory_space=pltpu.VMEM)
     return pl.pallas_call(
         conv_kernel,
         out_shape=jax.ShapeDtypeStruct((group, blocks, rows), jnp.float32),
-        in_specs=[vmem] * 9,
+        in_specs=[vmem] * (1 + len(tables)),
         out_specs=vmem,
         scratch_shapes=[
             pltpu.VMEM((streams * pad, rows), jnp.float32),
             pltpu.VMEM((streams * pad, rows), jnp.float32),
         ],
-    )(pieces, c1, s1, twc, tws, vc, vs, ci, si)
+    )(pieces, *tables)
 
 
 def on_device(qkv, short_w, skip, filt):

time: 96.7 us -> 89.2 us (0.922)
  other arithmetic: 8.68 us -> 4.37 us
  Pallas kernels: 78.1 us -> 75 us
    pallas_call x1, Pallas kernels: 14.8 us -> 11.6 us  [long_conv(): pl.pallas_call(conv_kernel, out_shape=jax.ShapeDtypeStruct((group, blocks...]
    sin x2 -> x0, other arithmetic: 2.72 us -> none  [phase_table(): return (jnp.cos(angles), jnp.sin(angles))]
    mul x2 -> x0, other arithmetic: 1.59 us -> none  [the longest x1 0.82 us: long_conv(): s1 = s1 * live[:, None]]
where the time goes in v5:
time: 89.2 us; the launch traced here: 88.8 us
  Pallas kernels  75 us (84%)
  local copies, waits for them, and re-layouts  9.33 us (10%)
  other arithmetic  4.37 us (5%)
    pallas_call x2, Pallas kernels, exchange(): pl.pallas_call(functools.partial(exchange_kernel, shards), out_shape=[jax...  63.4 us
    pallas_call x1, Pallas kernels, long_conv(): pl.pallas_call(conv_kernel, out_shape=jax.ShapeDtypeStruct((group, blocks...  11.6 us
    unnamed x6, local copies, waits for them, and re-layouts  3.26 us
    convert_element_type x1, other arithmetic, on_device(): mixed = (query * (conv + gain * signal)).astype(jnp.bfloat16)  2.08 us
    reshape x1, local copies, waits for them, and re-layouts, on_device(): return back.reshape(width, rows).T  1.8 us

profile of v5, /device:TPU:1, one launch (start us, length us, event | category | flops | bytes accessed | tf_op | source)
XLA Modules:
  0.0 88.8 jit_solution(2926152122968825627)
XLA Ops:
  0.0 0.0 copy-start
  0.0 0.8 dynamic_slice.7
  0.8 0.8 dynamic-slice_bitcast_fusion.2
  1.6 2.0 %copy.21 = f32[256,512]{0,1:T(8,128)} copy(f32[256,512]{1,0:T(8,128)} %param.17) | data formatting | bytes 1048576 | tf_op args[3]
  3.6 0.0 copy-done
  3.6 0.3 copy.19
  3.9 0.9 %copy_bitcast_fusion.refs_0_ = bf16[64,3,8,256]{3,2,1,0:T(8,128)(2,1)} fusion(bf16[256,3,512]{0,2,1:T(8,128)(2,1)S(1)} %copy.19), kind=kLoop, calls=%fused_computation.3 | loop fusion | bytes 1572864 | tf_op jit(solution)/shard_map/transpose | solution.py:179
  4.9 43.6 %shard_map.136 = (bf16[64,3,8,256]{3,2,1,0:T(8,128)(2,1)}, f32[64,8,256]{2,1,0:T(8,128)}) custom-call(bf16[64,3,8,256]{3,2,1,0:T(8,128)(2,1)} %copy_bitcast_fusion.refs_0_, f32[64,8,256]{2,1,0:T(8,128)} %bitcast.42), custom_call_target="tpu_custom_call" | custom-call | tf_op jit(solution)/shard_map/pallas_call | solution.py:79
  48.4 1.2 %convert_bitcast_fusion = f32[64,3,1,8,256]{4,3,2,1,0:T(8,128)S(1)} fusion(bf16[64,3,8,256]{3,2,1,0:T(8,128)(2,1)} %get-tuple-element.7), kind=kLoop, calls=%fused_computation | loop fusion | flops 393216 | bytes 2359296
  49.7 0.1 copy.26
  49.8 0.9 %multiply_add_fusion = f32[3,8,16384]{2,1,0:T(8,128)S(1)} fusion(f32[3,8,16384]{2,1,0:T(8,128)S(1)} %bitcast.41, f32[3,8]{1,0:T(4,128)S(1)} %get-tuple-element.11, f32[3,8]{1,0:T(4,128)S(1)} %get-tuple-element.10, f32[3,8]{1,0:T(4,128)S(1)} %get-tuple-element.9), kind=kLoop, calls=%fused_computation.1 | loop fusion | flops 1966080 | bytes 3146016 | tf_op jit(solution)/shard_map/add | solution.py:188
  50.7 0.0 copy-start.1
  50.7 0.1 fusion
  50.8 1.0 %copy-done.1 = f32[64,8,256]{2,1,0:T(8,128)S(1)} copy-done((f32[64,8,256]{2,1,0:T(8,128)S(1)}, f32[64,8,256]{2,1,0:T(8,128)}, u32[]{:S(2)}) %copy-start.1) | copy-done | bytes 524312
  51.8 0.1 maximum_bitcast_fusion
  51.8 1.6 %copy.23.x_ref = f32[16,64,256]{2,1,0:T(8,128)} copy(f32[16,64,256]{2,0,1:T(8,128)S(1)} %maximum_bitcast_fusion) | data formatting | bytes 2097152 | tf_op jit(solution)/shard_map/transpose | solution.py:192
  53.4 11.6 %shard_map.137 = f32[8,64,256]{2,1,0:T(8,128)} custom-call(f32[16,64,256]{2,1,0:T(8,128)} %copy.23.x_ref, f32[72,64]{1,0:T(8,128)} %constant.34.clone.c1_ref, f32[72,64]{1,0:T(8,128)} %constant.35.clone.s1_ref, f32[72,256]{1,0:T(8,128)} %constant.36.clone.twc_ref, f32[72,256]{1,0:T(8,128)} %constant.37.clone.tws_ref, f32[256,256]{1,0:T(8,128)} %constant.38.clone.vc_ref, ...), custom_call_target="tpu_custom_call" | custom-call | tf_op jit(solution)/shard_map/pallas_call | solution.py:161
  65.1 2.1 %fusion.2.refs_0_ = bf16[64,8,256]{2,1,0:T(8,128)(2,1)} fusion(f32[3,64,8,256]{3,2,1,0:T(8,128)S(1)} %bitcast.40, f32[8,64,256]{2,1,0:T(8,128)} %shard_map.137, f32[8]{0:T(128)S(1)} %dynamic_slice.7), kind=kLoop, calls=%fused_computation.8 | loop fusion | flops 655360 | bytes 2359328 | tf_op jit(solution)/shard_map/convert_element_type | solution.py:195
  67.2 19.8 %shard_map.138 = bf16[64,8,256]{2,1,0:T(8,128)(2,1)} custom-call(bf16[64,8,256]{2,1,0:T(8,128)(2,1)} %fusion.2.refs_0_), custom_call_target="tpu_custom_call" | custom-call | tf_op jit(solution)/shard_map/pallas_call | solution.py:79
  87.0 1.8 %copy.25 = bf16[512,256]{0,1:T(8,128)(2,1)} copy(bf16[512,256]{1,0:T(8,128)(2,1)} %bitcast.43) | data formatting | bytes 524288 | tf_op jit(solution)/shard_map/reshape | solution.py:197
Async XLA Ops:
  0.0 3.6 %copy-start = (bf16[256,3,512]{2,0,1:T(8,128)(2,1)S(1)}, bf16[256,3,512]{2,0,1:T(8,128)(2,1)}, u32[]{:S(2)}) copy-start(bf16[256,3,512]{2,0,1:T(8,128)(2,1)} %param.14) | copy-start | bytes 2359300
  50.7 1.0 %copy-start.1 = (f32[64,8,256]{2,1,0:T(8,128)S(1)}, f32[64,8,256]{2,1,0:T(8,128)}, u32[]{:S(2)}) copy-start(f32[64,8,256]{2,1,0:T(8,128)} %get-tuple-element.8) | copy-start | bytes 1572868

commit v6 on v5

v6 whole, which is shorter than its diff:
```python
import functools
import math

import jax
import numpy as np
import jax.numpy as jnp
from jax import lax
from jax.experimental import pallas as pl
from jax.experimental.pallas import tpu as pltpu
from jax.sharding import PartitionSpec as P

PRECISION = lax.Precision.HIGHEST


def phase_table(count_out, count_in, modulus, sign):
    phase = np.arange(count_out)[:, None] * np.arange(count_in)[None, :] % modulus
    angles = sign * 2.0 * np.pi / modulus * phase
    return np.cos(angles), np.sin(angles)


def conv_body(
    x_ref, c1_ref, s1_ref, twc_ref, tws_ref, vc_ref, vs_ref, vsum_ref, vdiff_ref, ci_ref, si_ref, o_ref,
    yre_ref, yim_ref,
):
    streams = x_ref.shape[0]
    group = streams // 2
    pad = c1_ref.shape[0]

    def dot(a, b):
        return jnp.dot(a, b, precision=PRECISION, preferred_element_type=jnp.float32)

    twc = twc_ref[...]
    tws = tws_ref[...]
    c1 = c1_ref[...]
    s1 = s1_ref[...]
    for j in range(streams):
        xj = x_ref[j]
        a = dot(c1, xj)
        b = dot(s1, xj)
        yre_ref[j * pad : (j + 1) * pad, :] = a * twc - b * tws
        yim_ref[j * pad : (j + 1) * pad, :] = a * tws + b * twc
    vc = vc_ref[...]
    vs = vs_ref[...]
    yre = yre_ref[...]
    yim = yim_ref[...]
    vsum = vsum_ref[...]
    ac = dot(yre, vc)
    bd = dot(yim, vs)
    zre = ac - bd
    zim = dot(yre + yim, vsum) - ac - bd
    half = group * pad
    pre = zre[:half] * zre[half:] - zim[:half] * zim[half:]
    pim = zre[:half] * zim[half:] + zim[:half] * zre[half:]
    vdiff = vdiff_ref[...]
    ac = dot(pre, vc)
    bd = dot(pim, vs)
    qre = ac + bd
    qim = dot(pre + pim, vdiff) - ac + bd
    ci = ci_ref[...]
    si = si_ref[...]
    for g in range(group):
        ure = qre[g * pad : (g + 1) * pad]
        uim = qim[g * pad : (g + 1) * pad]
        vre = ure * twc + uim * tws
        vim = uim * twc - ure * tws
        o_ref[g] = dot(ci, vre) - dot(si, vim)


def fused_kernel(shards, src_ref, *refs):
    tables = refs[:10]
    out_ref, recv_ref, stage_ref = refs[10:13]
    x_ref, o_ref, yre_ref, yim_ref, send_a, recv_a, send_b, recv_b, local = refs[13:]
    me = lax.axis_index("seq")
    row = lax.axis_index("ch")
    mesh_id = pl.DeviceIdType.MESH
    streams = x_ref.shape[0]
    barrier = pltpu.get_barrier_semaphore()

    def peer_of(step):
        return lax.rem(me + 1 + step, shards)

    def greet(step, carry):
        pl.semaphore_signal(barrier, inc=1, device_id=(peer_of(step), row), device_id_type=mesh_id)
        return carry

    lax.fori_loop(0, shards - 1, greet, 0)
    pl.semaphore_wait(barrier, shards - 1)

    def scatter(source, target, send_sem, recv_sem, own_sem):
        own = pltpu.make_async_copy(source(me), target.at[me], own_sem)
        own.start()

        def copy_to(peer, slot):
            return pltpu.make_async_remote_copy(
                src_ref=source(peer),
                dst_ref=target.at[slot],
                send_sem=send_sem.at[peer],
                recv_sem=recv_sem.at[slot],
                device_id=(peer, row),
                device_id_type=mesh_id,
            )

        def send(step, carry):
            copy_to(peer_of(step), me).start()
            return carry

        def finish(step, carry):
            peer = peer_of(step)
            copy_to(peer, me).wait_send()
            copy_to(peer, peer).wait_recv()
            return carry

        lax.fori_loop(0, shards - 1, send, 0)
        lax.fori_loop(0, shards - 1, finish, 0)
        own.wait()

    scatter(lambda j: src_ref.at[j], recv_ref, send_a, recv_a, local.at[0])
    gathers = [
        pltpu.make_async_copy(recv_ref.at[:, j, :], x_ref.at[j], local.at[2 + j])
        for j in range(streams)
    ]
    for copy in gathers:
        copy.start()
    for copy in gathers:
        copy.wait()
    conv_body(x_ref, *tables, o_ref, yre_ref, yim_ref)
    put = pltpu.make_async_copy(o_ref, stage_ref, local.at[1])
    put.start()
    put.wait()
    scatter(lambda j: stage_ref.at[:, j, :], out_ref, send_b, recv_b, local.at[0])


def long_conv(pieces):
    blocks, streams, rows = pieces.shape
    group = streams // 2
    coarse = 2 * blocks
    total = coarse * rows
    half = blocks + 1
    pad = -(-half // 8) * 8
    live = (np.arange(pad) < half).astype(np.float64)
    c1, s1 = phase_table(pad, blocks, coarse, -1.0)
    c1 = c1 * live[:, None]
    s1 = s1 * live[:, None]
    twc, tws = phase_table(pad, rows, total, -1.0)
    vc, vs = phase_table(rows, rows, rows, -1.0)
    k1 = np.arange(pad)
    weight = np.where((k1 == 0) | (k1 == blocks), 1.0, 2.0) * live / total
    ci, si = phase_table(blocks, pad, coarse, 1.0)
    ci = ci * weight[None, :]
    si = si * weight[None, :]
    tables = [c1, s1, twc, tws, vc, vs, vc + vs, vc - vs, ci, si]
    tables = [jnp.asarray(t, dtype=jnp.float32) for t in tables]
    vmem = pl.BlockSpec(memory_space=pltpu.VMEM)
    anywhere = pl.BlockSpec(memory_space=pl.ANY)
    f32 = jnp.float32
    return pl.pallas_call(
        functools.partial(fused_kernel, blocks),
        out_shape=[
            jax.ShapeDtypeStruct((blocks, group, rows), f32),
            jax.ShapeDtypeStruct((blocks, streams, rows), f32),
            jax.ShapeDtypeStruct((group, blocks, rows), f32),
        ],
        in_specs=[anywhere] + [vmem] * len(tables),
        out_specs=[anywhere] * 3,
        scratch_shapes=[
            pltpu.VMEM((streams, blocks, rows), f32),
            pltpu.VMEM((group, blocks, rows), f32),
            pltpu.VMEM((streams * pad, rows), f32),
            pltpu.VMEM((streams * pad, rows), f32),
            pltpu.SemaphoreType.DMA((blocks,)),
            pltpu.SemaphoreType.DMA((blocks,)),
            pltpu.SemaphoreType.DMA((blocks,)),
            pltpu.SemaphoreType.DMA((blocks,)),
            pltpu.SemaphoreType.DMA((2 + streams,)),
        ],
        compiler_params=pltpu.CompilerParams(collective_id=0, has_side_effects=True),
    )(pieces, *tables)[0]


def shifted(block, axis, distance):
    devices = range(lax.axis_size(axis))
    route = [(i - distance, i) for i in devices if i - distance in devices]
    return lax.ppermute(block, axis, route)


def on_device(qkv, short_w, skip, filt):
    rows, _, width = qkv.shape
    taps = short_w.shape[0]
    shards = lax.axis_size("seq")
    group = width // shards
    rim = shifted(qkv[rows - (taps - 1) :], "seq", 1)
    extended = jnp.concatenate([rim, qkv], axis=0).astype(jnp.float32)
    feat = short_w[0] * extended[taps - 1 : taps - 1 + rows]
    for tap in range(1, taps):
        feat = feat + short_w[tap] * extended[taps - 1 - tap : taps - 1 - tap + rows]
    query = feat[:, 0, :]
    signal = feat[:, 1, :] * feat[:, 2, :]
    source = jnp.stack([signal, filt]).reshape(2, rows, shards, group).transpose(2, 0, 3, 1)
    values = long_conv(source.reshape(shards, 2 * group, rows))
    conv = values.reshape(width, rows).T
    return (query * (conv + skip * signal)).astype(jnp.bfloat16)


def solution(mesh):
    return jax.shard_map(
        on_device,
        mesh=mesh,
        in_specs=(P("seq", None, "ch"), P(None, None, "ch"), P("ch"), P("seq", "ch")),
        out_specs=P("seq", "ch"),
        check_vma=False,
    )
```

time: 89.2 us -> 83.7 us (0.938)
  Pallas kernels: 75 us -> 67 us
  local copies, waits for them, and re-layouts: 9.33 us -> 4.26 us
  starting transfers between devices: 0 us -> 4.51 us
  waiting for transfers between devices: 0 us -> 2.49 us
    pallas_call x3 -> x1, Pallas kernels: 75 us -> 67 us  [long_conv(): pl.pallas_call(functools.partial(fused_kernel, blocks), out_shape=[jax.Sh...]
    ppermute x0 -> x1, starting transfers between devices: none -> 4.51 us  [shifted(): return lax.ppermute(block, axis, route)]
    transpose x2 -> x0, local copies, waits for them, and re-layouts: 2.52 us -> none  [the longest x1 1.58 us: on_device(): pieces = jnp.concatenate([signal, filt_in], axis=1).transpose(1, 0, 2)]
    ppermute x0 -> x1, waiting for transfers between devices: none -> 2.49 us  [shifted(): return lax.ppermute(block, axis, route)]
    reshape x2 -> x0, local copies, waits for them, and re-layouts: 1.93 us -> none  [the longest x1 1.8 us: on_device(): return back.reshape(width, rows).T]
    unnamed x6, local copies, waits for them, and re-layouts: 3.26 us -> 1.61 us
    unnamed x1 -> x0, other arithmetic: 1.25 us -> none
    slice x0 -> x2, local copies, waits for them, and re-layouts: none -> 1.07 us  [on_device(): rim = shifted(qkv[rows - (taps - 1):], 'seq', 1)]
  transfers between devices with their start and end apart: 0 -> 1, of which waited for: 0 -> 1; matrix products, arithmetic and copies ran while one was open for 0% -> 3% of each run, Pallas kernels for 0% -> 0%
where the time goes in v6:
time: 83.7 us; the launch traced here: 82.7 us
  Pallas kernels  67 us (80%)
  starting transfers between devices  4.51 us (5%)
  other arithmetic  4.44 us (5%)
  local copies, waits for them, and re-layouts  4.26 us (5%)
  waiting for transfers between devices  2.49 us (3%)
    pallas_call x1, Pallas kernels, long_conv(): pl.pallas_call(functools.partial(fused_kernel, blocks), out_shape=[jax.Sh...  67 us
    ppermute x1, starting transfers between devices, shifted(): return lax.ppermute(block, axis, route)  4.51 us
    ppermute x1, waiting for transfers between devices, shifted(): return lax.ppermute(block, axis, route)  2.49 us
  transfers between devices with their start and end apart: 1, of which 1 were waited for; matrix products, arithmetic and copies ran while one was open for 3% of the time, Pallas kernels for 0%

profile of v6, /device:TPU:1, one launch (start us, length us, event | category | flops | bytes accessed | tf_op | source)
XLA Modules:
  0.0 82.7 jit_solution(4962971555574088113)
XLA Ops:
  0.0 0.0 copy-start
  0.0 0.8 slice.31
  0.8 0.3 copy.18
  1.1 4.5 %collective-permute-start = (bf16[2,3,512]{0,2,1:T(8,128)(2,1)S(1)}, bf16[2,3,512]{0,2,1:T(8,128)(2,1)S(1)}, u32[]{:S(2)}, u32[]{:S(2)}) collective-permute-start(bf16[2,3,512]{0,2,1:T(8,128)(2,1)S(1)} %copy.18), channel_id=1, source_target_pairs={{0,8},{8,16},{16,24},{24,32},{32,40},{40,48},{48,56},{56,64},{64,7... | collective-permute-start | bytes 18440 | tf_op jit(solution)/shard_map/ppermute | solution.py:183
  5.6 0.7 slice_bitcast_fusion.3
  6.3 1.4 %copy.19 = bf16[256,3,512]{0,2,1:T(8,128)(2,1)S(1)} copy(bf16[256,3,512]{2,0,1:T(8,128)(2,1)} %param.14) | data formatting | bytes 1572864 | tf_op args[0]
  7.7 0.0 copy-done
  7.8 0.2 copy.20
  8.0 2.5 %collective-permute-done = bf16[2,3,512]{0,2,1:T(8,128)(2,1)S(1)} collective-permute-done((bf16[2,3,512]{0,2,1:T(8,128)(2,1)S(1)}, bf16[2,3,512]{0,2,1:T(8,128)(2,1)S(1)}, u32[]{:S(2)}, u32[]{:S(2)}) %collective-permute-start) | collective-permute-done | bytes 6176 | tf_op jit(solution)/shard_map/ppermute | solution.py:183
  10.5 0.5 maximum_convert_fusion
  11.0 1.6 %fusion = f32[256,3,512]{0,2,1:T(8,128)S(1)} fusion(f32[258,3,512]{0,2,1:T(8,128)S(1)} %maximum_convert_fusion, f32[3,512]{1,0:T(4,128)S(1)} %get-tuple-element.8, f32[3,512]{1,0:T(4,128)S(1)} %get-tuple-element.9, f32[3,512]{1,0:T(4,128)S(1)} %get-tuple-element.7), kind=kLoop, calls=%fused_computation.1 | loop fusion | flops 1966080 | bytes 6309888 | tf_op jit(solution)/shard_map/add | solution.py:195
  12.6 0.1 fusion.4
  12.7 1.1 %copy_bitcast_fusion.src_ref = f32[64,16,256]{2,1,0:T(8,128)} fusion(f32[1,256,64,8]{1,3,2,0:T(8,128)S(1)} %bitcast.30, f32[1,256,64,8]{1,3,2,0:T(8,128)S(1)} %fusion.4), kind=kLoop, calls=%fused_computation.7 | loop fusion | flops 262144 | bytes 2097152 | tf_op jit(solution)/shard_map/reshape | solution.py:199
  13.7 0.0 copy-start.1
  13.7 67.0 %shard_map.136 = (f32[64,8,256]{2,1,0:T(8,128)}, f32[64,16,256]{2,1,0:T(8,128)}, f32[8,64,256]{2,1,0:T(8,128)}) custom-call(f32[64,16,256]{2,1,0:T(8,128)} %copy_bitcast_fusion.src_ref, f32[72,64]{1,0:T(8,128)} %constant.20.clone.refs_0_, f32[72,64]{1,0:T(8,128)} %constant.21.clone.refs_1_, f32[72,256]{1,0:T(8,128)} %constant.22.clone.refs_2_, ...), custom_call_target="tpu_custom_call" | custom-call | tf_op jit(solution)/shard_map/pallas_call | solution.py:156
  80.7 0.0 copy-done.1
  80.7 1.2 %fusion.3 = bf16[256,512]{0,1:T(8,128)(2,1)S(1)} fusion(f32[256,3,512]{0,2,1:T(8,128)S(1)} %fusion, f32[64,8,256]{2,1,0:T(8,128)} %get-tuple-element.6, f32[512]{0:T(512)S(1)} %copy-done.1), kind=kLoop, calls=%fused_computation.11 | loop fusion | flops 655360 | bytes 2361344 | tf_op jit(solution)/shard_map/convert_element_type | solution.py:201
  81.9 0.8 %copy.22 = bf16[256,512]{1,0:T(8,128)(2,1)} copy(bf16[256,512]{0,1:T(8,128)(2,1)S(1)} %fusion.3) | data formatting | bytes 524288 | tf_op jit(solution)/shard_map/convert_element_type | solution.py:201
Async XLA Ops:
  0.0 7.7 %copy-start = (f32[256,512]{1,0:T(8,128)S(1)}, f32[256,512]{1,0:T(8,128)}, u32[]{:S(2)}) copy-start(f32[256,512]{1,0:T(8,128)} %param.17) | copy-start | bytes 1572868
  1.1 9.4 %collective-permute-start = (bf16[2,3,512]{0,2,1:T(8,128)(2,1)S(1)}, bf16[2,3,512]{0,2,1:T(8,128)(2,1)S(1)}, u32[]{:S(2)}, u32[]{:S(2)}) collective-permute-start(bf16[2,3,512]{0,2,1:T(8,128)(2,1)S(1)} %copy.18), channel_id=1, source_target_pairs={{0,8},{8,16},{16,24},{24,32},{32,40},{40,48},{48,56},{56,64},{64,7... | collective-permute-start | bytes 18440 | tf_op jit(solution)/shard_map/ppermute | solution.py:183
  13.7 67.0 %copy-start.1 = (f32[512]{0:T(512)S(1)}, f32[512]{0:T(512)}, u32[]{:S(2)}) copy-start(f32[512]{0:T(512)} %param.16) | copy-start | bytes 6148

commit v7 on v6

--- a/solution.py
+++ b/solution.py
@@ -66,10 +66,10 @@
         o_ref[g] = dot(ci, vre) - dot(si, vim)
 
 
-def fused_kernel(shards, src_ref, *refs):
+def fused_kernel(shards, parts, src_ref, *refs):
     tables = refs[:10]
     out_ref, recv_ref, stage_ref = refs[10:13]
-    x_ref, o_ref, yre_ref, yim_ref, send_a, recv_a, send_b, recv_b, local = refs[13:]
+    x_ref, o_ref, yre_ref, yim_ref, sends, recvs, local = refs[13:]
     me = lax.axis_index("seq")
     row = lax.axis_index("ch")
     mesh_id = pl.DeviceIdType.MESH
@@ -86,16 +86,16 @@
     lax.fori_loop(0, shards - 1, greet, 0)
     pl.semaphore_wait(barrier, shards - 1)
 
-    def scatter(source, target, send_sem, recv_sem, own_sem):
-        own = pltpu.make_async_copy(source(me), target.at[me], own_sem)
+    def scatter(source, target, phase):
+        own = pltpu.make_async_copy(source(me), target(me), local.at[phase])
         own.start()
 
         def copy_to(peer, slot):
             return pltpu.make_async_remote_copy(
                 src_ref=source(peer),
-                dst_ref=target.at[slot],
-                send_sem=send_sem.at[peer],
-                recv_sem=recv_sem.at[slot],
+                dst_ref=target(slot),
+                send_sem=sends.at[phase, peer],
+                recv_sem=recvs.at[phase, slot],
                 device_id=(peer, row),
                 device_id_type=mesh_id,
             )
@@ -104,34 +104,52 @@
             copy_to(peer_of(step), me).start()
             return carry
 
-        def finish(step, carry):
-            peer = peer_of(step)
-            copy_to(peer, me).wait_send()
-            copy_to(peer, peer).wait_recv()
-            return carry
-
         lax.fori_loop(0, shards - 1, send, 0)
-        lax.fori_loop(0, shards - 1, finish, 0)
-        own.wait()
-
-    scatter(lambda j: src_ref.at[j], recv_ref, send_a, recv_a, local.at[0])
-    gathers = [
-        pltpu.make_async_copy(recv_ref.at[:, j, :], x_ref.at[j], local.at[2 + j])
-        for j in range(streams)
+
+        def finish():
+            def wait_one(step, carry):
+                peer = peer_of(step)
+                copy_to(peer, me).wait_send()
+                copy_to(peer, peer).wait_recv()
+                return carry
+
+            lax.fori_loop(0, shards - 1, wait_one, 0)
+            own.wait()
+
+        return finish
+
+    arrivals = [
+        scatter(lambda j, h=h: src_ref.at[j, h], lambda j, h=h: recv_ref.at[j, h], h)
+        for h in range(parts)
     ]
-    for copy in gathers:
-        copy.start()
-    for copy in gathers:
-        copy.wait()
-    conv_body(x_ref, *tables, o_ref, yre_ref, yim_ref)
-    put = pltpu.make_async_copy(o_ref, stage_ref, local.at[1])
-    put.start()
-    put.wait()
-    scatter(lambda j: stage_ref.at[:, j, :], out_ref, send_b, recv_b, local.at[0])
+    returns = []
+    for h in range(parts):
+        arrivals[h]()
+        gathers = [
+            pltpu.make_async_copy(recv_ref.at[:, h, j, :], x_ref.at[j], local.at[2 * parts + j])
+            for j in range(streams)
+        ]
+        for copy in gathers:
+            copy.start()
+        for copy in gathers:
+            copy.wait()
+        conv_body(x_ref, *tables, o_ref, yre_ref, yim_ref)
+        put = pltpu.make_async_copy(o_ref, stage_ref.at[h], local.at[2 * parts + streams])
+        put.start()
+        put.wait()
+        returns.append(
+            scatter(
+                lambda j, h=h: stage_ref.at[h, :, j, :],
+                lambda j, h=h: out_ref.at[j, h],
+                parts + h,
+            )
+        )
+    for finish in returns:
+        finish()
 
 
 def long_conv(pieces):
-    blocks, streams, rows = pieces.shape
+    blocks, parts, streams, rows = pieces.shape
     group = streams // 2
     coarse = 2 * blocks
     total = coarse * rows
@@ -154,11 +172,11 @@
     anywhere = pl.BlockSpec(memory_space=pl.ANY)
     f32 = jnp.float32
     return pl.pallas_call(
-        functools.partial(fused_kernel, blocks),
+        functools.partial(fused_kernel, blocks, parts),
         out_shape=[
-            jax.ShapeDtypeStruct((blocks, group, rows), f32),
-            jax.ShapeDtypeStruct((blocks, streams, rows), f32),
-            jax.ShapeDtypeStruct((group, blocks, rows), f32),
+            jax.ShapeDtypeStruct((blocks, parts, group, rows), f32),
+            jax.ShapeDtypeStruct((blocks, parts, streams, rows), f32),
+            jax.ShapeDtypeStruct((parts, group, blocks, rows), f32),
         ],
         in_specs=[anywhere] + [vmem] * len(tables),
         out_specs=[anywhere] * 3,
@@ -167,11 +185,9 @@
             pltpu.VMEM((group, blocks, rows), f32),
             pltpu.VMEM((streams * pad, rows), f32),
             pltpu.VMEM((streams * pad, rows), f32),
-            pltpu.SemaphoreType.DMA((blocks,)),
-            pltpu.SemaphoreType.DMA((blocks,)),
-            pltpu.SemaphoreType.DMA((blocks,)),
-            pltpu.SemaphoreType.DMA((blocks,)),
-            pltpu.SemaphoreType.DMA((2 + streams,)),
+            pltpu.SemaphoreType.DMA((2 * parts, blocks)),
+            pltpu.SemaphoreType.DMA((2 * parts, blocks)),
+            pltpu.SemaphoreType.DMA((2 * parts + streams + 1,)),
         ],
         compiler_params=pltpu.CompilerParams(collective_id=0, has_side_effects=True),
     )(pieces, *tables)[0]
@@ -195,8 +211,10 @@
         feat = feat + short_w[tap] * extended[taps - 1 - tap : taps - 1 - tap + rows]
     query = feat[:, 0, :]
     signal = feat[:, 1, :] * feat[:, 2, :]
-    source = jnp.stack([signal, filt]).reshape(2, rows, shards, group).transpose(2, 0, 3, 1)
-    values = long_conv(source.reshape(shards, 2 * group, rows))
+    parts = 2
+    source = jnp.stack([signal, filt]).reshape(2, rows, shards, parts, group // parts)
+    source = source.transpose(2, 3, 0, 4, 1).reshape(shards, parts, 2 * group // parts, rows)
+    values = long_conv(source)
     conv = values.reshape(width, rows).T
     return (query * (conv + skip * signal)).astype(jnp.bfloat16)
 

time: 83.7 us -> 74.8 us (0.89)
  Pallas kernels: 67 us -> 58.6 us
  local copies, waits for them, and re-layouts: 4.26 us -> 6.76 us
  other arithmetic: 4.44 us -> 2.66 us
    pallas_call x1, Pallas kernels: 67 us -> 58.6 us  [long_conv(): pl.pallas_call(functools.partial(fused_kernel, blocks, parts), out_shape=...]
    reshape x0 -> x3, local copies, waits for them, and re-layouts: none -> 2.75 us  [the longest x2 1.42 us: on_device(): conv = values.reshape(width, rows).T]
    add x1, other arithmetic: 1.62 us -> 0.47 us  [on_device(): feat = feat + short_w[tap] * extended[taps - 1 - tap:taps - 1 - tap + rows]]
    reshape x1 -> x0, other arithmetic: 1.05 us -> none  [on_device(): values = long_conv(source.reshape(shards, 2 * group, rows))]
    transpose x0 -> x1, other arithmetic: none -> 0.95 us  [on_device(): source.transpose(2, 3, 0, 4, 1)]
    convert_element_type x1 -> x0, local copies, waits for them, and re-layouts: 0.84 us -> none  [on_device(): return (query * (conv + skip * signal)).astype(jnp.bfloat16)]
where the time goes in v7:
time: 74.8 us; the launch traced here: 74.4 us
  Pallas kernels  58.6 us (78%)
  local copies, waits for them, and re-layouts  6.76 us (9%)
  starting transfers between devices  4.51 us (6%)
  other arithmetic  2.66 us (4%)
  waiting for transfers between devices  1.78 us (2%)
    pallas_call x1, Pallas kernels, long_conv(): pl.pallas_call(functools.partial(fused_kernel, blocks, parts), out_shape=...  58.6 us
    ppermute x1, starting transfers between devices, shifted(): return lax.ppermute(block, axis, route)  4.51 us
    ppermute x1, waiting for transfers between devices, shifted(): return lax.ppermute(block, axis, route)  1.78 us
  transfers between devices with their start and end apart: 1, of which 1 were waited for; matrix products, arithmetic and copies ran while one was open for 3% of the time, Pallas kernels for 0%

profile of v7, /device:TPU:1, one launch (start us, length us, event | category | flops | bytes accessed | tf_op | source)
XLA Modules:
  0.0 74.4 jit_solution(1681925477404630844)
XLA Ops:
  0.0 0.0 copy-start
  0.0 0.8 %slice.31 = bf16[2,3,512]{2,0,1:T(2,128)(2,1)S(1)} slice(bf16[256,3,512]{2,0,1:T(8,128)(2,1)} %param.14), slice={[254:256], [0:3], [0:512]} | slice | bytes 12288 | tf_op jit(solution)/shard_map/slice | solution.py:207
  0.8 4.5 %collective-permute-start = (bf16[2,3,512]{2,0,1:T(2,128)(2,1)S(1)}, bf16[2,3,512]{2,0,1:T(2,128)(2,1)S(1)}, u32[]{:S(2)}, u32[]{:S(2)}) collective-permute-start(bf16[2,3,512]{2,0,1:T(2,128)(2,1)S(1)} %slice.31), channel_id=1, source_target_pairs={{0,8},{8,16},{16,24},{24,32},{32,40},{40,48},{48,56},{56,64},{64,7... | collective-permute-start | bytes 18440 | tf_op jit(solution)/shard_map/ppermute | solution.py:199
  5.3 0.7 slice_bitcast_fusion.3
  6.1 1.2 %copy.19 = f32[256,512]{0,1:T(8,128)S(1)} copy(f32[256,512]{1,0:T(8,128)} %param.17) | data formatting | bytes 1048576 | tf_op args[3]
  7.3 0.5 stack.9
  7.9 1.8 %collective-permute-done = bf16[2,3,512]{2,0,1:T(2,128)(2,1)S(1)} collective-permute-done((bf16[2,3,512]{2,0,1:T(2,128)(2,1)S(1)}, bf16[2,3,512]{2,0,1:T(2,128)(2,1)S(1)}, u32[]{:S(2)}, u32[]{:S(2)}) %collective-permute-start) | collective-permute-done | bytes 6176 | tf_op jit(solution)/shard_map/ppermute | solution.py:199
  9.6 0.0 copy-done
  9.6 0.2 maximum_convert_fusion
  9.9 0.5 fusion
  10.4 0.1 slice_multiply_fusion.3
  10.4 0.4 copy.18
  10.9 0.9 %maximum_bitcast_fusion = f32[64,2,2,4,256]{4,2,3,1,0:T(2,128)S(1)} fusion(f32[1,256,64,2,4]{1,0,4,3,2:T(1,128)S(1)} %stack.9, f32[1,256,64,2,4]{1,0,4,3,2:T(1,128)S(1)} %bitcast.25), kind=kLoop, calls=%fused_computation.5 | loop fusion | flops 262144 | bytes 2097152 | tf_op jit(solution)/shard_map/transpose | solution.py:216
  11.8 0.3 copy.21
  12.1 1.3 %reshape.32.src_ref = f32[64,2,8,256]{3,2,1,0:T(8,128)} reshape(f32[64,2,2,4,256]{4,3,2,1,0:T(4,128)S(1)} %copy.21) | data formatting | bytes 2097152 | tf_op jit(solution)/shard_map/reshape | solution.py:216
  13.4 58.6 %shard_map.136 = (f32[64,2,4,256]{3,2,1,0:T(4,128)}, f32[64,2,8,256]{3,2,1,0:T(8,128)}, f32[2,4,64,256]{3,2,1,0:T(8,128)}) custom-call(f32[64,2,8,256]{3,2,1,0:T(8,128)} %reshape.32.src_ref, f32[72,64]{1,0:T(8,128)} %constant.20.clone.refs_0_, f32[72,64]{1,0:T(8,128)} %constant.21.clone.refs_1_, f32[72,256]{1,0:T(8,128)} %constant.22.clone.refs_2_, ...), custom_call_target="tpu_custom_call" | custom-call | tf_op jit(solution)/shard_map/pallas_call | solution.py:174
  72.0 0.0 copy-start.1
  72.0 1.2 %reshape.33 = f32[512,256]{1,0:T(8,128)S(1)} reshape(f32[64,2,4,256]{3,2,1,0:T(4,128)} %get-tuple-element.6) | data formatting | bytes 1048576 | tf_op jit(solution)/shard_map/reshape | solution.py:218
  73.2 0.2 copy.22
  73.5 0.0 copy-done.1
  73.5 0.9 %fusion.3 = bf16[256,512]{1,0:T(8,128)(2,1)} fusion(f32[256,3,512]{2,0,1:T(8,128)S(1)} %fusion, f32[512,256]{0,1:T(8,128)S(1)} %copy.22, f32[512]{0:T(512)S(1)} %copy-done.1), kind=kLoop, calls=%fused_computation.10 | loop fusion | flops 655360 | bytes 2361344 | tf_op jit(solution)/shard_map/convert_element_type | solution.py:219
Async XLA Ops:
  0.0 9.6 %copy-start = (bf16[256,3,512]{2,0,1:T(8,128)(2,1)S(1)}, bf16[256,3,512]{2,0,1:T(8,128)(2,1)}, u32[]{:S(2)}) copy-start(bf16[256,3,512]{2,0,1:T(8,128)(2,1)} %param.14) | copy-start | bytes 2359300
  0.8 8.8 %collective-permute-start = (bf16[2,3,512]{2,0,1:T(2,128)(2,1)S(1)}, bf16[2,3,512]{2,0,1:T(2,128)(2,1)S(1)}, u32[]{:S(2)}, u32[]{:S(2)}) collective-permute-start(bf16[2,3,512]{2,0,1:T(2,128)(2,1)S(1)} %slice.31), channel_id=1, source_target_pairs={{0,8},{8,16},{16,24},{24,32},{32,40},{40,48},{48,56},{56,64},{64,7... | collective-permute-start | bytes 18440 | tf_op jit(solution)/shard_map/ppermute | solution.py:199
  72.0 1.4 %copy-start.1 = (f32[512]{0:T(512)S(1)}, f32[512]{0:T(512)}, u32[]{:S(2)}) copy-start(f32[512]{0:T(512)} %param.16) | copy-start | bytes 6148

commit v8 on v7

--- a/solution.py
+++ b/solution.py
@@ -211,7 +211,7 @@
         feat = feat + short_w[tap] * extended[taps - 1 - tap : taps - 1 - tap + rows]
     query = feat[:, 0, :]
     signal = feat[:, 1, :] * feat[:, 2, :]
-    parts = 2
+    parts = 4
     source = jnp.stack([signal, filt]).reshape(2, rows, shards, parts, group // parts)
     source = source.transpose(2, 3, 0, 4, 1).reshape(shards, parts, 2 * group // parts, rows)
     values = long_conv(source)

time: 74.8 us -> 77.6 us (1.037)
  Pallas kernels: 58.6 us -> 60.3 us
  local copies, waits for them, and re-layouts: 6.76 us -> 7.74 us
    pallas_call x1, Pallas kernels: 58.6 us -> 60.3 us  [long_conv(): pl.pallas_call(functools.partial(fused_kernel, blocks, parts), out_shape=...]
where the time goes in v8:
time: 77.6 us; the launch traced here: 77.1 us
  Pallas kernels  60.3 us (78%)
  local copies, waits for them, and re-layouts  7.74 us (10%)
  starting transfers between devices  4.51 us (6%)
  other arithmetic  2.66 us (3%)
  waiting for transfers between devices  1.78 us (2%)
    pallas_call x1, Pallas kernels, long_conv(): pl.pallas_call(functools.partial(fused_kernel, blocks, parts), out_shape=...  60.3 us
    ppermute x1, starting transfers between devices, shifted(): return lax.ppermute(block, axis, route)  4.51 us
    reshape x1, local copies, waits for them, and re-layouts, on_device(): source.transpose(2, 3, 0, 4, 1)  1.86 us
    ppermute x1, waiting for transfers between devices, shifted(): return lax.ppermute(block, axis, route)  1.78 us
    reshape x2, local copies, waits for them, and re-layouts, on_device(): conv = values.reshape(width, rows).T  1.6 us
  transfers between devices with their start and end apart: 1, of which 1 were waited for; matrix products, arithmetic and copies ran while one was open for 3% of the time, Pallas kernels for 0%

profile of v8, /device:TPU:1, one launch (start us, length us, event | category | flops | bytes accessed | tf_op | source)
XLA Modules:
  0.0 77.1 jit_solution(4761691616008238609)
XLA Ops:
  0.0 0.0 copy-start
  0.0 0.8 %slice.31 = bf16[2,3,512]{2,0,1:T(2,128)(2,1)S(1)} slice(bf16[256,3,512]{2,0,1:T(8,128)(2,1)} %param.14), slice={[254:256], [0:3], [0:512]} | slice | bytes 12288 | tf_op jit(solution)/shard_map/slice | solution.py:207
  0.8 4.5 %collective-permute-start = (bf16[2,3,512]{2,0,1:T(2,128)(2,1)S(1)}, bf16[2,3,512]{2,0,1:T(2,128)(2,1)S(1)}, u32[]{:S(2)}, u32[]{:S(2)}) collective-permute-start(bf16[2,3,512]{2,0,1:T(2,128)(2,1)S(1)} %slice.31), channel_id=1, source_target_pairs={{0,8},{8,16},{16,24},{24,32},{32,40},{40,48},{48,56},{56,64},{64,7... | collective-permute-start | bytes 18440 | tf_op jit(solution)/shard_map/ppermute | solution.py:199
  5.3 0.7 slice_bitcast_fusion.3
  6.1 1.2 %copy.19 = f32[256,512]{0,1:T(8,128)S(1)} copy(f32[256,512]{1,0:T(8,128)} %param.17) | data formatting | bytes 1048576 | tf_op args[3]
  7.3 0.5 stack.9
  7.9 1.8 %collective-permute-done = bf16[2,3,512]{2,0,1:T(2,128)(2,1)S(1)} collective-permute-done((bf16[2,3,512]{2,0,1:T(2,128)(2,1)S(1)}, bf16[2,3,512]{2,0,1:T(2,128)(2,1)S(1)}, u32[]{:S(2)}, u32[]{:S(2)}) %collective-permute-start) | collective-permute-done | bytes 6176 | tf_op jit(solution)/shard_map/ppermute | solution.py:199
  9.6 0.0 copy-done
  9.6 0.2 maximum_convert_fusion
  9.9 0.5 fusion
  10.4 0.1 slice_multiply_fusion.3
  10.4 0.4 copy.18
  10.9 0.9 %maximum_bitcast_fusion = f32[64,4,2,2,256]{4,2,3,1,0:T(2,128)S(1)} fusion(f32[1,256,64,4,2]{1,0,4,3,2:T(1,128)S(1)} %stack.9, f32[1,256,64,4,2]{1,0,4,3,2:T(1,128)S(1)} %bitcast.25), kind=kLoop, calls=%fused_computation.5 | loop fusion | flops 262144 | bytes 2097152 | tf_op jit(solution)/shard_map/transpose | solution.py:216
  11.8 0.5 copy.21
  12.4 1.9 %reshape.32.src_ref = f32[64,4,4,256]{3,2,1,0:T(4,128)} reshape(f32[64,4,2,2,256]{4,3,2,1,0:T(2,128)S(1)} %copy.21) | data formatting | bytes 2097152 | tf_op jit(solution)/shard_map/reshape | solution.py:216
  14.2 60.3 %shard_map.136 = (f32[64,4,2,256]{3,2,1,0:T(2,128)}, f32[64,4,4,256]{3,2,1,0:T(4,128)}, f32[4,2,64,256]{3,2,1,0:T(8,128)}) custom-call(f32[64,4,4,256]{3,2,1,0:T(4,128)} %reshape.32.src_ref, f32[72,64]{1,0:T(8,128)} %constant.20.clone.refs_0_, f32[72,64]{1,0:T(8,128)} %constant.21.clone.refs_1_, f32[72,256]{1,0:T(8,128)} %constant.22.clone.refs_2_, ...), custom_call_target="tpu_custom_call" | custom-call | tf_op jit(solution)/shard_map/pallas_call | solution.py:174
  74.5 0.0 copy-start.1
  74.5 1.4 %reshape.33 = f32[512,256]{1,0:T(8,128)S(1)} reshape(f32[64,4,2,256]{3,2,1,0:T(2,128)} %get-tuple-element.6) | data formatting | bytes 1048576 | tf_op jit(solution)/shard_map/reshape | solution.py:218
  76.0 0.2 copy.22
  76.2 0.0 copy-done.1
  76.2 0.9 %fusion.3 = bf16[256,512]{1,0:T(8,128)(2,1)} fusion(f32[256,3,512]{2,0,1:T(8,128)S(1)} %fusion, f32[512,256]{0,1:T(8,128)S(1)} %copy.22, f32[512]{0:T(512)S(1)} %copy-done.1), kind=kLoop, calls=%fused_computation.10 | loop fusion | flops 655360 | bytes 2361344 | tf_op jit(solution)/shard_map/convert_element_type | solution.py:219
Async XLA Ops:
  0.0 9.6 %copy-start = (bf16[256,3,512]{2,0,1:T(8,128)(2,1)S(1)}, bf16[256,3,512]{2,0,1:T(8,128)(2,1)}, u32[]{:S(2)}) copy-start(bf16[256,3,512]{2,0,1:T(8,128)(2,1)} %param.14) | copy-start | bytes 2359300
  0.8 8.8 %collective-permute-start = (bf16[2,3,512]{2,0,1:T(2,128)(2,1)S(1)}, bf16[2,3,512]{2,0,1:T(2,128)(2,1)S(1)}, u32[]{:S(2)}, u32[]{:S(2)}) collective-permute-start(bf16[2,3,512]{2,0,1:T(2,128)(2,1)S(1)} %slice.31), channel_id=1, source_target_pairs={{0,8},{8,16},{16,24},{24,32},{32,40},{40,48},{48,56},{56,64},{64,7... | collective-permute-start | bytes 18440 | tf_op jit(solution)/shard_map/ppermute | solution.py:199
  74.5 1.6 %copy-start.1 = (f32[512]{0:T(512)S(1)}, f32[512]{0:T(512)}, u32[]{:S(2)}) copy-start(f32[512]{0:T(512)} %param.16) | copy-start | bytes 6148

commit v9 on v7

--- a/solution.py
+++ b/solution.py
@@ -77,7 +77,9 @@
     barrier = pltpu.get_barrier_semaphore()
 
     def peer_of(step):
-        return lax.rem(me + 1 + step, shards)
+        distance = step // 2 + 1
+        sign = 1 - 2 * (step % 2)
+        return lax.rem(me + sign * distance + shards, shards)
 
     def greet(step, carry):
         pl.semaphore_signal(barrier, inc=1, device_id=(peer_of(step), row), device_id_type=mesh_id)

time: 74.8 us -> 74.4 us (level)
  Pallas kernels: 58.6 us -> 57.7 us
    pallas_call x1, Pallas kernels: 58.6 us -> 57.7 us  [long_conv(): pl.pallas_call(functools.partial(fused_kernel, blocks, parts), out_shape=...]
where the time goes in v9:
time: 74.4 us; the launch traced here: 73.5 us
  Pallas kernels  57.7 us (78%)
  local copies, waits for them, and re-layouts  6.76 us (9%)
  starting transfers between devices  4.51 us (6%)
  other arithmetic  2.66 us (4%)
  waiting for transfers between devices  1.78 us (2%)
    pallas_call x1, Pallas kernels, long_conv(): pl.pallas_call(functools.partial(fused_kernel, blocks, parts), out_shape=...  57.7 us
    ppermute x1, starting transfers between devices, shifted(): return lax.ppermute(block, axis, route)  4.51 us
    ppermute x1, waiting for transfers between devices, shifted(): return lax.ppermute(block, axis, route)  1.78 us
  transfers between devices with their start and end apart: 1, of which 1 were waited for; matrix products, arithmetic and copies ran while one was open for 3% of the time, Pallas kernels for 0%

profile of v9, /device:TPU:1, one launch (start us, length us, event | category | flops | bytes accessed | tf_op | source)
XLA Modules:
  0.0 73.5 jit_solution(6019507066451702545)
XLA Ops:
  0.0 0.0 copy-start
  0.0 0.8 %slice.31 = bf16[2,3,512]{2,0,1:T(2,128)(2,1)S(1)} slice(bf16[256,3,512]{2,0,1:T(8,128)(2,1)} %param.14), slice={[254:256], [0:3], [0:512]} | slice | bytes 12288 | tf_op jit(solution)/shard_map/slice | solution.py:209
  0.8 4.5 %collective-permute-start = (bf16[2,3,512]{2,0,1:T(2,128)(2,1)S(1)}, bf16[2,3,512]{2,0,1:T(2,128)(2,1)S(1)}, u32[]{:S(2)}, u32[]{:S(2)}) collective-permute-start(bf16[2,3,512]{2,0,1:T(2,128)(2,1)S(1)} %slice.31), channel_id=1, source_target_pairs={{0,8},{8,16},{16,24},{24,32},{32,40},{40,48},{48,56},{56,64},{64,7... | collective-permute-start | bytes 18440 | tf_op jit(solution)/shard_map/ppermute | solution.py:201
  5.3 0.7 %slice_bitcast_fusion.3 = (f32[3,512]{1,0:T(4,128)S(1)}, f32[3,512]{1,0:T(4,128)S(1)}, f32[3,512]{1,0:T(4,128)S(1)}) fusion(f32[3,3,512]{2,1,0:T(4,128)} %param.15), kind=kLoop, calls=%fused_computation.15 | loop fusion | bytes 36864 | tf_op jit(solution)/shard_map/mul | solution.py:211
  6.1 1.2 %copy.19 = f32[256,512]{0,1:T(8,128)S(1)} copy(f32[256,512]{1,0:T(8,128)} %param.17) | data formatting | bytes 1048576 | tf_op args[3]
  7.3 0.5 stack.9
  7.9 1.8 %collective-permute-done = bf16[2,3,512]{2,0,1:T(2,128)(2,1)S(1)} collective-permute-done((bf16[2,3,512]{2,0,1:T(2,128)(2,1)S(1)}, bf16[2,3,512]{2,0,1:T(2,128)(2,1)S(1)}, u32[]{:S(2)}, u32[]{:S(2)}) %collective-permute-start) | collective-permute-done | bytes 6176 | tf_op jit(solution)/shard_map/ppermute | solution.py:201
  9.6 0.0 copy-done
  9.6 0.2 maximum_convert_fusion
  9.9 0.5 fusion
  10.4 0.1 slice_multiply_fusion.3
  10.4 0.4 copy.18
  10.9 0.9 %maximum_bitcast_fusion = f32[64,2,2,4,256]{4,2,3,1,0:T(2,128)S(1)} fusion(f32[1,256,64,2,4]{1,0,4,3,2:T(1,128)S(1)} %stack.9, f32[1,256,64,2,4]{1,0,4,3,2:T(1,128)S(1)} %bitcast.25), kind=kLoop, calls=%fused_computation.5 | loop fusion | flops 262144 | bytes 2097152 | tf_op jit(solution)/shard_map/transpose | solution.py:218
  11.8 0.3 copy.21
  12.1 1.3 %reshape.32.src_ref = f32[64,2,8,256]{3,2,1,0:T(8,128)} reshape(f32[64,2,2,4,256]{4,3,2,1,0:T(4,128)S(1)} %copy.21) | data formatting | bytes 2097152 | tf_op jit(solution)/shard_map/reshape | solution.py:218
  13.4 57.7 %shard_map.136 = (f32[64,2,4,256]{3,2,1,0:T(4,128)}, f32[64,2,8,256]{3,2,1,0:T(8,128)}, f32[2,4,64,256]{3,2,1,0:T(8,128)}) custom-call(f32[64,2,8,256]{3,2,1,0:T(8,128)} %reshape.32.src_ref, f32[72,64]{1,0:T(8,128)} %constant.20.clone.refs_0_, f32[72,64]{1,0:T(8,128)} %constant.21.clone.refs_1_, f32[72,256]{1,0:T(8,128)} %constant.22.clone.refs_2_, ...), custom_call_target="tpu_custom_call" | custom-call | tf_op jit(solution)/shard_map/pallas_call | solution.py:176
  71.1 0.0 copy-start.1
  71.1 1.2 %reshape.33 = f32[512,256]{1,0:T(8,128)S(1)} reshape(f32[64,2,4,256]{3,2,1,0:T(4,128)} %get-tuple-element.6) | data formatting | bytes 1048576 | tf_op jit(solution)/shard_map/reshape | solution.py:220
  72.3 0.2 copy.22
  72.6 0.0 copy-done.1
  72.6 0.9 %fusion.3 = bf16[256,512]{1,0:T(8,128)(2,1)} fusion(f32[256,3,512]{2,0,1:T(8,128)S(1)} %fusion, f32[512,256]{0,1:T(8,128)S(1)} %copy.22, f32[512]{0:T(512)S(1)} %copy-done.1), kind=kLoop, calls=%fused_computation.10 | loop fusion | flops 655360 | bytes 2361344 | tf_op jit(solution)/shard_map/convert_element_type | solution.py:221
Async XLA Ops:
  0.0 9.6 %copy-start = (bf16[256,3,512]{2,0,1:T(8,128)(2,1)S(1)}, bf16[256,3,512]{2,0,1:T(8,128)(2,1)}, u32[]{:S(2)}) copy-start(bf16[256,3,512]{2,0,1:T(8,128)(2,1)} %param.14) | copy-start | bytes 2359300
  0.8 8.8 %collective-permute-start = (bf16[2,3,512]{2,0,1:T(2,128)(2,1)S(1)}, bf16[2,3,512]{2,0,1:T(2,128)(2,1)S(1)}, u32[]{:S(2)}, u32[]{:S(2)}) collective-permute-start(bf16[2,3,512]{2,0,1:T(2,128)(2,1)S(1)} %slice.31), channel_id=1, source_target_pairs={{0,8},{8,16},{16,24},{24,32},{32,40},{40,48},{48,56},{56,64},{64,7... | collective-permute-start | bytes 18440 | tf_op jit(solution)/shard_map/ppermute | solution.py:201
  71.1 1.4 %copy-start.1 = (f32[512]{0:T(512)S(1)}, f32[512]{0:T(512)}, u32[]{:S(2)}) copy-start(f32[512]{0:T(512)} %param.16) | copy-start | bytes 6148

commit v10 on v9

--- a/solution.py
+++ b/solution.py
@@ -66,14 +66,15 @@
         o_ref[g] = dot(ci, vre) - dot(si, vim)
 
 
-def fused_kernel(shards, parts, src_ref, *refs):
-    tables = refs[:10]
-    out_ref, recv_ref, stage_ref = refs[10:13]
-    x_ref, o_ref, yre_ref, yim_ref, sends, recvs, local = refs[13:]
+def fused_kernel(shards, sizes, *refs):
+    parts = len(sizes)
+    srcs = refs[:parts]
+    tables = refs[parts : parts + 10]
+    outs, recvs_hbm, stages = (refs[parts + 10 + k * parts : parts + 10 + (k + 1) * parts] for k in range(3))
+    x_all, o_all, yre_all, yim_all, sends, recvs, local = refs[parts + 10 + 3 * parts :]
     me = lax.axis_index("seq")
     row = lax.axis_index("ch")
     mesh_id = pl.DeviceIdType.MESH
-    streams = x_ref.shape[0]
     barrier = pltpu.get_barrier_semaphore()
 
     def peer_of(step):
@@ -121,14 +122,20 @@
         return finish
 
     arrivals = [
-        scatter(lambda j, h=h: src_ref.at[j, h], lambda j, h=h: recv_ref.at[j, h], h)
+        scatter(lambda j, h=h: srcs[h].at[j], lambda j, h=h: recvs_hbm[h].at[j], h)
         for h in range(parts)
     ]
     returns = []
+    pad = tables[0].shape[0]
     for h in range(parts):
+        streams = 2 * sizes[h]
+        x_ref = x_all.at[pl.ds(0, streams)]
+        o_ref = o_all.at[pl.ds(0, sizes[h])]
+        yre_ref = yre_all.at[pl.ds(0, streams * pad)]
+        yim_ref = yim_all.at[pl.ds(0, streams * pad)]
         arrivals[h]()
         gathers = [
-            pltpu.make_async_copy(recv_ref.at[:, h, j, :], x_ref.at[j], local.at[2 * parts + j])
+            pltpu.make_async_copy(recvs_hbm[h].at[:, j, :], x_ref.at[j], local.at[2 * parts + j])
             for j in range(streams)
         ]
         for copy in gathers:
@@ -136,13 +143,13 @@
         for copy in gathers:
             copy.wait()
         conv_body(x_ref, *tables, o_ref, yre_ref, yim_ref)
-        put = pltpu.make_async_copy(o_ref, stage_ref.at[h], local.at[2 * parts + streams])
+        put = pltpu.make_async_copy(o_ref, stages[h], local.at[2 * parts + 2 * max(sizes)])
         put.start()
         put.wait()
         returns.append(
             scatter(
-                lambda j, h=h: stage_ref.at[h, :, j, :],
-                lambda j, h=h: out_ref.at[j, h],
+                lambda j, h=h: stages[h].at[:, j, :],
+                lambda j, h=h: outs[h].at[j],
                 parts + h,
             )
         )
@@ -151,8 +158,11 @@
 
 
 def long_conv(pieces):
-    blocks, parts, streams, rows = pieces.shape
-    group = streams // 2
+    blocks, _, rows = pieces[0].shape
+    sizes = tuple(p.shape[1] // 2 for p in pieces)
+    group = max(sizes)
+    streams = 2 * group
+    parts = len(sizes)
     coarse = 2 * blocks
     total = coarse * rows
     half = blocks + 1
@@ -174,14 +184,12 @@
     anywhere = pl.BlockSpec(memory_space=pl.ANY)
     f32 = jnp.float32
     return pl.pallas_call(
-        functools.partial(fused_kernel, blocks, parts),
-        out_shape=[
-            jax.ShapeDtypeStruct((blocks, parts, group, rows), f32),
-            jax.ShapeDtypeStruct((blocks, parts, streams, rows), f32),
-            jax.ShapeDtypeStruct((parts, group, blocks, rows), f32),
-        ],
-        in_specs=[anywhere] + [vmem] * len(tables),
-        out_specs=[anywhere] * 3,
+        functools.partial(fused_kernel, blocks, sizes),
+        out_shape=[jax.ShapeDtypeStruct((blocks, s, rows), f32) for s in sizes]
+        + [jax.ShapeDtypeStruct((blocks, 2 * s, rows), f32) for s in sizes]
+        + [jax.ShapeDtypeStruct((s, blocks, rows), f32) for s in sizes],
+        in_specs=[anywhere] * parts + [vmem] * len(tables),
+        out_specs=[anywhere] * (3 * parts),
         scratch_shapes=[
             pltpu.VMEM((streams, blocks, rows), f32),
             pltpu.VMEM((group, blocks, rows), f32),
@@ -192,7 +200,7 @@
             pltpu.SemaphoreType.DMA((2 * parts + streams + 1,)),
         ],
         compiler_params=pltpu.CompilerParams(collective_id=0, has_side_effects=True),
-    )(pieces, *tables)[0]
+    )(*pieces, *tables)[:parts]
 
 
 def shifted(block, axis, distance):
@@ -213,10 +221,14 @@
         feat = feat + short_w[tap] * extended[taps - 1 - tap : taps - 1 - tap + rows]
     query = feat[:, 0, :]
     signal = feat[:, 1, :] * feat[:, 2, :]
-    parts = 2
-    source = jnp.stack([signal, filt]).reshape(2, rows, shards, parts, group // parts)
-    source = source.transpose(2, 3, 0, 4, 1).reshape(shards, parts, 2 * group // parts, rows)
-    values = long_conv(source)
+    sizes = (group - group * 3 // 8, group * 3 // 8)
+    source = jnp.stack([signal, filt]).reshape(2, rows, shards, group)
+    pieces, start = [], 0
+    for size in sizes:
+        piece = source[:, :, :, start : start + size].transpose(2, 0, 3, 1)
+        pieces.append(piece.reshape(shards, 2 * size, rows))
+        start += size
+    values = jnp.concatenate(long_conv(pieces), axis=1)
     conv = values.reshape(width, rows).T
     return (query * (conv + skip * signal)).astype(jnp.bfloat16)
 

time: 74.4 us -> 88.5 us (1.19)
  Pallas kernels: 57.7 us -> 70.3 us
  other arithmetic: 2.66 us -> 3.7 us
    pallas_call x1, Pallas kernels: 57.7 us -> 70.3 us  [long_conv(): pl.pallas_call(functools.partial(fused_kernel, blocks, sizes), out_shape=...]
    add x1, other arithmetic: 0.47 us -> 1.62 us  [on_device(): feat = feat + short_w[tap] * extended[taps - 1 - tap:taps - 1 - tap + rows]]
    reshape x3 -> x2, local copies, waits for them, and re-layouts: 2.75 us -> 2.39 us  [on_device(): pieces.append(piece.reshape(shards, 2 * size, rows))]
where the time goes in v10:
time: 88.5 us; the launch traced here: 88.1 us
  Pallas kernels  70.3 us (79%)
  local copies, waits for them, and re-layouts  6.93 us (8%)
  starting transfers between devices  4.51 us (5%)
  other arithmetic  3.7 us (4%)
  waiting for transfers between devices  2.49 us (3%)
    pallas_call x1, Pallas kernels, long_conv(): pl.pallas_call(functools.partial(fused_kernel, blocks, sizes), out_shape=...  70.3 us
    ppermute x1, starting transfers between devices, shifted(): return lax.ppermute(block, axis, route)  4.51 us
    ppermute x1, waiting for transfers between devices, shifted(): return lax.ppermute(block, axis, route)  2.49 us
    reshape x2, local copies, waits for them, and re-layouts, on_device(): pieces.append(piece.reshape(shards, 2 * size, rows))  2.39 us
  transfers between devices with their start and end apart: 1, of which 1 were waited for; matrix products, arithmetic and copies ran while one was open for 3% of the time, Pallas kernels for 0%

profile of v10, /device:TPU:1, one launch (start us, length us, event | category | flops | bytes accessed | tf_op | source)
XLA Modules:
  0.0 88.1 jit_solution(9990817526930594833)
XLA Ops:
  0.0 0.0 copy-start
  0.0 0.8 slice.37
  0.8 0.3 copy.18
  1.1 4.5 %collective-permute-start = (bf16[2,3,512]{0,2,1:T(8,128)(2,1)S(1)}, bf16[2,3,512]{0,2,1:T(8,128)(2,1)S(1)}, u32[]{:S(2)}, u32[]{:S(2)}) collective-permute-start(bf16[2,3,512]{0,2,1:T(8,128)(2,1)S(1)} %copy.18), channel_id=1, source_target_pairs={{0,8},{8,16},{16,24},{24,32},{32,40},{40,48},{48,56},{56,64},{64,7... | collective-permute-start | bytes 18440 | tf_op jit(solution)/shard_map/ppermute | solution.py:209
  5.6 0.7 slice_bitcast_fusion.3
  6.3 1.4 %copy.19 = bf16[256,3,512]{0,2,1:T(8,128)(2,1)S(1)} copy(bf16[256,3,512]{2,0,1:T(8,128)(2,1)} %param.14) | data formatting | bytes 1572864 | tf_op args[0]
  7.7 0.0 copy-done
  7.8 0.2 copy.20
  8.0 2.5 %collective-permute-done = bf16[2,3,512]{0,2,1:T(8,128)(2,1)S(1)} collective-permute-done((bf16[2,3,512]{0,2,1:T(8,128)(2,1)S(1)}, bf16[2,3,512]{0,2,1:T(8,128)(2,1)S(1)}, u32[]{:S(2)}, u32[]{:S(2)}) %collective-permute-start) | collective-permute-done | bytes 6176 | tf_op jit(solution)/shard_map/ppermute | solution.py:209
  10.5 0.5 maximum_convert_fusion
  11.0 1.6 %fusion = f32[256,3,512]{0,2,1:T(8,128)S(1)} fusion(f32[258,3,512]{0,2,1:T(8,128)S(1)} %maximum_convert_fusion, f32[3,512]{1,0:T(4,128)S(1)} %get-tuple-element.10, f32[3,512]{1,0:T(4,128)S(1)} %get-tuple-element.11, f32[3,512]{1,0:T(4,128)S(1)} %get-tuple-element.9), kind=kLoop, calls=%fused_computation.1 | loop fusion | flops 1966080 | bytes 6309888 | tf_op jit(solution)/shard_map/add | solution.py:221
  12.6 0.1 fusion.6
  12.7 0.1 fusion.2
  12.8 0.1 maximum_bitcast_fusion
  12.9 0.1 copy.22
  13.0 0.2 copy.21
  13.2 1.0 %copy.24.refs_1_ = f32[64,6,256]{2,1,0:T(8,128)} copy(f32[64,6,256]{2,0,1:T(8,128)S(1)} %bitcast.36) | data formatting | bytes 786432 | tf_op jit(solution)/shard_map/reshape | solution.py:229
  14.2 1.4 %copy.23.refs_0_ = f32[64,10,256]{2,1,0:T(8,128)} copy(f32[64,10,256]{2,0,1:T(8,128)S(1)} %bitcast.35) | data formatting | bytes 1310720 | tf_op jit(solution)/shard_map/reshape | solution.py:229
  15.6 0.0 copy-start.1
  15.6 70.3 %shard_map.136 = (f32[64,5,256]{2,1,0:T(8,128)}, f32[64,3,256]{2,1,0:T(4,128)}, f32[64,10,256]{2,1,0:T(8,128)}, f32[64,6,256]{2,1,0:T(8,128)}, f32[5,64,256]{2,1,0:T(8,128)}, /*index=5*/f32[3,64,256]{2,1,0:T(8,128)}) custom-call(f32[64,10,256]{2,1,0:T(8,128)} %copy.23.refs_0_, f32[64,6,256]{2,1,0:T(8,128)} %copy.24.refs_1_, ...), custom_call_target="tpu_custom_call" | custom-call | tf_op jit(solution)/shard_map/pallas_call | solution.py:186
  85.9 0.0 copy-done.1
  85.9 1.3 %fusion.4 = bf16[256,512]{0,1:T(8,128)(2,1)S(1)} fusion(f32[256,3,512]{0,2,1:T(8,128)S(1)} %fusion, f32[64,3,256]{2,1,0:T(4,128)} %get-tuple-element.8, f32[64,5,256]{2,1,0:T(8,128)} %get-tuple-element.7, f32[512]{0:T(512)S(1)} %copy-done.1), kind=kLoop, calls=%fused_computation.12 | loop fusion | flops 786432 | bytes 2361344 | tf_op jit(solution)/shard_map/convert_element_type | solution.py:233
  87.2 0.8 copy.25
Async XLA Ops:
  0.0 7.7 %copy-start = (f32[256,512]{1,0:T(8,128)S(1)}, f32[256,512]{1,0:T(8,128)}, u32[]{:S(2)}) copy-start(f32[256,512]{1,0:T(8,128)} %param.17) | copy-start | bytes 1572868
  1.1 9.4 %collective-permute-start = (bf16[2,3,512]{0,2,1:T(8,128)(2,1)S(1)}, bf16[2,3,512]{0,2,1:T(8,128)(2,1)S(1)}, u32[]{:S(2)}, u32[]{:S(2)}) collective-permute-start(bf16[2,3,512]{0,2,1:T(8,128)(2,1)S(1)} %copy.18), channel_id=1, source_target_pairs={{0,8},{8,16},{16,24},{24,32},{32,40},{40,48},{48,56},{56,64},{64,7... | collective-permute-start | bytes 18440 | tf_op jit(solution)/shard_map/ppermute | solution.py:209
  15.6 70.3 %copy-start.1 = (f32[512]{0:T(512)S(1)}, f32[512]{0:T(512)}, u32[]{:S(2)}) copy-start(f32[512]{0:T(512)} %param.16) | copy-start | bytes 6148

commit v11 on v9

--- a/solution.py
+++ b/solution.py
@@ -74,6 +74,7 @@
     row = lax.axis_index("ch")
     mesh_id = pl.DeviceIdType.MESH
     streams = x_ref.shape[0]
+    size = streams // 2
     barrier = pltpu.get_barrier_semaphore()
 
     def peer_of(step):
@@ -121,14 +122,20 @@
         return finish
 
     arrivals = [
-        scatter(lambda j, h=h: src_ref.at[j, h], lambda j, h=h: recv_ref.at[j, h], h)
+        scatter(
+            lambda j, h=h: src_ref.at[j, :, pl.ds(h * size, size), :],
+            lambda j, h=h: recv_ref.at[j, h],
+            h,
+        )
         for h in range(parts)
     ]
     returns = []
     for h in range(parts):
         arrivals[h]()
         gathers = [
-            pltpu.make_async_copy(recv_ref.at[:, h, j, :], x_ref.at[j], local.at[2 * parts + j])
+            pltpu.make_async_copy(
+                recv_ref.at[:, h, j // size, j % size, :], x_ref.at[j], local.at[2 * parts + j]
+            )
             for j in range(streams)
         ]
         for copy in gathers:
@@ -142,7 +149,7 @@
         returns.append(
             scatter(
                 lambda j, h=h: stage_ref.at[h, :, j, :],
-                lambda j, h=h: out_ref.at[j, h],
+                lambda j, h=h: out_ref.at[j, pl.ds(h * size, size), :],
                 parts + h,
             )
         )
@@ -150,9 +157,10 @@
         finish()
 
 
-def long_conv(pieces):
-    blocks, parts, streams, rows = pieces.shape
-    group = streams // 2
+def long_conv(pieces, parts):
+    blocks, _, channels, rows = pieces.shape
+    group = channels // parts
+    streams = 2 * group
     coarse = 2 * blocks
     total = coarse * rows
     half = blocks + 1
@@ -176,8 +184,8 @@
     return pl.pallas_call(
         functools.partial(fused_kernel, blocks, parts),
         out_shape=[
-            jax.ShapeDtypeStruct((blocks, parts, group, rows), f32),
-            jax.ShapeDtypeStruct((blocks, parts, streams, rows), f32),
+            jax.ShapeDtypeStruct((blocks, channels, rows), f32),
+            jax.ShapeDtypeStruct((blocks, parts, 2, group, rows), f32),
             jax.ShapeDtypeStruct((parts, group, blocks, rows), f32),
         ],
         in_specs=[anywhere] + [vmem] * len(tables),
@@ -213,10 +221,8 @@
         feat = feat + short_w[tap] * extended[taps - 1 - tap : taps - 1 - tap + rows]
     query = feat[:, 0, :]
     signal = feat[:, 1, :] * feat[:, 2, :]
-    parts = 2
-    source = jnp.stack([signal, filt]).reshape(2, rows, shards, parts, group // parts)
-    source = source.transpose(2, 3, 0, 4, 1).reshape(shards, parts, 2 * group // parts, rows)
-    values = long_conv(source)
+    source = jnp.stack([signal, filt]).reshape(2, rows, shards, group).transpose(2, 0, 3, 1)
+    values = long_conv(source, 2)
     conv = values.reshape(width, rows).T
     return (query * (conv + skip * signal)).astype(jnp.bfloat16)
 

time: 74.4 us -> 72.6 us (0.976)
  local copies, waits for them, and re-layouts: 6.76 us -> 4.24 us
    reshape x1 -> x0, local copies, waits for them, and re-layouts: 1.33 us -> none  [on_device(): source.transpose(2, 3, 0, 4, 1)]
where the time goes in v11:
time: 72.6 us; the launch traced here: 71.8 us
  Pallas kernels  57.9 us (80%)
  starting transfers between devices  4.51 us (6%)
  local copies, waits for them, and re-layouts  4.24 us (6%)
  other arithmetic  2.75 us (4%)
  waiting for transfers between devices  2.32 us (3%)
    pallas_call x1, Pallas kernels, long_conv(): pl.pallas_call(functools.partial(fused_kernel, blocks, parts), out_shape=...  57.9 us
    ppermute x1, starting transfers between devices, shifted(): return lax.ppermute(block, axis, route)  4.51 us
    ppermute x1, waiting for transfers between devices, shifted(): return lax.ppermute(block, axis, route)  2.32 us
  transfers between devices with their start and end apart: 1, of which 1 were waited for; matrix products, arithmetic and copies ran while one was open for 3% of the time, Pallas kernels for 0%

profile of v11, /device:TPU:1, one launch (start us, length us, event | category | flops | bytes accessed | tf_op | source)
XLA Modules:
  0.0 71.8 jit_solution(636195540681529716)
XLA Ops:
  0.0 0.0 copy-start
  0.0 0.8 %slice.31 = bf16[2,3,512]{2,0,1:T(2,128)(2,1)S(1)} slice(bf16[256,3,512]{2,0,1:T(8,128)(2,1)} %param.14), slice={[254:256], [0:3], [0:512]} | slice | bytes 12288 | tf_op jit(solution)/shard_map/slice | solution.py:217
  0.8 4.5 %collective-permute-start = (bf16[2,3,512]{2,0,1:T(2,128)(2,1)S(1)}, bf16[2,3,512]{2,0,1:T(2,128)(2,1)S(1)}, u32[]{:S(2)}, u32[]{:S(2)}) collective-permute-start(bf16[2,3,512]{2,0,1:T(2,128)(2,1)S(1)} %slice.31), channel_id=1, source_target_pairs={{0,8},{8,16},{16,24},{24,32},{32,40},{40,48},{48,56},{56,64},{64,7... | collective-permute-start | bytes 18440 | tf_op jit(solution)/shard_map/ppermute | solution.py:209
  5.3 0.7 %slice_bitcast_fusion.3 = (f32[3,512]{1,0:T(4,128)S(1)}, f32[3,512]{1,0:T(4,128)S(1)}, f32[3,512]{1,0:T(4,128)S(1)}) fusion(f32[3,3,512]{2,1,0:T(4,128)} %param.15), kind=kLoop, calls=%fused_computation.15 | loop fusion | bytes 36864 | tf_op jit(solution)/shard_map/mul | solution.py:219
  6.1 1.2 %copy.16 = f32[256,512]{0,1:T(8,128)S(1)} copy(f32[256,512]{1,0:T(8,128)} %param.17) | data formatting | bytes 1048576 | tf_op args[3]
  7.3 2.3 %collective-permute-done = bf16[2,3,512]{2,0,1:T(2,128)(2,1)S(1)} collective-permute-done((bf16[2,3,512]{2,0,1:T(2,128)(2,1)S(1)}, bf16[2,3,512]{2,0,1:T(2,128)(2,1)S(1)}, u32[]{:S(2)}, u32[]{:S(2)}) %collective-permute-start) | collective-permute-done | bytes 6176 | tf_op jit(solution)/shard_map/ppermute | solution.py:209
  9.6 0.0 copy-done
  9.6 0.2 maximum_convert_fusion
  9.9 0.5 fusion
  10.4 0.1 slice_multiply_fusion.3
  10.4 0.2 copy.15
  10.7 1.0 %maximum_bitcast_fusion.src_ref = f32[64,2,8,256]{3,2,1,0:T(8,128)} fusion(f32[1,256,64,8]{1,3,0,2:T(8,128)S(1)} %bitcast.25, f32[1,256,64,8]{1,3,0,2:T(8,128)S(1)} %bitcast.26), kind=kLoop, calls=%fused_computation.5 | loop fusion | flops 262144 | bytes 2097152 | tf_op jit(solution)/shard_map/transpose | solution.py:224
  11.7 0.0 copy-start.1
  11.7 57.9 %shard_map.136 = (f32[64,8,256]{2,1,0:T(8,128)}, f32[64,2,2,4,256]{4,3,2,1,0:T(4,128)}, f32[2,4,64,256]{3,2,1,0:T(8,128)}) custom-call(f32[64,2,8,256]{3,2,1,0:T(8,128)} %maximum_bitcast_fusion.src_ref, f32[72,64]{1,0:T(8,128)} %constant.20.clone.refs_0_, f32[72,64]{1,0:T(8,128)} %constant.21.clone.refs_1_, f32[72,256]{1,0:T(8,128)} %constant.22.clone.refs_2_, ...), custom_call_target="tpu_custom_call" | custom-call | tf_op jit(solution)/shard_map/pallas_call | solution.py:184
  69.6 1.2 %copy.17 = f32[512,256]{0,1:T(8,128)S(1)} copy(f32[512,256]{1,0:T(8,128)} %bitcast.27) | data formatting | bytes 1048576 | tf_op jit(solution)/shard_map/reshape | solution.py:226
  70.8 0.0 copy-done.1
  70.8 0.9 %fusion.3 = bf16[256,512]{1,0:T(8,128)(2,1)} fusion(f32[256,3,512]{2,0,1:T(8,128)S(1)} %fusion, f32[512,256]{0,1:T(8,128)S(1)} %copy.17, f32[512]{0:T(512)S(1)} %copy-done.1), kind=kLoop, calls=%fused_computation.10 | loop fusion | flops 655360 | bytes 2361344 | tf_op jit(solution)/shard_map/convert_element_type | solution.py:227
Async XLA Ops:
  0.0 9.6 %copy-start = (bf16[256,3,512]{2,0,1:T(8,128)(2,1)S(1)}, bf16[256,3,512]{2,0,1:T(8,128)(2,1)}, u32[]{:S(2)}) copy-start(bf16[256,3,512]{2,0,1:T(8,128)(2,1)} %param.14) | copy-start | bytes 2359300
  0.8 8.8 %collective-permute-start = (bf16[2,3,512]{2,0,1:T(2,128)(2,1)S(1)}, bf16[2,3,512]{2,0,1:T(2,128)(2,1)S(1)}, u32[]{:S(2)}, u32[]{:S(2)}) collective-permute-start(bf16[2,3,512]{2,0,1:T(2,128)(2,1)S(1)} %slice.31), channel_id=1, source_target_pairs={{0,8},{8,16},{16,24},{24,32},{32,40},{40,48},{48,56},{56,64},{64,7... | collective-permute-start | bytes 18440 | tf_op jit(solution)/shard_map/ppermute | solution.py:209
  11.7 59.1 %copy-start.1 = (f32[512]{0:T(512)S(1)}, f32[512]{0:T(512)}, u32[]{:S(2)}) copy-start(f32[512]{0:T(512)} %param.16) | copy-start | bytes 6148

commit v12 on v11

--- a/solution.py
+++ b/solution.py
@@ -66,10 +66,10 @@
         o_ref[g] = dot(ci, vre) - dot(si, vim)
 
 
-def fused_kernel(shards, parts, src_ref, *refs):
+def fused_kernel(shards, parts, sig_ref, filt_ref, *refs):
     tables = refs[:10]
-    out_ref, recv_ref, stage_ref = refs[10:13]
-    x_ref, o_ref, yre_ref, yim_ref, sends, recvs, local = refs[13:]
+    res_ref, out_ref, recv_ref, stage_ref, src_ref = refs[10:15]
+    srcv_ref, outv_ref, x_ref, o_ref, yre_ref, yim_ref, sends, recvs, local = refs[15:]
     me = lax.axis_index("seq")
     row = lax.axis_index("ch")
     mesh_id = pl.DeviceIdType.MESH
@@ -87,6 +87,12 @@
         return carry
 
     lax.fori_loop(0, shards - 1, greet, 0)
+    chunk = srcv_ref.shape[1:]
+    srcv_ref[:, 0] = sig_ref[...].T.reshape(shards, *chunk[1:])
+    srcv_ref[:, 1] = filt_ref[...].T.reshape(shards, *chunk[1:])
+    fill = pltpu.make_async_copy(srcv_ref, src_ref, local.at[2 * parts + streams + 1])
+    fill.start()
+    fill.wait()
     pl.semaphore_wait(barrier, shards - 1)
 
     def scatter(source, target, phase):
@@ -155,10 +161,15 @@
         )
     for finish in returns:
         finish()
-
-
-def long_conv(pieces, parts):
-    blocks, _, channels, rows = pieces.shape
+    drain = pltpu.make_async_copy(out_ref, outv_ref, local.at[2 * parts + streams + 2])
+    drain.start()
+    drain.wait()
+    res_ref[...] = outv_ref[...].reshape(res_ref.shape[1], res_ref.shape[0]).T
+
+
+def long_conv(signal, filt, blocks, parts):
+    rows, width = signal.shape
+    channels = width // blocks
     group = channels // parts
     streams = 2 * group
     coarse = 2 * blocks
@@ -184,23 +195,27 @@
     return pl.pallas_call(
         functools.partial(fused_kernel, blocks, parts),
         out_shape=[
+            jax.ShapeDtypeStruct((rows, width), f32),
             jax.ShapeDtypeStruct((blocks, channels, rows), f32),
             jax.ShapeDtypeStruct((blocks, parts, 2, group, rows), f32),
             jax.ShapeDtypeStruct((parts, group, blocks, rows), f32),
+            jax.ShapeDtypeStruct((blocks, 2, channels, rows), f32),
         ],
-        in_specs=[anywhere] + [vmem] * len(tables),
-        out_specs=[anywhere] * 3,
+        in_specs=[vmem] * (2 + len(tables)),
+        out_specs=[vmem] + [anywhere] * 4,
         scratch_shapes=[
+            pltpu.VMEM((blocks, 2, channels, rows), f32),
+            pltpu.VMEM((blocks, channels, rows), f32),
             pltpu.VMEM((streams, blocks, rows), f32),
             pltpu.VMEM((group, blocks, rows), f32),
             pltpu.VMEM((streams * pad, rows), f32),
             pltpu.VMEM((streams * pad, rows), f32),
             pltpu.SemaphoreType.DMA((2 * parts, blocks)),
             pltpu.SemaphoreType.DMA((2 * parts, blocks)),
-            pltpu.SemaphoreType.DMA((2 * parts + streams + 1,)),
+            pltpu.SemaphoreType.DMA((2 * parts + streams + 3,)),
         ],
         compiler_params=pltpu.CompilerParams(collective_id=0, has_side_effects=True),
-    )(pieces, *tables)[0]
+    )(signal, filt, *tables)[0]
 
 
 def shifted(block, axis, distance):
@@ -221,9 +236,7 @@
         feat = feat + short_w[tap] * extended[taps - 1 - tap : taps - 1 - tap + rows]
     query = feat[:, 0, :]
     signal = feat[:, 1, :] * feat[:, 2, :]
-    source = jnp.stack([signal, filt]).reshape(2, rows, shards, group).transpose(2, 0, 3, 1)
-    values = long_conv(source, 2)
-    conv = values.reshape(width, rows).T
+    conv = long_conv(signal, filt, shards, 2)
     return (query * (conv + skip * signal)).astype(jnp.bfloat16)
 
 

time: 72.6 us -> 75.5 us (1.040)
  local copies, waits for them, and re-layouts: 4.24 us -> 1.49 us
  Pallas kernels: 57.9 us -> 60.2 us
  other arithmetic: 2.75 us -> 4.68 us
  waiting for transfers between devices: 2.32 us -> 3.56 us
    pallas_call x1, Pallas kernels: 57.9 us -> 60.2 us  [long_conv(): pl.pallas_call(functools.partial(fused_kernel, blocks, parts), out_shape=...]
    ppermute x1, waiting for transfers between devices: 2.32 us -> 3.56 us  [shifted(): return lax.ppermute(block, axis, route)]
    unnamed x5 -> x2, local copies, waits for them, and re-layouts: 1.24 us -> 0.01 us
    reshape x1 -> x0, local copies, waits for them, and re-layouts: 1.24 us -> none  [on_device(): conv = values.reshape(width, rows).T]
    convert_element_type x1, other arithmetic: 0.23 us -> 1.37 us  [on_device(): extended = jnp.concatenate([rim, qkv], axis=0).astype(jnp.float32)]
    transpose x1 -> x0, other arithmetic: 1.05 us -> none  [on_device(): jnp.stack([signal, filt]).reshape(2, rows, shards, group)]
    convert_element_type x1, other arithmetic: 0.93 us -> 1.97 us  [on_device(): return (query * (conv + skip * signal)).astype(jnp.bfloat16)]
    mul x1, other arithmetic: 0.08 us -> 0.87 us  [on_device(): signal = feat[:, 1, :] * feat[:, 2, :]]
  transfers between devices with their start and end apart: 1 -> 1, of which waited for: 1 -> 1; matrix products, arithmetic and copies ran while one was open for 3% -> 1% of each run, Pallas kernels for 0% -> 0%
where the time goes in v12:
time: 75.5 us; the launch traced here: 74.5 us
  Pallas kernels  60.2 us (80%)
  other arithmetic  4.68 us (6%)
  starting transfers between devices  4.51 us (6%)
  waiting for transfers between devices  3.56 us (5%)
  local copies, waits for them, and re-layouts  1.49 us (2%)
    pallas_call x1, Pallas kernels, long_conv(): pl.pallas_call(functools.partial(fused_kernel, blocks, parts), out_shape=...  60.2 us
    ppermute x1, starting transfers between devices, shifted(): return lax.ppermute(block, axis, route)  4.51 us
    ppermute x1, waiting for transfers between devices, shifted(): return lax.ppermute(block, axis, route)  3.56 us
    convert_element_type x1, other arithmetic, on_device(): return (query * (conv + skip * signal)).astype(jnp.bfloat16)  1.97 us
  transfers between devices with their start and end apart: 1, of which 1 were waited for; matrix products, arithmetic and copies ran while one was open for 1% of the time, Pallas kernels for 0%

profile of v12, /device:TPU:1, one launch (start us, length us, event | category | flops | bytes accessed | tf_op | source)
XLA Modules:
  0.0 74.5 jit_solution(12991238263494923796)
XLA Ops:
  0.0 0.7 %slice.31 = bf16[2,3,512]{2,0,1:T(2,128)(2,1)S(1)} slice(bf16[256,3,512]{2,0,1:T(8,128)(2,1)} %param.14), slice={[254:256], [0:3], [0:512]} | slice | bytes 12288 | tf_op jit(solution)/shard_map/slice | solution.py:232
  0.8 4.5 %collective-permute-start = (bf16[2,3,512]{2,0,1:T(2,128)(2,1)S(1)}, bf16[2,3,512]{2,0,1:T(2,128)(2,1)S(1)}, u32[]{:S(2)}, u32[]{:S(2)}) collective-permute-start(bf16[2,3,512]{2,0,1:T(2,128)(2,1)S(1)} %slice.31), channel_id=1, source_target_pairs={{0,8},{8,16},{16,24},{24,32},{32,40},{40,48},{48,56},{56,64},{64,7... | collective-permute-start | bytes 18440 | tf_op jit(solution)/shard_map/ppermute | solution.py:224
  5.3 0.7 slice_bitcast_fusion.3
  6.0 3.6 %collective-permute-done = bf16[2,3,512]{2,0,1:T(2,128)(2,1)S(1)} collective-permute-done((bf16[2,3,512]{2,0,1:T(2,128)(2,1)S(1)}, bf16[2,3,512]{2,0,1:T(2,128)(2,1)S(1)}, u32[]{:S(2)}, u32[]{:S(2)}) %collective-permute-start) | collective-permute-done | bytes 6176 | tf_op jit(solution)/shard_map/ppermute | solution.py:224
  9.6 1.4 %maximum_convert_fusion = f32[258,3,512]{2,0,1:T(8,128)S(1)} fusion(bf16[256,3,512]{2,0,1:T(8,128)(2,1)} %param.14, bf16[2,3,512]{2,0,1:T(2,128)(2,1)S(1)} %collective-permute-done), kind=kLoop, calls=%fused_computation.5 | loop fusion | flops 1585152 | bytes 2377728 | tf_op jit(solution)/shard_map/convert_element_type | solution.py:233
  10.9 0.5 fusion
  11.4 0.9 %fusion.2.sig_ref = f32[256,512]{1,0:T(8,128)} fusion(f32[256,3,512]{2,0,1:T(8,128)S(1)} %fusion), kind=kLoop, calls=%fused_computation.7 | loop fusion | flops 131072 | bytes 1572864 | tf_op jit(solution)/shard_map/mul | solution.py:238
  12.3 0.0 copy-start
  12.3 60.2 %shard_map.136 = (f32[256,512]{1,0:T(8,128)}, f32[64,8,256]{2,1,0:T(8,128)}, f32[64,2,2,4,256]{4,3,2,1,0:T(4,128)}, f32[2,4,64,256]{3,2,1,0:T(8,128)}, f32[64,2,8,256]{3,2,1,0:T(8,128)}) custom-call(f32[256,512]{1,0:T(8,128)} %fusion.2.sig_ref, f32[256,512]{1,0:T(8,128)} %filt_ref.1, f32[72,64]{1,0:T(8,128)} %constant.20.clone.refs_0_, ...), custom_call_target="tpu_custom_call" | custom-call | tf_op jit(solution)/shard_map/pallas_call | solution.py:195
  72.5 0.0 copy-done
  72.5 2.0 %fusion.4 = bf16[256,512]{1,0:T(8,128)(2,1)} fusion(f32[256,3,512]{2,0,1:T(8,128)S(1)} %fusion, f32[256,512]{1,0:T(8,128)} %get-tuple-element.6, f32[512]{0:T(512)S(1)} %copy-done), kind=kLoop, calls=%fused_computation.10 | loop fusion | flops 655360 | bytes 2361344 | tf_op jit(solution)/shard_map/convert_element_type | solution.py:240
Async XLA Ops:
  0.8 8.8 %collective-permute-start = (bf16[2,3,512]{2,0,1:T(2,128)(2,1)S(1)}, bf16[2,3,512]{2,0,1:T(2,128)(2,1)S(1)}, u32[]{:S(2)}, u32[]{:S(2)}) collective-permute-start(bf16[2,3,512]{2,0,1:T(2,128)(2,1)S(1)} %slice.31), channel_id=1, source_target_pairs={{0,8},{8,16},{16,24},{24,32},{32,40},{40,48},{48,56},{56,64},{64,7... | collective-permute-start | bytes 18440 | tf_op jit(solution)/shard_map/ppermute | solution.py:224
  12.3 60.2 %copy-start = (f32[512]{0:T(512)S(1)}, f32[512]{0:T(512)}, u32[]{:S(2)}) copy-start(f32[512]{0:T(512)} %param.16) | copy-start | bytes 6148

commit v13 on v11

--- a/solution.py
+++ b/solution.py
@@ -9,7 +9,7 @@
 from jax.experimental.pallas import tpu as pltpu
 from jax.sharding import PartitionSpec as P
 
-PRECISION = lax.Precision.HIGHEST
+PRECISION = lax.Precision.HIGH
 
 
 def phase_table(count_out, count_in, modulus, sign):

time: 72.6 us -> 70.3 us (0.968)
  Pallas kernels: 57.9 us -> 55.9 us
    pallas_call x1, Pallas kernels: 57.9 us -> 55.9 us  [long_conv(): pl.pallas_call(functools.partial(fused_kernel, blocks, parts), out_shape=...]
where the time goes in v13:
time: 70.3 us; the launch traced here: 69.8 us
  Pallas kernels  55.9 us (80%)
  starting transfers between devices  4.51 us (6%)
  local copies, waits for them, and re-layouts  4.24 us (6%)
  other arithmetic  2.75 us (4%)
  waiting for transfers between devices  2.32 us (3%)
    pallas_call x1, Pallas kernels, long_conv(): pl.pallas_call(functools.partial(fused_kernel, blocks, parts), out_shape=...  55.9 us
    ppermute x1, starting transfers between devices, shifted(): return lax.ppermute(block, axis, route)  4.51 us
    ppermute x1, waiting for transfers between devices, shifted(): return lax.ppermute(block, axis, route)  2.32 us
  transfers between devices with their start and end apart: 1, of which 1 were waited for; matrix products, arithmetic and copies ran while one was open for 3% of the time, Pallas kernels for 0%

profile of v13, /device:TPU:1, one launch (start us, length us, event | category | flops | bytes accessed | tf_op | source)
XLA Modules:
  0.0 69.8 jit_solution(12962084411991611647)
XLA Ops:
  0.0 0.0 copy-start
  0.0 0.8 %slice.31 = bf16[2,3,512]{2,0,1:T(2,128)(2,1)S(1)} slice(bf16[256,3,512]{2,0,1:T(8,128)(2,1)} %param.14), slice={[254:256], [0:3], [0:512]} | slice | bytes 12288 | tf_op jit(solution)/shard_map/slice | solution.py:217
  0.8 4.5 %collective-permute-start = (bf16[2,3,512]{2,0,1:T(2,128)(2,1)S(1)}, bf16[2,3,512]{2,0,1:T(2,128)(2,1)S(1)}, u32[]{:S(2)}, u32[]{:S(2)}) collective-permute-start(bf16[2,3,512]{2,0,1:T(2,128)(2,1)S(1)} %slice.31), channel_id=1, source_target_pairs={{0,8},{8,16},{16,24},{24,32},{32,40},{40,48},{48,56},{56,64},{64,7... | collective-permute-start | bytes 18440 | tf_op jit(solution)/shard_map/ppermute | solution.py:209
  5.3 0.7 %slice_bitcast_fusion.3 = (f32[3,512]{1,0:T(4,128)S(1)}, f32[3,512]{1,0:T(4,128)S(1)}, f32[3,512]{1,0:T(4,128)S(1)}) fusion(f32[3,3,512]{2,1,0:T(4,128)} %param.15), kind=kLoop, calls=%fused_computation.15 | loop fusion | bytes 36864 | tf_op jit(solution)/shard_map/mul | solution.py:219
  6.1 1.2 %copy.16 = f32[256,512]{0,1:T(8,128)S(1)} copy(f32[256,512]{1,0:T(8,128)} %param.17) | data formatting | bytes 1048576 | tf_op args[3]
  7.3 2.3 %collective-permute-done = bf16[2,3,512]{2,0,1:T(2,128)(2,1)S(1)} collective-permute-done((bf16[2,3,512]{2,0,1:T(2,128)(2,1)S(1)}, bf16[2,3,512]{2,0,1:T(2,128)(2,1)S(1)}, u32[]{:S(2)}, u32[]{:S(2)}) %collective-permute-start) | collective-permute-done | bytes 6176 | tf_op jit(solution)/shard_map/ppermute | solution.py:209
  9.6 0.0 copy-done
  9.6 0.2 maximum_convert_fusion
  9.9 0.5 fusion
  10.4 0.1 slice_multiply_fusion.3
  10.4 0.2 copy.15
  10.7 1.0 %maximum_bitcast_fusion.src_ref = f32[64,2,8,256]{3,2,1,0:T(8,128)} fusion(f32[1,256,64,8]{1,3,0,2:T(8,128)S(1)} %bitcast.25, f32[1,256,64,8]{1,3,0,2:T(8,128)S(1)} %bitcast.26), kind=kLoop, calls=%fused_computation.5 | loop fusion | flops 262144 | bytes 2097152 | tf_op jit(solution)/shard_map/transpose | solution.py:224
  11.7 0.0 copy-start.1
  11.7 55.9 %shard_map.136 = (f32[64,8,256]{2,1,0:T(8,128)}, f32[64,2,2,4,256]{4,3,2,1,0:T(4,128)}, f32[2,4,64,256]{3,2,1,0:T(8,128)}) custom-call(f32[64,2,8,256]{3,2,1,0:T(8,128)} %maximum_bitcast_fusion.src_ref, f32[72,64]{1,0:T(8,128)} %constant.20.clone.refs_0_, f32[72,64]{1,0:T(8,128)} %constant.21.clone.refs_1_, f32[72,256]{1,0:T(8,128)} %constant.22.clone.refs_2_, ...), custom_call_target="tpu_custom_call" | custom-call | tf_op jit(solution)/shard_map/pallas_call | solution.py:184
  67.6 1.2 %copy.17 = f32[512,256]{0,1:T(8,128)S(1)} copy(f32[512,256]{1,0:T(8,128)} %bitcast.27) | data formatting | bytes 1048576 | tf_op jit(solution)/shard_map/reshape | solution.py:226
  68.8 0.0 copy-done.1
  68.9 0.9 %fusion.3 = bf16[256,512]{1,0:T(8,128)(2,1)} fusion(f32[256,3,512]{2,0,1:T(8,128)S(1)} %fusion, f32[512,256]{0,1:T(8,128)S(1)} %copy.17, f32[512]{0:T(512)S(1)} %copy-done.1), kind=kLoop, calls=%fused_computation.10 | loop fusion | flops 655360 | bytes 2361344 | tf_op jit(solution)/shard_map/convert_element_type | solution.py:227
Async XLA Ops:
  0.0 9.6 %copy-start = (bf16[256,3,512]{2,0,1:T(8,128)(2,1)S(1)}, bf16[256,3,512]{2,0,1:T(8,128)(2,1)}, u32[]{:S(2)}) copy-start(bf16[256,3,512]{2,0,1:T(8,128)(2,1)} %param.14) | copy-start | bytes 2359300
  0.8 8.8 %collective-permute-start = (bf16[2,3,512]{2,0,1:T(2,128)(2,1)S(1)}, bf16[2,3,512]{2,0,1:T(2,128)(2,1)S(1)}, u32[]{:S(2)}, u32[]{:S(2)}) collective-permute-start(bf16[2,3,512]{2,0,1:T(2,128)(2,1)S(1)} %slice.31), channel_id=1, source_target_pairs={{0,8},{8,16},{16,24},{24,32},{32,40},{40,48},{48,56},{56,64},{64,7... | collective-permute-start | bytes 18440 | tf_op jit(solution)/shard_map/ppermute | solution.py:209
  11.7 57.2 %copy-start.1 = (f32[512]{0:T(512)S(1)}, f32[512]{0:T(512)}, u32[]{:S(2)}) copy-start(f32[512]{0:T(512)} %param.16) | copy-start | bytes 6148

commit v14 on v11

--- a/solution.py
+++ b/solution.py
@@ -68,8 +68,8 @@
 
 def fused_kernel(shards, parts, src_ref, *refs):
     tables = refs[:10]
-    out_ref, recv_ref, stage_ref = refs[10:13]
-    x_ref, o_ref, yre_ref, yim_ref, sends, recvs, local = refs[13:]
+    out_ref, stage_ref = refs[10:12]
+    recv_ref, x_ref, o_ref, yre_ref, yim_ref, sends, recvs, local = refs[12:]
     me = lax.axis_index("seq")
     row = lax.axis_index("ch")
     mesh_id = pl.DeviceIdType.MESH
@@ -185,12 +185,12 @@
         functools.partial(fused_kernel, blocks, parts),
         out_shape=[
             jax.ShapeDtypeStruct((blocks, channels, rows), f32),
-            jax.ShapeDtypeStruct((blocks, parts, 2, group, rows), f32),
             jax.ShapeDtypeStruct((parts, group, blocks, rows), f32),
         ],
         in_specs=[anywhere] + [vmem] * len(tables),
-        out_specs=[anywhere] * 3,
+        out_specs=[anywhere] * 2,
         scratch_shapes=[
+            pltpu.VMEM((blocks, parts, 2, group, rows), f32),
             pltpu.VMEM((streams, blocks, rows), f32),
             pltpu.VMEM((group, blocks, rows), f32),
             pltpu.VMEM((streams * pad, rows), f32),

time: 72.6 us -> 71.7 us (0.988)
  no operation moved by 1% of the time
where the time goes in v14:
time: 71.7 us; the launch traced here: 71.1 us
  Pallas kernels  57.2 us (80%)
  starting transfers between devices  4.51 us (6%)
  local copies, waits for them, and re-layouts  4.24 us (6%)
  other arithmetic  2.75 us (4%)
  waiting for transfers between devices  2.32 us (3%)
    pallas_call x1, Pallas kernels, long_conv(): pl.pallas_call(functools.partial(fused_kernel, blocks, parts), out_shape=...  57.2 us
    ppermute x1, starting transfers between devices, shifted(): return lax.ppermute(block, axis, route)  4.51 us
    ppermute x1, waiting for transfers between devices, shifted(): return lax.ppermute(block, axis, route)  2.32 us
  transfers between devices with their start and end apart: 1, of which 1 were waited for; matrix products, arithmetic and copies ran while one was open for 3% of the time, Pallas kernels for 0%

profile of v14, /device:TPU:1, one launch (start us, length us, event | category | flops | bytes accessed | tf_op | source)
XLA Modules:
  0.0 71.1 jit_solution(13035199477115093235)
XLA Ops:
  0.0 0.0 copy-start
  0.0 0.8 %slice.31 = bf16[2,3,512]{2,0,1:T(2,128)(2,1)S(1)} slice(bf16[256,3,512]{2,0,1:T(8,128)(2,1)} %param.14), slice={[254:256], [0:3], [0:512]} | slice | bytes 12288 | tf_op jit(solution)/shard_map/slice | solution.py:217
  0.8 4.5 %collective-permute-start = (bf16[2,3,512]{2,0,1:T(2,128)(2,1)S(1)}, bf16[2,3,512]{2,0,1:T(2,128)(2,1)S(1)}, u32[]{:S(2)}, u32[]{:S(2)}) collective-permute-start(bf16[2,3,512]{2,0,1:T(2,128)(2,1)S(1)} %slice.31), channel_id=1, source_target_pairs={{0,8},{8,16},{16,24},{24,32},{32,40},{40,48},{48,56},{56,64},{64,7... | collective-permute-start | bytes 18440 | tf_op jit(solution)/shard_map/ppermute | solution.py:209
  5.3 0.7 %slice_bitcast_fusion.3 = (f32[3,512]{1,0:T(4,128)S(1)}, f32[3,512]{1,0:T(4,128)S(1)}, f32[3,512]{1,0:T(4,128)S(1)}) fusion(f32[3,3,512]{2,1,0:T(4,128)} %param.15), kind=kLoop, calls=%fused_computation.15 | loop fusion | bytes 36864 | tf_op jit(solution)/shard_map/mul | solution.py:219
  6.1 1.2 %copy.16 = f32[256,512]{0,1:T(8,128)S(1)} copy(f32[256,512]{1,0:T(8,128)} %param.17) | data formatting | bytes 1048576 | tf_op args[3]
  7.3 2.3 %collective-permute-done = bf16[2,3,512]{2,0,1:T(2,128)(2,1)S(1)} collective-permute-done((bf16[2,3,512]{2,0,1:T(2,128)(2,1)S(1)}, bf16[2,3,512]{2,0,1:T(2,128)(2,1)S(1)}, u32[]{:S(2)}, u32[]{:S(2)}) %collective-permute-start) | collective-permute-done | bytes 6176 | tf_op jit(solution)/shard_map/ppermute | solution.py:209
  9.6 0.0 copy-done
  9.6 0.2 maximum_convert_fusion
  9.9 0.5 fusion
  10.4 0.1 slice_multiply_fusion.3
  10.4 0.2 copy.15
  10.7 1.0 %maximum_bitcast_fusion.src_ref = f32[64,2,8,256]{3,2,1,0:T(8,128)} fusion(f32[1,256,64,8]{1,3,0,2:T(8,128)S(1)} %bitcast.25, f32[1,256,64,8]{1,3,0,2:T(8,128)S(1)} %bitcast.26), kind=kLoop, calls=%fused_computation.5 | loop fusion | flops 262144 | bytes 2097152 | tf_op jit(solution)/shard_map/transpose | solution.py:224
  11.7 0.0 copy-start.1
  11.7 57.2 %shard_map.136 = (f32[64,8,256]{2,1,0:T(8,128)}, f32[2,4,64,256]{3,2,1,0:T(8,128)}) custom-call(f32[64,2,8,256]{3,2,1,0:T(8,128)} %maximum_bitcast_fusion.src_ref, f32[72,64]{1,0:T(8,128)} %constant.20.clone.refs_0_, f32[72,64]{1,0:T(8,128)} %constant.21.clone.refs_1_, f32[72,256]{1,0:T(8,128)} %constant.22.clone.refs_2_, f32[72,256]{1,0:T(8,128)} %constant.23.clone.refs_3_, ...), custom_call_target="tpu_custom_call" | custom-call | tf_op jit(solution)/shard_map/pallas_call | solution.py:184
  68.9 1.2 %copy.17 = f32[512,256]{0,1:T(8,128)S(1)} copy(f32[512,256]{1,0:T(8,128)} %bitcast.27) | data formatting | bytes 1048576 | tf_op jit(solution)/shard_map/reshape | solution.py:226
  70.1 0.0 copy-done.1
  70.1 0.9 %fusion.3 = bf16[256,512]{1,0:T(8,128)(2,1)} fusion(f32[256,3,512]{2,0,1:T(8,128)S(1)} %fusion, f32[512,256]{0,1:T(8,128)S(1)} %copy.17, f32[512]{0:T(512)S(1)} %copy-done.1), kind=kLoop, calls=%fused_computation.10 | loop fusion | flops 655360 | bytes 2361344 | tf_op jit(solution)/shard_map/convert_element_type | solution.py:227
Async XLA Ops:
  0.0 9.6 %copy-start = (bf16[256,3,512]{2,0,1:T(8,128)(2,1)S(1)}, bf16[256,3,512]{2,0,1:T(8,128)(2,1)}, u32[]{:S(2)}) copy-start(bf16[256,3,512]{2,0,1:T(8,128)(2,1)} %param.14) | copy-start | bytes 2359300
  0.8 8.8 %collective-permute-start = (bf16[2,3,512]{2,0,1:T(2,128)(2,1)S(1)}, bf16[2,3,512]{2,0,1:T(2,128)(2,1)S(1)}, u32[]{:S(2)}, u32[]{:S(2)}) collective-permute-start(bf16[2,3,512]{2,0,1:T(2,128)(2,1)S(1)} %slice.31), channel_id=1, source_target_pairs={{0,8},{8,16},{16,24},{24,32},{32,40},{40,48},{48,56},{56,64},{64,7... | collective-permute-start | bytes 18440 | tf_op jit(solution)/shard_map/ppermute | solution.py:209
  11.7 58.4 %copy-start.1 = (f32[512]{0:T(512)S(1)}, f32[512]{0:T(512)}, u32[]{:S(2)}) copy-start(f32[512]{0:T(512)} %param.16) | copy-start | bytes 6148

commit v15 on v14

--- a/solution.py
+++ b/solution.py
@@ -68,8 +68,8 @@
 
 def fused_kernel(shards, parts, src_ref, *refs):
     tables = refs[:10]
-    out_ref, stage_ref = refs[10:12]
-    recv_ref, x_ref, o_ref, yre_ref, yim_ref, sends, recvs, local = refs[12:]
+    out_ref = refs[10]
+    recv_ref, x_ref, o_all, yre_ref, yim_ref, sends, recvs, local = refs[11:]
     me = lax.axis_index("seq")
     row = lax.axis_index("ch")
     mesh_id = pl.DeviceIdType.MESH
@@ -142,13 +142,10 @@
             copy.start()
         for copy in gathers:
             copy.wait()
-        conv_body(x_ref, *tables, o_ref, yre_ref, yim_ref)
-        put = pltpu.make_async_copy(o_ref, stage_ref.at[h], local.at[2 * parts + streams])
-        put.start()
-        put.wait()
+        conv_body(x_ref, *tables, o_all.at[h], yre_ref, yim_ref)
         returns.append(
             scatter(
-                lambda j, h=h: stage_ref.at[h, :, j, :],
+                lambda j, h=h: o_all.at[h, :, j, :],
                 lambda j, h=h: out_ref.at[j, pl.ds(h * size, size), :],
                 parts + h,
             )
@@ -185,14 +182,13 @@
         functools.partial(fused_kernel, blocks, parts),
         out_shape=[
             jax.ShapeDtypeStruct((blocks, channels, rows), f32),
-            jax.ShapeDtypeStruct((parts, group, blocks, rows), f32),
         ],
         in_specs=[anywhere] + [vmem] * len(tables),
-        out_specs=[anywhere] * 2,
+        out_specs=[anywhere],
         scratch_shapes=[
             pltpu.VMEM((blocks, parts, 2, group, rows), f32),
             pltpu.VMEM((streams, blocks, rows), f32),
-            pltpu.VMEM((group, blocks, rows), f32),
+            pltpu.VMEM((parts, group, blocks, rows), f32),
             pltpu.VMEM((streams * pad, rows), f32),
             pltpu.VMEM((streams * pad, rows), f32),
             pltpu.SemaphoreType.DMA((2 * parts, blocks)),

time: 71.7 us -> 70.9 us (0.989)
  no operation moved by 1% of the time
where the time goes in v15:
time: 70.9 us; the launch traced here: 70.5 us
  Pallas kernels  56.6 us (80%)
  starting transfers between devices  4.51 us (6%)
  local copies, waits for them, and re-layouts  4.24 us (6%)
  other arithmetic  2.76 us (4%)
  waiting for transfers between devices  2.32 us (3%)
    pallas_call x1, Pallas kernels, long_conv(): pl.pallas_call(functools.partial(fused_kernel, blocks, parts), out_shape=...  56.6 us
    ppermute x1, starting transfers between devices, shifted(): return lax.ppermute(block, axis, route)  4.51 us
    ppermute x1, waiting for transfers between devices, shifted(): return lax.ppermute(block, axis, route)  2.32 us
  transfers between devices with their start and end apart: 1, of which 1 were waited for; matrix products, arithmetic and copies ran while one was open for 3% of the time, Pallas kernels for 0%

profile of v15, /device:TPU:1, one launch (start us, length us, event | category | flops | bytes accessed | tf_op | source)
XLA Modules:
  0.0 70.5 jit_solution(740604896477755342)
XLA Ops:
  0.0 0.0 copy-start
  0.0 0.8 %slice.31 = bf16[2,3,512]{2,0,1:T(2,128)(2,1)S(1)} slice(bf16[256,3,512]{2,0,1:T(8,128)(2,1)} %param.14), slice={[254:256], [0:3], [0:512]} | slice | bytes 12288 | tf_op jit(solution)/shard_map/slice | solution.py:213
  0.8 4.5 %collective-permute-start = (bf16[2,3,512]{2,0,1:T(2,128)(2,1)S(1)}, bf16[2,3,512]{2,0,1:T(2,128)(2,1)S(1)}, u32[]{:S(2)}, u32[]{:S(2)}) collective-permute-start(bf16[2,3,512]{2,0,1:T(2,128)(2,1)S(1)} %slice.31), channel_id=1, source_target_pairs={{0,8},{8,16},{16,24},{24,32},{32,40},{40,48},{48,56},{56,64},{64,7... | collective-permute-start | bytes 18440 | tf_op jit(solution)/shard_map/ppermute | solution.py:205
  5.3 0.7 %slice_bitcast_fusion.3 = (f32[3,512]{1,0:T(4,128)S(1)}, f32[3,512]{1,0:T(4,128)S(1)}, f32[3,512]{1,0:T(4,128)S(1)}) fusion(f32[3,3,512]{2,1,0:T(4,128)} %param.15), kind=kLoop, calls=%fused_computation.15 | loop fusion | bytes 36864 | tf_op jit(solution)/shard_map/mul | solution.py:215
  6.1 1.2 %copy.16 = f32[256,512]{0,1:T(8,128)S(1)} copy(f32[256,512]{1,0:T(8,128)} %param.17) | data formatting | bytes 1048576 | tf_op args[3]
  7.3 2.3 %collective-permute-done = bf16[2,3,512]{2,0,1:T(2,128)(2,1)S(1)} collective-permute-done((bf16[2,3,512]{2,0,1:T(2,128)(2,1)S(1)}, bf16[2,3,512]{2,0,1:T(2,128)(2,1)S(1)}, u32[]{:S(2)}, u32[]{:S(2)}) %collective-permute-start) | collective-permute-done | bytes 6176 | tf_op jit(solution)/shard_map/ppermute | solution.py:205
  9.6 0.0 copy-done
  9.6 0.2 maximum_convert_fusion
  9.9 0.5 fusion
  10.4 0.1 slice_multiply_fusion.3
  10.4 0.2 copy.15
  10.7 1.0 %maximum_bitcast_fusion.src_ref = f32[64,2,8,256]{3,2,1,0:T(8,128)} fusion(f32[1,256,64,8]{1,3,0,2:T(8,128)S(1)} %bitcast.25, f32[1,256,64,8]{1,3,0,2:T(8,128)S(1)} %bitcast.27), kind=kLoop, calls=%fused_computation.5 | loop fusion | flops 262144 | bytes 2097152 | tf_op jit(solution)/shard_map/transpose | solution.py:220
  11.7 0.0 copy-start.1
  11.7 56.6 %shard_map.136 = f32[64,8,256]{2,1,0:T(8,128)} custom-call(f32[64,2,8,256]{3,2,1,0:T(8,128)} %maximum_bitcast_fusion.src_ref, f32[72,64]{1,0:T(8,128)} %constant.20.clone.refs_0_, f32[72,64]{1,0:T(8,128)} %constant.21.clone.refs_1_, f32[72,256]{1,0:T(8,128)} %constant.22.clone.refs_2_, f32[72,256]{1,0:T(8,128)} %constant.23.clone.refs_3_, ...), custom_call_target="tpu_custom_call" | custom-call | tf_op jit(solution)/shard_map/pallas_call | solution.py:181
  68.3 1.2 %copy.17 = f32[512,256]{0,1:T(8,128)S(1)} copy(f32[512,256]{1,0:T(8,128)} %bitcast.26) | data formatting | bytes 1048576 | tf_op jit(solution)/shard_map/reshape | solution.py:222
  69.6 0.0 copy-done.1
  69.6 0.9 %fusion.3 = bf16[256,512]{1,0:T(8,128)(2,1)} fusion(f32[256,3,512]{2,0,1:T(8,128)S(1)} %fusion, f32[512,256]{0,1:T(8,128)S(1)} %copy.17, f32[512]{0:T(512)S(1)} %copy-done.1), kind=kLoop, calls=%fused_computation.10 | loop fusion | flops 655360 | bytes 2361344 | tf_op jit(solution)/shard_map/convert_element_type | solution.py:223
Async XLA Ops:
  0.0 9.6 %copy-start = (bf16[256,3,512]{2,0,1:T(8,128)(2,1)S(1)}, bf16[256,3,512]{2,0,1:T(8,128)(2,1)}, u32[]{:S(2)}) copy-start(bf16[256,3,512]{2,0,1:T(8,128)(2,1)} %param.14) | copy-start | bytes 2359300
  0.8 8.8 %collective-permute-start = (bf16[2,3,512]{2,0,1:T(2,128)(2,1)S(1)}, bf16[2,3,512]{2,0,1:T(2,128)(2,1)S(1)}, u32[]{:S(2)}, u32[]{:S(2)}) collective-permute-start(bf16[2,3,512]{2,0,1:T(2,128)(2,1)S(1)} %slice.31), channel_id=1, source_target_pairs={{0,8},{8,16},{16,24},{24,32},{32,40},{40,48},{48,56},{56,64},{64,7... | collective-permute-start | bytes 18440 | tf_op jit(solution)/shard_map/ppermute | solution.py:205
  11.7 57.9 %copy-start.1 = (f32[512]{0:T(512)S(1)}, f32[512]{0:T(512)}, u32[]{:S(2)}) copy-start(f32[512]{0:T(512)} %param.16) | copy-start | bytes 6148

commit v16 on v15

--- a/solution.py
+++ b/solution.py
@@ -22,7 +22,7 @@
     x_ref, c1_ref, s1_ref, twc_ref, tws_ref, vc_ref, vs_ref, vsum_ref, vdiff_ref, ci_ref, si_ref, o_ref,
     yre_ref, yim_ref,
 ):
-    streams = x_ref.shape[0]
+    streams = len(x_ref)
     group = streams // 2
     pad = c1_ref.shape[0]
 
@@ -34,7 +34,7 @@
     c1 = c1_ref[...]
     s1 = s1_ref[...]
     for j in range(streams):
-        xj = x_ref[j]
+        xj = x_ref[j][...]
         a = dot(c1, xj)
         b = dot(s1, xj)
         yre_ref[j * pad : (j + 1) * pad, :] = a * twc - b * tws
@@ -69,12 +69,12 @@
 def fused_kernel(shards, parts, src_ref, *refs):
     tables = refs[:10]
     out_ref = refs[10]
-    recv_ref, x_ref, o_all, yre_ref, yim_ref, sends, recvs, local = refs[11:]
+    x_all, o_all, yre_ref, yim_ref, sends, recvs, local = refs[11:]
     me = lax.axis_index("seq")
     row = lax.axis_index("ch")
     mesh_id = pl.DeviceIdType.MESH
-    streams = x_ref.shape[0]
-    size = streams // 2
+    size = x_all.shape[2]
+    streams = 2 * size
     barrier = pltpu.get_barrier_semaphore()
 
     def peer_of(step):
@@ -124,7 +124,7 @@
     arrivals = [
         scatter(
             lambda j, h=h: src_ref.at[j, :, pl.ds(h * size, size), :],
-            lambda j, h=h: recv_ref.at[j, h],
+            lambda j, h=h: x_all.at[h, :, :, j, :],
             h,
         )
         for h in range(parts)
@@ -132,16 +132,7 @@
     returns = []
     for h in range(parts):
         arrivals[h]()
-        gathers = [
-            pltpu.make_async_copy(
-                recv_ref.at[:, h, j // size, j % size, :], x_ref.at[j], local.at[2 * parts + j]
-            )
-            for j in range(streams)
-        ]
-        for copy in gathers:
-            copy.start()
-        for copy in gathers:
-            copy.wait()
+        x_ref = [x_all.at[h, s, g] for s in range(2) for g in range(size)]
         conv_body(x_ref, *tables, o_all.at[h], yre_ref, yim_ref)
         returns.append(
             scatter(
@@ -186,8 +177,7 @@
         in_specs=[anywhere] + [vmem] * len(tables),
         out_specs=[anywhere],
         scratch_shapes=[
-            pltpu.VMEM((blocks, parts, 2, group, rows), f32),
-            pltpu.VMEM((streams, blocks, rows), f32),
+            pltpu.VMEM((parts, 2, group, blocks, rows), f32),
             pltpu.VMEM((parts, group, blocks, rows), f32),
             pltpu.VMEM((streams * pad, rows), f32),
             pltpu.VMEM((streams * pad, rows), f32),

time: 70.9 us -> 70.7 us (level)
  no operation moved by 1% of the time
where the time goes in v16:
time: 70.7 us; the launch traced here: 70.3 us
  Pallas kernels  56.4 us (80%)
  starting transfers between devices  4.51 us (6%)
  local copies, waits for them, and re-layouts  4.24 us (6%)
  other arithmetic  2.76 us (4%)
  waiting for transfers between devices  2.32 us (3%)
    pallas_call x1, Pallas kernels, long_conv(): pl.pallas_call(functools.partial(fused_kernel, blocks, parts), out_shape=...  56.4 us
    ppermute x1, starting transfers between devices, shifted(): return lax.ppermute(block, axis, route)  4.51 us
    ppermute x1, waiting for transfers between devices, shifted(): return lax.ppermute(block, axis, route)  2.32 us
  transfers between devices with their start and end apart: 1, of which 1 were waited for; matrix products, arithmetic and copies ran while one was open for 3% of the time, Pallas kernels for 0%

profile of v16, /device:TPU:1, one launch (start us, length us, event | category | flops | bytes accessed | tf_op | source)
XLA Modules:
  0.0 70.3 jit_solution(16983576691197631203)
XLA Ops:
  0.0 0.0 copy-start
  0.0 0.8 %slice.31 = bf16[2,3,512]{2,0,1:T(2,128)(2,1)S(1)} slice(bf16[256,3,512]{2,0,1:T(8,128)(2,1)} %param.14), slice={[254:256], [0:3], [0:512]} | slice | bytes 12288 | tf_op jit(solution)/shard_map/slice | solution.py:203
  0.8 4.5 %collective-permute-start = (bf16[2,3,512]{2,0,1:T(2,128)(2,1)S(1)}, bf16[2,3,512]{2,0,1:T(2,128)(2,1)S(1)}, u32[]{:S(2)}, u32[]{:S(2)}) collective-permute-start(bf16[2,3,512]{2,0,1:T(2,128)(2,1)S(1)} %slice.31), channel_id=1, source_target_pairs={{0,8},{8,16},{16,24},{24,32},{32,40},{40,48},{48,56},{56,64},{64,7... | collective-permute-start | bytes 18440 | tf_op jit(solution)/shard_map/ppermute | solution.py:195
  5.3 0.7 %slice_bitcast_fusion.3 = (f32[3,512]{1,0:T(4,128)S(1)}, f32[3,512]{1,0:T(4,128)S(1)}, f32[3,512]{1,0:T(4,128)S(1)}) fusion(f32[3,3,512]{2,1,0:T(4,128)} %param.15), kind=kLoop, calls=%fused_computation.15 | loop fusion | bytes 36864 | tf_op jit(solution)/shard_map/mul | solution.py:205
  6.1 1.2 %copy.16 = f32[256,512]{0,1:T(8,128)S(1)} copy(f32[256,512]{1,0:T(8,128)} %param.17) | data formatting | bytes 1048576 | tf_op args[3]
  7.3 2.3 %collective-permute-done = bf16[2,3,512]{2,0,1:T(2,128)(2,1)S(1)} collective-permute-done((bf16[2,3,512]{2,0,1:T(2,128)(2,1)S(1)}, bf16[2,3,512]{2,0,1:T(2,128)(2,1)S(1)}, u32[]{:S(2)}, u32[]{:S(2)}) %collective-permute-start) | collective-permute-done | bytes 6176 | tf_op jit(solution)/shard_map/ppermute | solution.py:195
  9.6 0.0 copy-done
  9.6 0.2 maximum_convert_fusion
  9.9 0.5 fusion
  10.4 0.1 slice_multiply_fusion.3
  10.4 0.2 copy.15
  10.7 1.0 %maximum_bitcast_fusion.src_ref = f32[64,2,8,256]{3,2,1,0:T(8,128)} fusion(f32[1,256,64,8]{1,3,0,2:T(8,128)S(1)} %bitcast.25, f32[1,256,64,8]{1,3,0,2:T(8,128)S(1)} %bitcast.27), kind=kLoop, calls=%fused_computation.5 | loop fusion | flops 262144 | bytes 2097152 | tf_op jit(solution)/shard_map/transpose | solution.py:210
  11.7 0.0 copy-start.1
  11.7 56.4 %shard_map.136 = f32[64,8,256]{2,1,0:T(8,128)} custom-call(f32[64,2,8,256]{3,2,1,0:T(8,128)} %maximum_bitcast_fusion.src_ref, f32[72,64]{1,0:T(8,128)} %constant.20.clone.refs_0_, f32[72,64]{1,0:T(8,128)} %constant.21.clone.refs_1_, f32[72,256]{1,0:T(8,128)} %constant.22.clone.refs_2_, f32[72,256]{1,0:T(8,128)} %constant.23.clone.refs_3_, ...), custom_call_target="tpu_custom_call" | custom-call | tf_op jit(solution)/shard_map/pallas_call | solution.py:172
  68.1 1.2 %copy.17 = f32[512,256]{0,1:T(8,128)S(1)} copy(f32[512,256]{1,0:T(8,128)} %bitcast.26) | data formatting | bytes 1048576 | tf_op jit(solution)/shard_map/reshape | solution.py:212
  69.4 0.0 copy-done.1
  69.4 0.9 %fusion.3 = bf16[256,512]{1,0:T(8,128)(2,1)} fusion(f32[256,3,512]{2,0,1:T(8,128)S(1)} %fusion, f32[512,256]{0,1:T(8,128)S(1)} %copy.17, f32[512]{0:T(512)S(1)} %copy-done.1), kind=kLoop, calls=%fused_computation.10 | loop fusion | flops 655360 | bytes 2361344 | tf_op jit(solution)/shard_map/convert_element_type | solution.py:213
Async XLA Ops:
  0.0 9.6 %copy-start = (bf16[256,3,512]{2,0,1:T(8,128)(2,1)S(1)}, bf16[256,3,512]{2,0,1:T(8,128)(2,1)}, u32[]{:S(2)}) copy-start(bf16[256,3,512]{2,0,1:T(8,128)(2,1)} %param.14) | copy-start | bytes 2359300
  0.8 8.8 %collective-permute-start = (bf16[2,3,512]{2,0,1:T(2,128)(2,1)S(1)}, bf16[2,3,512]{2,0,1:T(2,128)(2,1)S(1)}, u32[]{:S(2)}, u32[]{:S(2)}) collective-permute-start(bf16[2,3,512]{2,0,1:T(2,128)(2,1)S(1)} %slice.31), channel_id=1, source_target_pairs={{0,8},{8,16},{16,24},{24,32},{32,40},{40,48},{48,56},{56,64},{64,7... | collective-permute-start | bytes 18440 | tf_op jit(solution)/shard_map/ppermute | solution.py:195
  11.7 57.7 %copy-start.1 = (f32[512]{0:T(512)S(1)}, f32[512]{0:T(512)}, u32[]{:S(2)}) copy-start(f32[512]{0:T(512)} %param.16) | copy-start | bytes 6148

commit v17 on v16

--- a/solution.py
+++ b/solution.py
@@ -109,29 +109,38 @@
 
         lax.fori_loop(0, shards - 1, send, 0)
 
-        def finish():
+        def sent():
+            def wait_one(step, carry):
+                copy_to(peer_of(step), me).wait_send()
+                return carry
+
+            lax.fori_loop(0, shards - 1, wait_one, 0)
+
+        def arrived():
             def wait_one(step, carry):
                 peer = peer_of(step)
-                copy_to(peer, me).wait_send()
                 copy_to(peer, peer).wait_recv()
                 return carry
 
             lax.fori_loop(0, shards - 1, wait_one, 0)
             own.wait()
 
-        return finish
-
-    arrivals = [
-        scatter(
-            lambda j, h=h: src_ref.at[j, :, pl.ds(h * size, size), :],
-            lambda j, h=h: x_all.at[h, :, :, j, :],
-            h,
+        return sent, arrived
+
+    arrivals = []
+    for h in range(parts):
+        if h:
+            arrivals[h - 1][0]()
+        arrivals.append(
+            scatter(
+                lambda j, h=h: src_ref.at[j, :, pl.ds(h * size, size), :],
+                lambda j, h=h: x_all.at[h, :, :, j, :],
+                h,
+            )
         )
-        for h in range(parts)
-    ]
     returns = []
     for h in range(parts):
-        arrivals[h]()
+        arrivals[h][1]()
         x_ref = [x_all.at[h, s, g] for s in range(2) for g in range(size)]
         conv_body(x_ref, *tables, o_all.at[h], yre_ref, yim_ref)
         returns.append(
@@ -141,8 +150,10 @@
                 parts + h,
             )
         )
-    for finish in returns:
-        finish()
+    arrivals[-1][0]()
+    for sent, arrived in returns:
+        sent()
+        arrived()
 
 
 def long_conv(pieces, parts):

time: 70.7 us -> 73.9 us (1.045)
  Pallas kernels: 56.4 us -> 59.7 us
    pallas_call x1, Pallas kernels: 56.4 us -> 59.7 us  [long_conv(): pl.pallas_call(functools.partial(fused_kernel, blocks, parts), out_shape=...]
where the time goes in v17:
time: 73.9 us; the launch traced here: 73.6 us
  Pallas kernels  59.7 us (81%)
  starting transfers between devices  4.51 us (6%)
  local copies, waits for them, and re-layouts  4.24 us (6%)
  other arithmetic  2.76 us (4%)
  waiting for transfers between devices  2.32 us (3%)
    pallas_call x1, Pallas kernels, long_conv(): pl.pallas_call(functools.partial(fused_kernel, blocks, parts), out_shape=...  59.7 us
    ppermute x1, starting transfers between devices, shifted(): return lax.ppermute(block, axis, route)  4.51 us
    ppermute x1, waiting for transfers between devices, shifted(): return lax.ppermute(block, axis, route)  2.32 us
  transfers between devices with their start and end apart: 1, of which 1 were waited for; matrix products, arithmetic and copies ran while one was open for 3% of the time, Pallas kernels for 0%

profile of v17, /device:TPU:1, one launch (start us, length us, event | category | flops | bytes accessed | tf_op | source)
XLA Modules:
  0.0 73.6 jit_solution(13567852970015173675)
XLA Ops:
  0.0 0.0 copy-start
  0.0 0.8 %slice.31 = bf16[2,3,512]{2,0,1:T(2,128)(2,1)S(1)} slice(bf16[256,3,512]{2,0,1:T(8,128)(2,1)} %param.14), slice={[254:256], [0:3], [0:512]} | slice | bytes 12288 | tf_op jit(solution)/shard_map/slice | solution.py:214
  0.8 4.5 %collective-permute-start = (bf16[2,3,512]{2,0,1:T(2,128)(2,1)S(1)}, bf16[2,3,512]{2,0,1:T(2,128)(2,1)S(1)}, u32[]{:S(2)}, u32[]{:S(2)}) collective-permute-start(bf16[2,3,512]{2,0,1:T(2,128)(2,1)S(1)} %slice.31), channel_id=1, source_target_pairs={{0,8},{8,16},{16,24},{24,32},{32,40},{40,48},{48,56},{56,64},{64,7... | collective-permute-start | bytes 18440 | tf_op jit(solution)/shard_map/ppermute | solution.py:206
  5.3 0.7 %slice_bitcast_fusion.3 = (f32[3,512]{1,0:T(4,128)S(1)}, f32[3,512]{1,0:T(4,128)S(1)}, f32[3,512]{1,0:T(4,128)S(1)}) fusion(f32[3,3,512]{2,1,0:T(4,128)} %param.15), kind=kLoop, calls=%fused_computation.15 | loop fusion | bytes 36864 | tf_op jit(solution)/shard_map/mul | solution.py:216
  6.1 1.2 %copy.16 = f32[256,512]{0,1:T(8,128)S(1)} copy(f32[256,512]{1,0:T(8,128)} %param.17) | data formatting | bytes 1048576 | tf_op args[3]
  7.3 2.3 %collective-permute-done = bf16[2,3,512]{2,0,1:T(2,128)(2,1)S(1)} collective-permute-done((bf16[2,3,512]{2,0,1:T(2,128)(2,1)S(1)}, bf16[2,3,512]{2,0,1:T(2,128)(2,1)S(1)}, u32[]{:S(2)}, u32[]{:S(2)}) %collective-permute-start) | collective-permute-done | bytes 6176 | tf_op jit(solution)/shard_map/ppermute | solution.py:206
  9.6 0.0 copy-done
  9.6 0.2 maximum_convert_fusion
  9.9 0.5 fusion
  10.4 0.1 slice_multiply_fusion.3
  10.4 0.2 copy.15
  10.7 1.0 %maximum_bitcast_fusion.src_ref = f32[64,2,8,256]{3,2,1,0:T(8,128)} fusion(f32[1,256,64,8]{1,3,0,2:T(8,128)S(1)} %bitcast.25, f32[1,256,64,8]{1,3,0,2:T(8,128)S(1)} %bitcast.27), kind=kLoop, calls=%fused_computation.5 | loop fusion | flops 262144 | bytes 2097152 | tf_op jit(solution)/shard_map/transpose | solution.py:221
  11.7 0.0 copy-start.1
  11.7 59.7 %shard_map.136 = f32[64,8,256]{2,1,0:T(8,128)} custom-call(f32[64,2,8,256]{3,2,1,0:T(8,128)} %maximum_bitcast_fusion.src_ref, f32[72,64]{1,0:T(8,128)} %constant.20.clone.refs_0_, f32[72,64]{1,0:T(8,128)} %constant.21.clone.refs_1_, f32[72,256]{1,0:T(8,128)} %constant.22.clone.refs_2_, f32[72,256]{1,0:T(8,128)} %constant.23.clone.refs_3_, ...), custom_call_target="tpu_custom_call" | custom-call | tf_op jit(solution)/shard_map/pallas_call | solution.py:183
  71.4 1.2 %copy.17 = f32[512,256]{0,1:T(8,128)S(1)} copy(f32[512,256]{1,0:T(8,128)} %bitcast.26) | data formatting | bytes 1048576 | tf_op jit(solution)/shard_map/reshape | solution.py:223
  72.7 0.0 copy-done.1
  72.7 0.9 %fusion.3 = bf16[256,512]{1,0:T(8,128)(2,1)} fusion(f32[256,3,512]{2,0,1:T(8,128)S(1)} %fusion, f32[512,256]{0,1:T(8,128)S(1)} %copy.17, f32[512]{0:T(512)S(1)} %copy-done.1), kind=kLoop, calls=%fused_computation.10 | loop fusion | flops 655360 | bytes 2361344 | tf_op jit(solution)/shard_map/convert_element_type | solution.py:224
Async XLA Ops:
  0.0 9.6 %copy-start = (bf16[256,3,512]{2,0,1:T(8,128)(2,1)S(1)}, bf16[256,3,512]{2,0,1:T(8,128)(2,1)}, u32[]{:S(2)}) copy-start(bf16[256,3,512]{2,0,1:T(8,128)(2,1)} %param.14) | copy-start | bytes 2359300
  0.8 8.8 %collective-permute-start = (bf16[2,3,512]{2,0,1:T(2,128)(2,1)S(1)}, bf16[2,3,512]{2,0,1:T(2,128)(2,1)S(1)}, u32[]{:S(2)}, u32[]{:S(2)}) collective-permute-start(bf16[2,3,512]{2,0,1:T(2,128)(2,1)S(1)} %slice.31), channel_id=1, source_target_pairs={{0,8},{8,16},{16,24},{24,32},{32,40},{40,48},{48,56},{56,64},{64,7... | collective-permute-start | bytes 18440 | tf_op jit(solution)/shard_map/ppermute | solution.py:206
  11.7 61.0 %copy-start.1 = (f32[512]{0:T(512)S(1)}, f32[512]{0:T(512)}, u32[]{:S(2)}) copy-start(f32[512]{0:T(512)} %param.16) | copy-start | bytes 6148

commit v18 on v17

--- a/solution.py
+++ b/solution.py
@@ -109,14 +109,16 @@
 
         lax.fori_loop(0, shards - 1, send, 0)
 
-        def sent():
+        def sent(first, last):
             def wait_one(step, carry):
                 copy_to(peer_of(step), me).wait_send()
                 return carry
 
-            lax.fori_loop(0, shards - 1, wait_one, 0)
-
-        def arrived():
+            lax.fori_loop(first, last, wait_one, 0)
+
+        def finish(first=0):
+            sent(first, shards - 1)
+
             def wait_one(step, carry):
                 peer = peer_of(step)
                 copy_to(peer, peer).wait_recv()
@@ -125,12 +127,13 @@
             lax.fori_loop(0, shards - 1, wait_one, 0)
             own.wait()
 
-        return sent, arrived
-
+        return sent, finish
+
+    early = shards // 2
     arrivals = []
     for h in range(parts):
         if h:
-            arrivals[h - 1][0]()
+            arrivals[h - 1][0](0, early)
         arrivals.append(
             scatter(
                 lambda j, h=h: src_ref.at[j, :, pl.ds(h * size, size), :],
@@ -140,7 +143,7 @@
         )
     returns = []
     for h in range(parts):
-        arrivals[h][1]()
+        arrivals[h][1](early if h < parts - 1 else 0)
         x_ref = [x_all.at[h, s, g] for s in range(2) for g in range(size)]
         conv_body(x_ref, *tables, o_all.at[h], yre_ref, yim_ref)
         returns.append(
@@ -150,10 +153,8 @@
                 parts + h,
             )
         )
-    arrivals[-1][0]()
-    for sent, arrived in returns:
-        sent()
-        arrived()
+    for _, finish in returns:
+        finish()
 
 
 def long_conv(pieces, parts):

time: 73.9 us -> 70.5 us (0.954)
  Pallas kernels: 59.7 us -> 56.3 us
    pallas_call x1, Pallas kernels: 59.7 us -> 56.3 us  [long_conv(): pl.pallas_call(functools.partial(fused_kernel, blocks, parts), out_shape=...]
where the time goes in v18:
time: 70.5 us; the launch traced here: 70.2 us
  Pallas kernels  56.3 us (80%)
  starting transfers between devices  4.51 us (6%)
  local copies, waits for them, and re-layouts  4.24 us (6%)
  other arithmetic  2.76 us (4%)
  waiting for transfers between devices  2.32 us (3%)
    pallas_call x1, Pallas kernels, long_conv(): pl.pallas_call(functools.partial(fused_kernel, blocks, parts), out_shape=...  56.3 us
    ppermute x1, starting transfers between devices, shifted(): return lax.ppermute(block, axis, route)  4.51 us
    ppermute x1, waiting for transfers between devices, shifted(): return lax.ppermute(block, axis, route)  2.32 us
  transfers between devices with their start and end apart: 1, of which 1 were waited for; matrix products, arithmetic and copies ran while one was open for 3% of the time, Pallas kernels for 0%

profile of v18, /device:TPU:1, one launch (start us, length us, event | category | flops | bytes accessed | tf_op | source)
XLA Modules:
  0.0 70.2 jit_solution(2016321685895950949)
XLA Ops:
  0.0 0.0 copy-start
  0.0 0.8 %slice.31 = bf16[2,3,512]{2,0,1:T(2,128)(2,1)S(1)} slice(bf16[256,3,512]{2,0,1:T(8,128)(2,1)} %param.14), slice={[254:256], [0:3], [0:512]} | slice | bytes 12288 | tf_op jit(solution)/shard_map/slice | solution.py:215
  0.8 4.5 %collective-permute-start = (bf16[2,3,512]{2,0,1:T(2,128)(2,1)S(1)}, bf16[2,3,512]{2,0,1:T(2,128)(2,1)S(1)}, u32[]{:S(2)}, u32[]{:S(2)}) collective-permute-start(bf16[2,3,512]{2,0,1:T(2,128)(2,1)S(1)} %slice.31), channel_id=1, source_target_pairs={{0,8},{8,16},{16,24},{24,32},{32,40},{40,48},{48,56},{56,64},{64,7... | collective-permute-start | bytes 18440 | tf_op jit(solution)/shard_map/ppermute | solution.py:207
  5.3 0.7 %slice_bitcast_fusion.3 = (f32[3,512]{1,0:T(4,128)S(1)}, f32[3,512]{1,0:T(4,128)S(1)}, f32[3,512]{1,0:T(4,128)S(1)}) fusion(f32[3,3,512]{2,1,0:T(4,128)} %param.15), kind=kLoop, calls=%fused_computation.15 | loop fusion | bytes 36864 | tf_op jit(solution)/shard_map/mul | solution.py:217
  6.1 1.2 %copy.16 = f32[256,512]{0,1:T(8,128)S(1)} copy(f32[256,512]{1,0:T(8,128)} %param.17) | data formatting | bytes 1048576 | tf_op args[3]
  7.3 2.3 %collective-permute-done = bf16[2,3,512]{2,0,1:T(2,128)(2,1)S(1)} collective-permute-done((bf16[2,3,512]{2,0,1:T(2,128)(2,1)S(1)}, bf16[2,3,512]{2,0,1:T(2,128)(2,1)S(1)}, u32[]{:S(2)}, u32[]{:S(2)}) %collective-permute-start) | collective-permute-done | bytes 6176 | tf_op jit(solution)/shard_map/ppermute | solution.py:207
  9.6 0.0 copy-done
  9.6 0.2 maximum_convert_fusion
  9.9 0.5 fusion
  10.4 0.1 slice_multiply_fusion.3
  10.4 0.2 copy.15
  10.7 1.0 %maximum_bitcast_fusion.src_ref = f32[64,2,8,256]{3,2,1,0:T(8,128)} fusion(f32[1,256,64,8]{1,3,0,2:T(8,128)S(1)} %bitcast.25, f32[1,256,64,8]{1,3,0,2:T(8,128)S(1)} %bitcast.27), kind=kLoop, calls=%fused_computation.5 | loop fusion | flops 262144 | bytes 2097152 | tf_op jit(solution)/shard_map/transpose | solution.py:222
  11.7 0.0 copy-start.1
  11.7 56.3 %shard_map.136 = f32[64,8,256]{2,1,0:T(8,128)} custom-call(f32[64,2,8,256]{3,2,1,0:T(8,128)} %maximum_bitcast_fusion.src_ref, f32[72,64]{1,0:T(8,128)} %constant.20.clone.refs_0_, f32[72,64]{1,0:T(8,128)} %constant.21.clone.refs_1_, f32[72,256]{1,0:T(8,128)} %constant.22.clone.refs_2_, f32[72,256]{1,0:T(8,128)} %constant.23.clone.refs_3_, ...), custom_call_target="tpu_custom_call" | custom-call | tf_op jit(solution)/shard_map/pallas_call | solution.py:184
  68.1 1.2 %copy.17 = f32[512,256]{0,1:T(8,128)S(1)} copy(f32[512,256]{1,0:T(8,128)} %bitcast.26) | data formatting | bytes 1048576 | tf_op jit(solution)/shard_map/reshape | solution.py:224
  69.3 0.0 copy-done.1
  69.3 0.9 %fusion.3 = bf16[256,512]{1,0:T(8,128)(2,1)} fusion(f32[256,3,512]{2,0,1:T(8,128)S(1)} %fusion, f32[512,256]{0,1:T(8,128)S(1)} %copy.17, f32[512]{0:T(512)S(1)} %copy-done.1), kind=kLoop, calls=%fused_computation.10 | loop fusion | flops 655360 | bytes 2361344 | tf_op jit(solution)/shard_map/convert_element_type | solution.py:225
Async XLA Ops:
  0.0 9.6 %copy-start = (bf16[256,3,512]{2,0,1:T(8,128)(2,1)S(1)}, bf16[256,3,512]{2,0,1:T(8,128)(2,1)}, u32[]{:S(2)}) copy-start(bf16[256,3,512]{2,0,1:T(8,128)(2,1)} %param.14) | copy-start | bytes 2359300
  0.8 8.8 %collective-permute-start = (bf16[2,3,512]{2,0,1:T(2,128)(2,1)S(1)}, bf16[2,3,512]{2,0,1:T(2,128)(2,1)S(1)}, u32[]{:S(2)}, u32[]{:S(2)}) collective-permute-start(bf16[2,3,512]{2,0,1:T(2,128)(2,1)S(1)} %slice.31), channel_id=1, source_target_pairs={{0,8},{8,16},{16,24},{24,32},{32,40},{40,48},{48,56},{56,64},{64,7... | collective-permute-start | bytes 18440 | tf_op jit(solution)/shard_map/ppermute | solution.py:207
  11.7 57.6 %copy-start.1 = (f32[512]{0:T(512)S(1)}, f32[512]{0:T(512)}, u32[]{:S(2)}) copy-start(f32[512]{0:T(512)} %param.16) | copy-start | bytes 6148
